TPU v7x, 512 devices: a whole 4x4x16 slice. The times are simulated.
512 devices in a mesh: leaf: 512 (over y, x, z, core).
Axes of the slice: x: 4, y: 4, z: 16, core: 2. Of those that a mesh axis runs over, the one named last changes fastest.
Arguments:
- vectors: float32 [512, 512, 128], P('leaf'), may hold values from -6 to 6
- points: float32 [512, 3, 512], P('leaf')
- leaf_basis: float32 [512, 512, 128], P('leaf'), may hold values from -0.25 to 0.25
- transfer_leaf: float32 [512, 128, 128], P('leaf'), may hold values from -0.5 to 0.5
- transfer_pair: float32 [32768, 128], P('leaf'), may hold values from -0.5 to 0.5
- transfer_quad: float32 [16384, 128], P('leaf'), may hold values from -0.5 to 0.5
- skel_leaf: float32 [512, 3, 128], P('leaf')
- skel_pair: float32 [256, 3, 128], replicated
- skel_quad: float32 [128, 3, 128], replicated
- skel_top: float32 [64, 3, 128], replicated
- near_list: int32 [512, 16], P('leaf'), may hold values from -1 to 511, as said below
- far_leaf: int32 [512, 8], P('leaf'), may hold values from -1 to 511, as said below
- far_pair: int32 [256, 8], replicated, may hold values from -1 to 255, as said below
- far_quad: int32 [128, 8], replicated, may hold values from -1 to 127, as said below
- far_top: int32 [64, 8], replicated, may hold values from -1 to 63, as said below
Outputs:
- product: float32 [512, 512, 128], P('leaf')
Inputs may be any that keep to these rules, and one draw needn't show every extreme that they name: `near_list`: entry 0 of row l is l; the other entries are distinct leaves within 8 of l, or -1 for an unused slot. `far_leaf`: distinct leaves within 8 of the row's leaf, none of them in that leaf's row of near_list, or -1 for an unused slot. `far_pair`: distinct clusters within 4 of the row's cluster and other than it, or -1 for an unused slot. `far_quad`: distinct clusters within 4 of the row's cluster and other than it, or -1 for an unused slot. `far_top`: distinct top clusters other than the row's cluster, or -1 for an unused slot.
All inputs are finite; a program needn't handle non-finite values.
Results may differ from a plain program's by a relative error of at most 0.0003.
Values sent between devices are 32-bit elements; how exact they have to be, the bound alone decides.
A program may use at most 64 MiB of HBM per device.

v0:
```python
import functools

import jax
import jax.numpy as jnp
from jax import lax
from jax.experimental import pallas as pl
from jax.experimental.pallas import tpu as pltpu
from jax.sharding import Mesh
from jax.sharding import PartitionSpec as P

REACH = 8
FAR_REACH = 4


INV_FOUR_PI = 0.07957747154594767
DELTA_SQ = 0.01
HIGHEST = lax.Precision.HIGHEST

AX = ("cl", "q", "p", "c")
MEMBERS = ("q", "p", "c")


def from_partner(value, axis, bit):
    mask = 2**bit
    pairs = [(source, source ^ mask) for source in range(lax.axis_size(axis))]
    return lax.ppermute(value, axis, pairs)


def from_behind(block, axis, distance):
    devices = range(lax.axis_size(axis))
    route = [(i - distance, i) for i in devices if i - distance in devices]
    return lax.ppermute(block, axis, route)


def kernel_block(left_pts, right_pts):
    distance = jnp.zeros((left_pts.shape[1], right_pts.shape[1]), jnp.float32)
    for axis_id in range(3):
        offset_gap = left_pts[axis_id][:, None] - right_pts[axis_id][None, :]
        distance = distance + offset_gap * offset_gap
    return INV_FOUR_PI * lax.rsqrt(distance + DELTA_SQ)


def transposed_dot(matrix, values):
    return lax.dot_general(matrix, values, (((0,), (0,)), ((), ())), precision=HIGHEST)


def listed_sum(own_coords, entries, fetcher, width):

    def advance(running, partner):
        coords, values = fetcher(jnp.maximum(partner, 0))
        contrib = jnp.dot(kernel_block(own_coords, coords), values, precision=HIGHEST)
        return (running + jnp.where(partner >= 0, contrib, 0.0), None)

    start_value = jnp.zeros((own_coords.shape[1], width), jnp.float32)
    result, _ = lax.scan(advance, start_value, entries)
    return result


def batched_far(own_coords, coords, values, valid):
    count, _, span = coords.shape
    right = jnp.transpose(coords, (1, 0, 2)).reshape(3, count * span)
    masked = jnp.where(valid[:, None, None], values, 0.0)
    flat = masked.reshape(count * span, values.shape[2])
    return jnp.dot(kernel_block(own_coords, right), flat, precision=HIGHEST)


def pair_total(partial_value, levels):
    for bit_index in range(levels):
        partial_value = partial_value + from_partner(partial_value, AX, bit_index)
    return partial_value


def join_rows(block, levels, device):
    for bit_index in range(levels):
        other = from_partner(block, AX, bit_index)
        upper = device // 2**bit_index % 2
        block = jnp.where(
            upper == 0, jnp.concatenate([block, other], 0), jnp.concatenate([other, block], 0)
        )
    return block


def window(shipped):
    gathered = []
    for distance in range(-REACH, REACH + 1):
        if distance == 0:
            gathered.append(shipped)
        else:
            gathered.append(from_behind(shipped, AX, -distance))
    return jnp.stack(gathered)


def partner_stack(coefs, stride):
    gathered = []
    for offset in list(range(-FAR_REACH, 0)) + list(range(1, FAR_REACH + 1)):
        gathered.append(from_behind(coefs, AX, -offset * stride))
    stacked = jnp.stack(gathered)

    def slot_of(distance):
        return distance + FAR_REACH - (distance > 0).astype(jnp.int32)

    return (stacked, slot_of)


def middle_level(coefs, skeletons, lists, transfer_rows, above, stride, device):
    rank_rows = coefs.shape[0] // stride
    cluster = device // stride
    member = device % stride
    own_full = lax.dynamic_index_in_dim(skeletons, cluster, 0, keepdims=False)
    own_coords = lax.dynamic_slice_in_dim(own_full, member * rank_rows, rank_rows, 1)
    stacked, slot_of = partner_stack(coefs, stride)
    entries = lax.dynamic_index_in_dim(lists, cluster, 0, keepdims=False)
    chosen = jnp.maximum(entries, 0)
    coords = jnp.take(skeletons, chosen, axis=0)
    slots = jnp.clip(slot_of(chosen - cluster), 0, stacked.shape[0] - 1)
    values = jnp.take(stacked, slots, axis=0)
    rows_here = batched_far(own_coords, coords, values, entries >= 0) + jnp.dot(
        transfer_rows, above, precision=HIGHEST
    )
    return join_rows(rows_here, stride.bit_length() - 1, device)


def cluster_gather(block, device, clusters):
    gathered = block[None]
    for level in range(clusters.bit_length() - 1):
        bit_index = 3 + level
        other = from_partner(gathered, AX, bit_index)
        upper = device // 2**bit_index % 2
        gathered = jnp.where(
            upper == 0,
            jnp.concatenate([gathered, other], 0),
            jnp.concatenate([other, gathered], 0),
        )
    return gathered


def near_sum(own_points, near_entries, shipped, device):
    leaf_points = own_points.shape[1]
    point_rows = leaf_points + 3 * leaf_points // shipped.shape[1]

    def contribution(block, distance):
        listed = jnp.any(near_entries == device + distance)
        coords = block[leaf_points:point_rows].reshape(3, leaf_points)
        contrib = jnp.dot(
            kernel_block(own_points, coords), block[:leaf_points], precision=lax.Precision.HIGH
        )
        return jnp.where(listed, contrib, 0.0)

    total = contribution(shipped, 0)
    ahead = shipped
    behind = shipped
    rim = [None] * (2 * REACH + 1)
    rim[REACH] = shipped[point_rows:]
    for step in range(1, REACH + 1):
        ahead = from_behind(ahead, AX, 1)
        behind = from_behind(behind, AX, -1)
        rim[REACH - step] = ahead[point_rows:]
        rim[REACH + step] = behind[point_rows:]
        total = total + contribution(ahead, -step) + contribution(behind, step)
    return total, jnp.stack(rim)


def middle_full(coefs, skeletons, lists, transfer, above, stride, device):
    cluster = device // stride
    own_coords = lax.dynamic_index_in_dim(skeletons, cluster, 0, keepdims=False)
    stacked, slot_of = partner_stack(coefs, stride)
    entries = lax.dynamic_index_in_dim(lists, cluster, 0, keepdims=False)
    chosen = jnp.maximum(entries, 0)
    coords = jnp.take(skeletons, chosen, axis=0)
    slots = jnp.clip(slot_of(chosen - cluster), 0, stacked.shape[0] - 1)
    values = jnp.take(stacked, slots, axis=0)
    return batched_far(own_coords, coords, values, entries >= 0) + jnp.dot(
        transfer, above, precision=HIGHEST
    )


def gather_kernel(clusters, block_ref, out_ref, landing, send_sem, recv_sem):
    me = lax.axis_index("cl")
    mesh_id = pl.DeviceIdType.MESH
    barrier = pltpu.get_barrier_semaphore()

    def greet(step, carry):
        peer = lax.rem(me + step, clusters)
        pl.semaphore_signal(barrier, inc=1, device_id={"cl": peer}, device_id_type=mesh_id)
        return carry

    lax.fori_loop(1, clusters, greet, 0)
    pl.semaphore_wait(barrier, clusters - 1)

    def outgoing(step):
        peer = lax.rem(me + step, clusters)
        return pltpu.make_async_remote_copy(
            src_ref=block_ref,
            dst_ref=landing.at[me],
            send_sem=send_sem.at[step],
            recv_sem=recv_sem.at[me],
            device_id={"cl": peer},
            device_id_type=mesh_id,
        )

    def incoming(step):
        source = lax.rem(me - step + clusters, clusters)
        return pltpu.make_async_remote_copy(
            src_ref=block_ref,
            dst_ref=landing.at[source],
            send_sem=send_sem.at[step],
            recv_sem=recv_sem.at[source],
            device_id={"cl": source},
            device_id_type=mesh_id,
        )

    def send(step, carry):
        outgoing(step).start()
        return carry

    lax.fori_loop(1, clusters, send, 0)
    landing[me] = block_ref[...]

    def finish(step, carry):
        outgoing(step).wait_send()
        incoming(step).wait_recv()
        return carry

    lax.fori_loop(1, clusters, finish, 0)
    out_ref[...] = landing[...]


def cluster_gather_kernel(block):
    clusters = lax.axis_size("cl")
    rows, cols = block.shape
    return pl.pallas_call(
        functools.partial(gather_kernel, clusters),
        out_shape=jax.ShapeDtypeStruct((clusters, rows, cols), jnp.float32),
        in_specs=[pl.BlockSpec(memory_space=pltpu.VMEM)],
        out_specs=pl.BlockSpec(memory_space=pltpu.VMEM),
        scratch_shapes=[
            pltpu.VMEM((clusters, rows, cols), jnp.float32),
            pltpu.SemaphoreType.DMA((clusters,)),
            pltpu.SemaphoreType.DMA((clusters,)),
        ],
        compiler_params=pltpu.CompilerParams(collective_id=0, has_side_effects=True),
    )(block)


def per_device(
    vectors,
    points,
    leaf_basis,
    transfer_leaf,
    transfer_pair,
    transfer_quad,
    skel_leaf,
    skel_pair,
    skel_quad,
    skel_top,
    near_list,
    far_leaf,
    far_pair,
    far_quad,
    far_top,
):
    leaf_points = vectors.shape[1]
    width = vectors.shape[2]
    rank = leaf_basis.shape[2]
    device = lax.axis_index(AX)
    own_points = points[0]
    coef_leaf = transposed_dot(leaf_basis[0], vectors[0])
    pair_matrix = join_rows(transfer_pair, 1, device)
    quad_matrix = join_rows(transfer_quad, 2, device)
    up_pair = transposed_dot(transfer_leaf[0], coef_leaf)
    up_quad = transposed_dot(pair_matrix, up_pair)
    up_top = transposed_dot(quad_matrix, up_quad)
    first = jnp.stack([up_pair, up_quad, up_top])
    first = first + from_partner(first, AX, 0)
    coef_pair = first[0]
    second = first[1:] + from_partner(first[1:], AX, 1)
    coef_quad = second[0]
    coef_top = second[1] + from_partner(second[1], AX, 2)
    shipped = jnp.concatenate(
        [vectors[0], own_points.reshape(3 * leaf_points // width, width), coef_leaf, skel_leaf[0]],
        axis=0,
    )
    near_field, leaf_rim = near_sum(own_points, near_list[0], shipped, device)
    coef_top, coef_pair, coef_quad = lax.optimization_barrier((coef_top, coef_pair, coef_quad))
    top_cluster = device // 8
    top_member = device % 8
    share = width // 8
    top_cols_own = lax.dynamic_slice_in_dim(coef_top.T, top_member * share, share, 0)
    all_top = jnp.swapaxes(cluster_gather_kernel(top_cols_own), 1, 2)
    top_coords = lax.dynamic_index_in_dim(skel_top, top_cluster, 0, keepdims=False)
    top_entries = lax.dynamic_index_in_dim(far_top, top_cluster, 0, keepdims=False)
    top_chosen = jnp.maximum(top_entries, 0)
    top_cols = batched_far(
        top_coords,
        jnp.take(skel_top, top_chosen, axis=0),
        jnp.take(all_top, top_chosen, axis=0),
        top_entries >= 0,
    )
    local_top = lax.all_gather(top_cols, MEMBERS, axis=1, tiled=True)
    local_quad = middle_full(coef_quad, skel_quad, far_quad, quad_matrix, local_top, 4, device)
    local_pair = middle_full(coef_pair, skel_pair, far_pair, pair_matrix, local_quad, 2, device)
    leaf_entries = far_leaf[0]
    positions = jnp.clip(jnp.maximum(leaf_entries, 0) - device + REACH, 0, 2 * REACH)
    leaf_blocks = jnp.take(leaf_rim, positions, axis=0)
    local_leaf = batched_far(
        skel_leaf[0], leaf_blocks[:, rank:], leaf_blocks[:, :rank], leaf_entries >= 0
    ) + jnp.dot(transfer_leaf[0], local_pair, precision=HIGHEST)
    product = near_field + jnp.dot(leaf_basis[0], local_leaf, precision=HIGHEST)
    return product[None]


def solution(mesh):
    count = mesh.devices.size
    grid = Mesh(mesh.devices.reshape(count // 8, 2, 2, 2), AX)
    spread = P(AX, None, None)
    rows = P(AX, None)
    placed = (
        spread,
        spread,
        spread,
        spread,
        rows,
        rows,
        spread,
        P(),
        P(),
        P(),
        rows,
        rows,
        P(),
        P(),
        P(),
    )
    return jax.shard_map(per_device, mesh=grid, in_specs=placed, out_specs=spread, check_vma=False)
```

profile of v0, /device:TPU:24, one launch (start us, length us, event | category | flops | bytes accessed | tf_op | source)
XLA Modules:
  0.0 309.7 jit_solution(8159404523096498413)
XLA Ops:
  1.7 1.6 fusion.407
  4.3 1.9 collective-permute-start
  6.2 13.2 %collective-permute-start.1 = (f32[655,128]{1,0:T(8,128)S(1)}, f32[655,128]{1,0:T(8,128)S(1)}, u32[]{:S(2)}, u32[]{:S(2)}) collective-permute-start(f32[655,128]{1,0:T(8,128)S(1)} %pad_maximum_fusion), channel_id=1, source_target_pairs={{1,0},{2,1},{3,2},{4,3},{5,4},{6,5},{7,6},{8,7},{9,8},{10,9},{11,1... | collective-permute-start | bytes 1006088 | tf_op jit(solution)/shard_map/ppermute | solution.py:32
  19.5 1.9 collective-permute-start.16
  21.4 2.4 collective-permute-start.17
  26.1 1.6 gather_fusion.1
  30.8 1.6 convolution_select_fusion.16
  33.8 1.9 collective-permute-start.18
  36.1 3.5 %collective-permute-done.18 = f32[64,128]{1,0:T(8,128)S(1)} collective-permute-done((f32[64,128]{1,0:T(8,128)S(1)}, f32[64,128]{1,0:T(8,128)S(1)}, u32[]{:S(2)}, u32[]{:S(2)}) %collective-permute-start.18) | collective-permute-done | bytes 32800 | tf_op jit(solution)/shard_map/ppermute | solution.py:26
  39.9 1.9 collective-permute-start.19
  43.3 1.9 collective-permute-start.20
  45.2 2.0 collective-permute-start.2
  48.1 7.7 %collective-permute-start.3 = (f32[655,128]{1,0:T(8,128)S(1)}, f32[655,128]{1,0:T(8,128)}, u32[]{:S(2)}, u32[]{:S(2)}) collective-permute-start(f32[655,128]{1,0:T(8,128)S(1)} %collective-permute-done.1), channel_id=1, source_target_pairs={{1,0},{2,1},{3,2},{4,3},{5,4},{6,5},{7,6},{8,7},{9,8},{10,9},{11,1... | collective-permute-start | bytes 1006088 | tf_op jit(solution)/shard_map/ppermute | solution.py:32
  55.8 2.5 fusion.17
  58.4 1.9 collective-permute-start.21
  60.3 2.2 fusion.16
  62.5 2.9 collective-permute-done.21
  65.4 1.9 collective-permute-start.22
  67.4 1.9 collective-permute-start.23
  69.3 5.8 %collective-permute-start.24 = (f32[128,128]{0,1:T(8,128)S(1)}, f32[128,128]{0,1:T(8,128)S(1)}, u32[]{:S(2)}, u32[]{:S(2)}) collective-permute-start(f32[128,128]{0,1:T(8,128)S(1)} %slice_bitcast_fusion.18), channel_id=1, source_target_pairs={{0,4},{1,5},{2,6},{3,7},{4,8},{5,9},{6,10},{7,11},{8,12},{9,13},{1... | collective-permute-start | bytes 196616 | tf_op jit(solution)/shard_map/ppermute | solution.py:32
  75.7 32.3 %shard_map.145 = f32[64,16,128]{2,1,0:T(8,128)} custom-call(f32[16,128]{1,0:T(8,128)} %dynamic-slice_bitcast_fusion.block_ref), custom_call_target="tpu_custom_call" | custom-call | tf_op jit(solution)/shard_map/pallas_call | solution.py:231
  108.0 1.6 gather_fusion.4
  110.4 16.6 %all_gather.3 = f32[128,128]{0,1:T(8,128)S(1)} all-gather(f32[128,16]{0,1:T(8,128)S(1)} %fusion.206), channel_id=1, replica_groups=mesh['cl'=64,'q'=2,'p'=2,'c'=2] {'q','p','c'}, dimensions={1}, use_global_device_ids=true | all-gather | bytes 73728 | tf_op jit(solution)/shard_map/all_gather | solution.py:299
  127.0 3.9 %collective-permute-start.25 = (f32[128,128]{0,1:T(8,128)S(1)}, f32[128,128]{0,1:T(8,128)S(1)}, u32[]{:S(2)}, u32[]{:S(2)}) collective-permute-start(f32[128,128]{0,1:T(8,128)S(1)} %slice_bitcast_fusion.18), channel_id=1, source_target_pairs={{0,2},{1,3},{2,4},{3,5},{4,6},{5,7},{6,8},{7,9},{8,10},{9,11},{10,... | collective-permute-start | bytes 196616 | tf_op jit(solution)/shard_map/ppermute | solution.py:32
  131.0 7.3 %collective-permute-start.26 = (f32[128,128]{0,1:T(8,128)S(1)}, f32[128,128]{0,1:T(8,128)S(1)}, u32[]{:S(2)}, u32[]{:S(2)}) collective-permute-start(f32[128,128]{0,1:T(8,128)S(1)} %slice_bitcast_fusion.18), channel_id=1, source_target_pairs={{2,0},{3,1},{4,2},{5,3},{6,4},{7,5},{8,6},{9,7},{10,8},{11,9},{12,... | collective-permute-start | bytes 196616 | tf_op jit(solution)/shard_map/ppermute | solution.py:32
  138.3 3.4 %collective-permute-start.27 = (f32[128,128]{0,1:T(8,128)S(1)}, f32[128,128]{0,1:T(8,128)S(1)}, u32[]{:S(2)}, u32[]{:S(2)}) collective-permute-start(f32[128,128]{0,1:T(8,128)S(1)} %slice_bitcast_fusion.18), channel_id=1, source_target_pairs={{4,0},{5,1},{6,2},{7,3},{8,4},{9,5},{10,6},{11,7},{12,8},{13,9},{1... | collective-permute-start | bytes 196616 | tf_op jit(solution)/shard_map/ppermute | solution.py:32
  141.7 3.7 %collective-permute-start.28 = (f32[128,128]{0,1:T(8,128)S(1)}, f32[128,128]{0,1:T(8,128)S(1)}, u32[]{:S(2)}, u32[]{:S(2)}) collective-permute-start(f32[128,128]{0,1:T(8,128)S(1)} %slice_bitcast_fusion.18), channel_id=1, source_target_pairs={{6,0},{7,1},{8,2},{9,3},{10,4},{11,5},{12,6},{13,7},{14,8},{15,9},... | collective-permute-start | bytes 196616 | tf_op jit(solution)/shard_map/ppermute | solution.py:32
  145.4 7.1 %collective-permute-start.29 = (f32[128,128]{0,1:T(8,128)S(1)}, f32[128,128]{0,1:T(8,128)S(1)}, u32[]{:S(2)}, u32[]{:S(2)}) collective-permute-start(f32[128,128]{0,1:T(8,128)S(1)} %slice_bitcast_fusion.18), channel_id=1, source_target_pairs={{8,0},{9,1},{10,2},{11,3},{12,4},{13,5},{14,6},{15,7},{16,8},{17,9... | collective-permute-start | bytes 196616 | tf_op jit(solution)/shard_map/ppermute | solution.py:32
  152.6 6.8 %collective-permute-start.30 = (f32[128,128]{0,1:T(8,128)S(1)}, f32[128,128]{0,1:T(8,128)S(1)}, u32[]{:S(2)}, u32[]{:S(2)}) collective-permute-start(f32[128,128]{0,1:T(8,128)S(1)} %get-tuple-element.10), channel_id=1, source_target_pairs={{0,16},{1,17},{2,18},{3,19},{4,20},{5,21},{6,22},{7,23},{8,24},{9,... | collective-permute-start | bytes 196616 | tf_op jit(solution)/shard_map/ppermute | solution.py:32
  159.4 2.5 collective-permute-start.31
  161.9 3.9 %collective-permute-start.32 = (f32[128,128]{0,1:T(8,128)S(1)}, f32[128,128]{0,1:T(8,128)S(1)}, u32[]{:S(2)}, u32[]{:S(2)}) collective-permute-start(f32[128,128]{0,1:T(8,128)S(1)} %get-tuple-element.10), channel_id=1, source_target_pairs={{0,8},{1,9},{2,10},{3,11},{4,12},{5,13},{6,14},{7,15},{8,16},{9,17... | collective-permute-start | bytes 196616 | tf_op jit(solution)/shard_map/ppermute | solution.py:32
  166.6 3.9 %collective-permute-done.30 = f32[128,128]{0,1:T(8,128)S(1)} collective-permute-done((f32[128,128]{0,1:T(8,128)S(1)}, f32[128,128]{0,1:T(8,128)S(1)}, u32[]{:S(2)}, u32[]{:S(2)}) %collective-permute-start.30) | collective-permute-done | bytes 65568 | tf_op jit(solution)/shard_map/ppermute | solution.py:32
  170.5 1.9 collective-permute-start.33
  172.5 9.5 %collective-permute-done.31 = f32[128,128]{0,1:T(8,128)S(1)} collective-permute-done((f32[128,128]{0,1:T(8,128)S(1)}, f32[128,128]{0,1:T(8,128)S(1)}, u32[]{:S(2)}, u32[]{:S(2)}) %collective-permute-start.31) | collective-permute-done | bytes 65568 | tf_op jit(solution)/shard_map/ppermute | solution.py:32
  181.9 2.3 collective-permute-start.34
  184.3 3.7 %collective-permute-start.35 = (f32[128,128]{0,1:T(8,128)S(1)}, f32[128,128]{0,1:T(8,128)S(1)}, u32[]{:S(2)}, u32[]{:S(2)}) collective-permute-start(f32[128,128]{0,1:T(8,128)S(1)} %get-tuple-element.10), channel_id=1, source_target_pairs={{8,0},{9,1},{10,2},{11,3},{12,4},{13,5},{14,6},{15,7},{16,8},{17,9... | collective-permute-start | bytes 196616 | tf_op jit(solution)/shard_map/ppermute | solution.py:32
  187.9 8.4 %collective-permute-start.36 = (f32[128,128]{0,1:T(8,128)S(1)}, f32[128,128]{0,1:T(8,128)S(1)}, u32[]{:S(2)}, u32[]{:S(2)}) collective-permute-start(f32[128,128]{0,1:T(8,128)S(1)} %get-tuple-element.10), channel_id=1, source_target_pairs={{12,0},{13,1},{14,2},{15,3},{16,4},{17,5},{18,6},{19,7},{20,8},{21... | collective-permute-start | bytes 196616 | tf_op jit(solution)/shard_map/ppermute | solution.py:32
  196.4 4.8 %collective-permute-start.37 = (f32[128,128]{0,1:T(8,128)S(1)}, f32[128,128]{0,1:T(8,128)S(1)}, u32[]{:S(2)}, u32[]{:S(2)}) collective-permute-start(f32[128,128]{0,1:T(8,128)S(1)} %get-tuple-element.10), channel_id=1, source_target_pairs={{16,0},{17,1},{18,2},{19,3},{20,4},{21,5},{22,6},{23,7},{24,8},{25... | collective-permute-start | bytes 196616 | tf_op jit(solution)/shard_map/ppermute | solution.py:32
  201.5 10.3 %collective-permute-done.37 = f32[128,128]{0,1:T(8,128)S(1)} collective-permute-done((f32[128,128]{0,1:T(8,128)S(1)}, f32[128,128]{0,1:T(8,128)S(1)}, u32[]{:S(2)}, u32[]{:S(2)}) %collective-permute-start.37) | collective-permute-done | bytes 65568 | tf_op jit(solution)/shard_map/ppermute | solution.py:32
  215.4 1.9 collective-permute-start.5
  218.1 2.6 collective-permute-start.4
  220.7 2.6 convolution_select_fusion.12
  224.1 2.5 fusion.15
  226.6 7.3 %collective-permute-start.7 = (f32[655,128]{1,0:T(8,128)S(1)}, f32[655,128]{1,0:T(8,128)S(1)}, u32[]{:S(2)}, u32[]{:S(2)}) collective-permute-start(f32[655,128]{1,0:T(8,128)S(1)} %collective-permute-done.5), channel_id=1, source_target_pairs={{1,0},{2,1},{3,2},{4,3},{5,4},{6,5},{7,6},{8,7},{9,8},{10,9},{11,1... | collective-permute-start | bytes 1006088 | tf_op jit(solution)/shard_map/ppermute | solution.py:32
  234.0 1.9 collective-permute-start.6
  235.9 1.5 convolution_select_fusion.10
  237.4 1.6 fusion.13
  239.0 7.9 %collective-permute-start.9 = (f32[655,128]{1,0:T(8,128)S(1)}, f32[655,128]{1,0:T(8,128)S(1)}, u32[]{:S(2)}, u32[]{:S(2)}) collective-permute-start(f32[655,128]{1,0:T(8,128)S(1)} %collective-permute-done.7), channel_id=1, source_target_pairs={{1,0},{2,1},{3,2},{4,3},{5,4},{6,5},{7,6},{8,7},{9,8},{10,9},{11,1... | collective-permute-start | bytes 1006088 | tf_op jit(solution)/shard_map/ppermute | solution.py:32
  246.9 1.9 collective-permute-start.8
  248.9 1.6 convolution_select_fusion.8
  252.0 7.9 %collective-permute-start.11 = (f32[655,128]{1,0:T(8,128)S(1)}, f32[655,128]{1,0:T(8,128)S(1)}, u32[]{:S(2)}, u32[]{:S(2)}) collective-permute-start(f32[655,128]{1,0:T(8,128)S(1)} %collective-permute-done.9), channel_id=1, source_target_pairs={{1,0},{2,1},{3,2},{4,3},{5,4},{6,5},{7,6},{8,7},{9,8},{10,9},{11,1... | collective-permute-start | bytes 1006088 | tf_op jit(solution)/shard_map/ppermute | solution.py:32
  259.9 1.9 collective-permute-start.10
  261.8 1.6 convolution_select_fusion.6
  263.4 1.5 fusion.9
  264.9 7.9 %collective-permute-start.13 = (f32[655,128]{1,0:T(8,128)S(1)}, f32[655,128]{1,0:T(8,128)S(1)}, u32[]{:S(2)}, u32[]{:S(2)}) collective-permute-start(f32[655,128]{1,0:T(8,128)S(1)} %collective-permute-done.11), channel_id=1, source_target_pairs={{1,0},{2,1},{3,2},{4,3},{5,4},{6,5},{7,6},{8,7},{9,8},{10,9},{11,1... | collective-permute-start | bytes 1006088 | tf_op jit(solution)/shard_map/ppermute | solution.py:32
  272.8 1.9 collective-permute-start.12
  274.7 1.6 convolution_select_fusion.4
  277.8 7.9 %collective-permute-start.15 = (f32[655,128]{1,0:T(8,128)S(1)}, f32[655,128]{1,0:T(8,128)S(1)}, u32[]{:S(2)}, u32[]{:S(2)}) collective-permute-start(f32[655,128]{1,0:T(8,128)S(1)} %collective-permute-done.13), channel_id=1, source_target_pairs={{1,0},{2,1},{3,2},{4,3},{5,4},{6,5},{7,6},{8,7},{9,8},{10,9},{11,1... | collective-permute-start | bytes 1006088 | tf_op jit(solution)/shard_map/ppermute | solution.py:32
  285.7 2.1 collective-permute-start.14
  287.9 1.6 convolution_select_fusion.2
  289.4 2.3 fusion.5
  291.8 6.7 %collective-permute-done.14 = f32[655,128]{1,0:T(8,128)S(1)} collective-permute-done((f32[655,128]{1,0:T(8,128)S(1)}, f32[655,128]{1,0:T(8,128)S(1)}, u32[]{:S(2)}, u32[]{:S(2)}) %collective-permute-start.14) | collective-permute-done | bytes 335392 | tf_op jit(solution)/shard_map/ppermute | solution.py:32
  306.0 1.5 convolution_select_fusion
  307.5 2.3 fusion.3
  (213 shorter events, 29.7 us)
Async XLA Ops:
  0.0 1.7 copy-start
  0.0 24.1 %copy-start.15 = (f32[1,3,128]{2,0,1:T(1,128)S(1)}, f32[1,3,128]{2,0,1:T(1,128)}, u32[]{:S(2)}) copy-start(f32[1,3,128]{2,0,1:T(1,128)} %param.23) | copy-start | bytes 4612
  0.0 25.7 %copy-start.6 = (f32[1,3,512]{2,0,1:T(1,128)S(1)}, f32[1,3,512]{2,0,1:T(1,128)}, u32[]{:S(2)}) copy-start(f32[1,3,512]{2,0,1:T(1,128)} %param.18) | copy-start | bytes 18436
  0.0 19.4 %copy-start.4 = (f32[64,128]{1,0:T(8,128)S(1)}, f32[64,128]{1,0:T(8,128)}, u32[]{:S(2)}) copy-start(f32[64,128]{1,0:T(8,128)} %param.21) | copy-start | bytes 98308
  0.0 21.4 %copy-start.13 = (f32[32,128]{1,0:T(8,128)S(1)}, f32[32,128]{1,0:T(8,128)}, u32[]{:S(2)}) copy-start(f32[32,128]{1,0:T(8,128)} %param.22) | copy-start | bytes 49156
  0.0 23.8 %copy-start.16 = (s32[1,8]{1,0:T(1,128)S(1)}, s32[1,8]{1,0:T(1,128)}, u32[]{:S(2)}) copy-start(s32[1,8]{1,0:T(1,128)} %param.28) | copy-start | bytes 100
  0.0 24.6 %copy-start.14 = (s32[256,8]{0,1:T(8,128)S(1)}, s32[256,8]{0,1:T(8,128)}, u32[]{:S(2)}) copy-start(s32[256,8]{0,1:T(8,128)} %param.29) | copy-start | bytes 24580
  0.1 25.0 %copy-start.11 = (s32[64,8]{0,1:T(8,128)S(1)}, s32[64,8]{0,1:T(8,128)}, u32[]{:S(2)}) copy-start(s32[64,8]{0,1:T(8,128)} %param.31) | copy-start | bytes 6148
  0.1 25.3 %copy-start.12 = (s32[128,8]{0,1:T(8,128)S(1)}, s32[128,8]{0,1:T(8,128)}, u32[]{:S(2)}) copy-start(s32[128,8]{0,1:T(8,128)} %param.30) | copy-start | bytes 12292
  0.1 25.7 %copy-start.2 = (f32[1,128,128]{2,1,0:T(8,128)S(1)}, f32[1,128,128]{2,1,0:T(8,128)}, u32[]{:S(2)}) copy-start(f32[1,128,128]{2,1,0:T(8,128)} %param.20) | copy-start | bytes 196612
  0.1 27.7 %copy-start.5 = (f32[128,3,128]{2,0,1:T(8,128)S(1)}, f32[128,3,128]{2,0,1:T(8,128)}, u32[]{:S(2)}) copy-start(f32[128,3,128]{2,0,1:T(8,128)} %param.25) | copy-start | bytes 589828
  0.1 28.4 %copy-start.3 = (f32[64,3,128]{2,0,1:T(8,128)S(1)}, f32[64,3,128]{2,0,1:T(8,128)}, u32[]{:S(2)}) copy-start(f32[64,3,128]{2,0,1:T(8,128)} %param.26) | copy-start | bytes 294916
  1.7 28.2 %copy-start.17 = (s32[1,16]{1,0:T(1,128)S(1)}, s32[1,16]{1,0:T(1,128)}, u32[]{:S(2)}) copy-start(s32[1,16]{1,0:T(1,128)} %param.27) | copy-start | bytes 196
  1.7 29.1 %copy-start.1 = (f32[1,512,128]{2,1,0:T(8,128)S(1)}, f32[1,512,128]{2,1,0:T(8,128)}, u32[]{:S(2)}) copy-start(f32[1,512,128]{2,1,0:T(8,128)} %param.17) | copy-start | bytes 786436
  4.3 40.9 %collective-permute-start = (f32[655,128]{1,0:T(8,128)S(1)}, f32[655,128]{1,0:T(8,128)}, u32[]{:S(2)}, u32[]{:S(2)}) collective-permute-start(f32[655,128]{1,0:T(8,128)S(1)} %pad_maximum_fusion), channel_id=1, source_target_pairs={{0,1},{1,2},{2,3},{3,4},{4,5},{5,6},{6,7},{7,8},{8,9},{9,10},{10,1... | collective-permute-start | bytes 1006088 | tf_op jit(solution)/shard_map/ppermute | solution.py:32
  6.2 41.8 %collective-permute-start.1 = (f32[655,128]{1,0:T(8,128)S(1)}, f32[655,128]{1,0:T(8,128)S(1)}, u32[]{:S(2)}, u32[]{:S(2)}) collective-permute-start(f32[655,128]{1,0:T(8,128)S(1)} %pad_maximum_fusion), channel_id=1, source_target_pairs={{1,0},{2,1},{3,2},{4,3},{5,4},{6,5},{7,6},{8,7},{9,8},{10,9},{11,1... | collective-permute-start | bytes 1006088 | tf_op jit(solution)/shard_map/ppermute | solution.py:32
  19.5 16.3 %collective-permute-start.16 = (f32[64,128]{1,0:T(8,128)S(1)}, f32[64,128]{1,0:T(8,128)S(1)}, u32[]{:S(2)}, u32[]{:S(2)}) collective-permute-start(f32[64,128]{1,0:T(8,128)S(1)} %copy-done.4), channel_id=1, source_target_pairs={{0,1},{1,0},{2,3},{3,2},{4,5},{5,4},{6,7},{7,6},{8,9},{9,8},{10,11... | collective-permute-start | bytes 98312 | tf_op jit(solution)/shard_map/ppermute | solution.py:26
  21.4 12.4 %collective-permute-start.17 = (f32[32,128]{1,0:T(8,128)S(1)}, f32[32,128]{1,0:T(8,128)S(1)}, u32[]{:S(2)}, u32[]{:S(2)}) collective-permute-start(f32[32,128]{1,0:T(8,128)S(1)} %copy-done.13), channel_id=1, source_target_pairs={{0,1},{1,0},{2,3},{3,2},{4,5},{5,4},{6,7},{7,6},{8,9},{9,8},{10,11... | collective-permute-start | bytes 49160 | tf_op jit(solution)/shard_map/ppermute | solution.py:26
  33.8 5.8 %collective-permute-start.18 = (f32[64,128]{1,0:T(8,128)S(1)}, f32[64,128]{1,0:T(8,128)S(1)}, u32[]{:S(2)}, u32[]{:S(2)}) collective-permute-start(f32[64,128]{1,0:T(8,128)S(1)} %maximum_select_fusion.6), channel_id=1, source_target_pairs={{0,2},{1,3},{2,0},{3,1},{4,6},{5,7},{6,4},{7,5},{8,10},{9,11},{10,... | collective-permute-start | bytes 98312 | tf_op jit(solution)/shard_map/ppermute | solution.py:26
  39.9 3.3 %collective-permute-start.19 = (f32[3,128,128]{1,2,0:T(8,128)S(1)}, f32[3,128,128]{1,2,0:T(8,128)S(1)}, u32[]{:S(2)}, u32[]{:S(2)}) collective-permute-start(f32[3,128,128]{1,2,0:T(8,128)S(1)} %pad_maximum_fusion.1), channel_id=1, source_target_pairs={{0,1},{1,0},{2,3},{3,2},{4,5},{5,4},{6,7},{7,6},{8,9},{9,8},{10,11... | collective-permute-start | bytes 589832 | tf_op jit(solution)/shard_map/ppermute | solution.py:26
  43.3 15.0 %collective-permute-start.20 = (f32[2,128,128]{1,2,0:T(8,128)S(1)}, f32[2,128,128]{1,2,0:T(8,128)S(1)}, u32[]{:S(2)}, u32[]{:S(2)}) collective-permute-start(f32[2,128,128]{1,2,0:T(8,128)S(1)} %slice.748), channel_id=1, source_target_pairs={{0,2},{1,3},{2,0},{3,1},{4,6},{5,7},{6,4},{7,5},{8,10},{9,11},{10,... | collective-permute-start | bytes 393224 | tf_op jit(solution)/shard_map/ppermute | solution.py:26
  45.2 172.8 %collective-permute-start.2 = (f32[655,128]{1,0:T(8,128)}, f32[655,128]{1,0:T(8,128)}, u32[]{:S(2)}, u32[]{:S(2)}) collective-permute-start(f32[655,128]{1,0:T(8,128)} %collective-permute-done), channel_id=1, source_target_pairs={{0,1},{1,2},{2,3},{3,4},{4,5},{5,6},{6,7},{7,8},{8,9},{9,10},{10,1... | collective-permute-start | bytes 1006088 | tf_op jit(solution)/shard_map/ppermute | solution.py:32
  48.1 167.3 %collective-permute-start.3 = (f32[655,128]{1,0:T(8,128)S(1)}, f32[655,128]{1,0:T(8,128)}, u32[]{:S(2)}, u32[]{:S(2)}) collective-permute-start(f32[655,128]{1,0:T(8,128)S(1)} %collective-permute-done.1), channel_id=1, source_target_pairs={{1,0},{2,1},{3,2},{4,3},{5,4},{6,5},{7,6},{8,7},{9,8},{10,9},{11,1... | collective-permute-start | bytes 1006088 | tf_op jit(solution)/shard_map/ppermute | solution.py:32
  58.4 7.1 %collective-permute-start.21 = (f32[128,128]{0,1:T(8,128)S(1)}, f32[128,128]{0,1:T(8,128)S(1)}, u32[]{:S(2)}, u32[]{:S(2)}) collective-permute-start(f32[128,128]{0,1:T(8,128)S(1)} %get-tuple-element.97), channel_id=1, source_target_pairs={{0,4},{1,5},{2,6},{3,7},{4,0},{5,1},{6,2},{7,3},{8,12},{9,13},{10,... | collective-permute-start | bytes 196616 | tf_op jit(solution)/shard_map/ppermute | solution.py:26
  65.4 61.6 %collective-permute-start.22 = (f32[128,128]{0,1:T(8,128)S(1)}, f32[128,128]{0,1:T(8,128)S(1)}, u32[]{:S(2)}, u32[]{:S(2)}) collective-permute-start(f32[128,128]{0,1:T(8,128)S(1)} %slice_bitcast_fusion.18), channel_id=1, source_target_pairs={{0,8},{1,9},{2,10},{3,11},{4,12},{5,13},{6,14},{7,15},{8,16},{9,17... | collective-permute-start | bytes 196616 | tf_op jit(solution)/shard_map/ppermute | solution.py:32
  67.4 63.6 %collective-permute-start.23 = (f32[128,128]{0,1:T(8,128)S(1)}, f32[128,128]{0,1:T(8,128)S(1)}, u32[]{:S(2)}, u32[]{:S(2)}) collective-permute-start(f32[128,128]{0,1:T(8,128)S(1)} %slice_bitcast_fusion.18), channel_id=1, source_target_pairs={{0,6},{1,7},{2,8},{3,9},{4,10},{5,11},{6,12},{7,13},{8,14},{9,15},... | collective-permute-start | bytes 196616 | tf_op jit(solution)/shard_map/ppermute | solution.py:32
  69.3 69.0 %collective-permute-start.24 = (f32[128,128]{0,1:T(8,128)S(1)}, f32[128,128]{0,1:T(8,128)S(1)}, u32[]{:S(2)}, u32[]{:S(2)}) collective-permute-start(f32[128,128]{0,1:T(8,128)S(1)} %slice_bitcast_fusion.18), channel_id=1, source_target_pairs={{0,4},{1,5},{2,6},{3,7},{4,8},{5,9},{6,10},{7,11},{8,12},{9,13},{1... | collective-permute-start | bytes 196616 | tf_op jit(solution)/shard_map/ppermute | solution.py:32
  127.0 14.7 %collective-permute-start.25 = (f32[128,128]{0,1:T(8,128)S(1)}, f32[128,128]{0,1:T(8,128)S(1)}, u32[]{:S(2)}, u32[]{:S(2)}) collective-permute-start(f32[128,128]{0,1:T(8,128)S(1)} %slice_bitcast_fusion.18), channel_id=1, source_target_pairs={{0,2},{1,3},{2,4},{3,5},{4,6},{5,7},{6,8},{7,9},{8,10},{9,11},{10,... | collective-permute-start | bytes 196616 | tf_op jit(solution)/shard_map/ppermute | solution.py:32
  131.0 14.4 %collective-permute-start.26 = (f32[128,128]{0,1:T(8,128)S(1)}, f32[128,128]{0,1:T(8,128)S(1)}, u32[]{:S(2)}, u32[]{:S(2)}) collective-permute-start(f32[128,128]{0,1:T(8,128)S(1)} %slice_bitcast_fusion.18), channel_id=1, source_target_pairs={{2,0},{3,1},{4,2},{5,3},{6,4},{7,5},{8,6},{9,7},{10,8},{11,9},{12,... | collective-permute-start | bytes 196616 | tf_op jit(solution)/shard_map/ppermute | solution.py:32
  138.3 14.3 %collective-permute-start.27 = (f32[128,128]{0,1:T(8,128)S(1)}, f32[128,128]{0,1:T(8,128)S(1)}, u32[]{:S(2)}, u32[]{:S(2)}) collective-permute-start(f32[128,128]{0,1:T(8,128)S(1)} %slice_bitcast_fusion.18), channel_id=1, source_target_pairs={{4,0},{5,1},{6,2},{7,3},{8,4},{9,5},{10,6},{11,7},{12,8},{13,9},{1... | collective-permute-start | bytes 196616 | tf_op jit(solution)/shard_map/ppermute | solution.py:32
  141.7 17.7 %collective-permute-start.28 = (f32[128,128]{0,1:T(8,128)S(1)}, f32[128,128]{0,1:T(8,128)S(1)}, u32[]{:S(2)}, u32[]{:S(2)}) collective-permute-start(f32[128,128]{0,1:T(8,128)S(1)} %slice_bitcast_fusion.18), channel_id=1, source_target_pairs={{6,0},{7,1},{8,2},{9,3},{10,4},{11,5},{12,6},{13,7},{14,8},{15,9},... | collective-permute-start | bytes 196616 | tf_op jit(solution)/shard_map/ppermute | solution.py:32
  145.4 16.5 %collective-permute-start.29 = (f32[128,128]{0,1:T(8,128)S(1)}, f32[128,128]{0,1:T(8,128)S(1)}, u32[]{:S(2)}, u32[]{:S(2)}) collective-permute-start(f32[128,128]{0,1:T(8,128)S(1)} %slice_bitcast_fusion.18), channel_id=1, source_target_pairs={{8,0},{9,1},{10,2},{11,3},{12,4},{13,5},{14,6},{15,7},{16,8},{17,9... | collective-permute-start | bytes 196616 | tf_op jit(solution)/shard_map/ppermute | solution.py:32
  152.6 17.9 %collective-permute-start.30 = (f32[128,128]{0,1:T(8,128)S(1)}, f32[128,128]{0,1:T(8,128)S(1)}, u32[]{:S(2)}, u32[]{:S(2)}) collective-permute-start(f32[128,128]{0,1:T(8,128)S(1)} %get-tuple-element.10), channel_id=1, source_target_pairs={{0,16},{1,17},{2,18},{3,19},{4,20},{5,21},{6,22},{7,23},{8,24},{9,... | collective-permute-start | bytes 196616 | tf_op jit(solution)/shard_map/ppermute | solution.py:32
  159.4 22.6 %collective-permute-start.31 = (f32[128,128]{0,1:T(8,128)S(1)}, f32[128,128]{0,1:T(8,128)S(1)}, u32[]{:S(2)}, u32[]{:S(2)}) collective-permute-start(f32[128,128]{0,1:T(8,128)S(1)} %get-tuple-element.10), channel_id=1, source_target_pairs={{0,12},{1,13},{2,14},{3,15},{4,16},{5,17},{6,18},{7,19},{8,20},{9,... | collective-permute-start | bytes 196616 | tf_op jit(solution)/shard_map/ppermute | solution.py:32
  161.9 22.3 %collective-permute-start.32 = (f32[128,128]{0,1:T(8,128)S(1)}, f32[128,128]{0,1:T(8,128)S(1)}, u32[]{:S(2)}, u32[]{:S(2)}) collective-permute-start(f32[128,128]{0,1:T(8,128)S(1)} %get-tuple-element.10), channel_id=1, source_target_pairs={{0,8},{1,9},{2,10},{3,11},{4,12},{5,13},{6,14},{7,15},{8,16},{9,17... | collective-permute-start | bytes 196616 | tf_op jit(solution)/shard_map/ppermute | solution.py:32
  170.5 17.4 %collective-permute-start.33 = (f32[128,128]{0,1:T(8,128)S(1)}, f32[128,128]{0,1:T(8,128)S(1)}, u32[]{:S(2)}, u32[]{:S(2)}) collective-permute-start(f32[128,128]{0,1:T(8,128)S(1)} %get-tuple-element.10), channel_id=1, source_target_pairs={{0,4},{1,5},{2,6},{3,7},{4,8},{5,9},{6,10},{7,11},{8,12},{9,13},{1... | collective-permute-start | bytes 196616 | tf_op jit(solution)/shard_map/ppermute | solution.py:32
  181.9 14.5 %collective-permute-start.34 = (f32[128,128]{0,1:T(8,128)S(1)}, f32[128,128]{0,1:T(8,128)S(1)}, u32[]{:S(2)}, u32[]{:S(2)}) collective-permute-start(f32[128,128]{0,1:T(8,128)S(1)} %get-tuple-element.10), channel_id=1, source_target_pairs={{4,0},{5,1},{6,2},{7,3},{8,4},{9,5},{10,6},{11,7},{12,8},{13,9},{1... | collective-permute-start | bytes 196616 | tf_op jit(solution)/shard_map/ppermute | solution.py:32
  184.3 17.0 %collective-permute-start.35 = (f32[128,128]{0,1:T(8,128)S(1)}, f32[128,128]{0,1:T(8,128)S(1)}, u32[]{:S(2)}, u32[]{:S(2)}) collective-permute-start(f32[128,128]{0,1:T(8,128)S(1)} %get-tuple-element.10), channel_id=1, source_target_pairs={{8,0},{9,1},{10,2},{11,3},{12,4},{13,5},{14,6},{15,7},{16,8},{17,9... | collective-permute-start | bytes 196616 | tf_op jit(solution)/shard_map/ppermute | solution.py:32
  187.9 13.4 %collective-permute-start.36 = (f32[128,128]{0,1:T(8,128)S(1)}, f32[128,128]{0,1:T(8,128)S(1)}, u32[]{:S(2)}, u32[]{:S(2)}) collective-permute-start(f32[128,128]{0,1:T(8,128)S(1)} %get-tuple-element.10), channel_id=1, source_target_pairs={{12,0},{13,1},{14,2},{15,3},{16,4},{17,5},{18,6},{19,7},{20,8},{21... | collective-permute-start | bytes 196616 | tf_op jit(solution)/shard_map/ppermute | solution.py:32
  196.4 15.4 %collective-permute-start.37 = (f32[128,128]{0,1:T(8,128)S(1)}, f32[128,128]{0,1:T(8,128)S(1)}, u32[]{:S(2)}, u32[]{:S(2)}) collective-permute-start(f32[128,128]{0,1:T(8,128)S(1)} %get-tuple-element.10), channel_id=1, source_target_pairs={{16,0},{17,1},{18,2},{19,3},{20,4},{21,5},{22,6},{23,7},{24,8},{25... | collective-permute-start | bytes 196616 | tf_op jit(solution)/shard_map/ppermute | solution.py:32
  212.6 1.4 copy-start.18
  212.6 1.4 copy-start.19
  212.6 1.4 copy-start.20
  215.4 11.2 %collective-permute-start.5 = (f32[655,128]{1,0:T(8,128)}, f32[655,128]{1,0:T(8,128)S(1)}, u32[]{:S(2)}, u32[]{:S(2)}) collective-permute-start(f32[655,128]{1,0:T(8,128)} %collective-permute-done.3), channel_id=1, source_target_pairs={{1,0},{2,1},{3,2},{4,3},{5,4},{6,5},{7,6},{8,7},{9,8},{10,9},{11,1... | collective-permute-start | bytes 1006088 | tf_op jit(solution)/shard_map/ppermute | solution.py:32
  218.1 15.9 %collective-permute-start.4 = (f32[655,128]{1,0:T(8,128)}, f32[655,128]{1,0:T(8,128)S(1)}, u32[]{:S(2)}, u32[]{:S(2)}) collective-permute-start(f32[655,128]{1,0:T(8,128)} %collective-permute-done.2), channel_id=1, source_target_pairs={{0,1},{1,2},{2,3},{3,4},{4,5},{5,6},{6,7},{7,8},{8,9},{9,10},{10,1... | collective-permute-start | bytes 1006088 | tf_op jit(solution)/shard_map/ppermute | solution.py:32
  220.7 3.4 %copy-start.28 = (f32[512,128]{1,0:T(8,128)S(1)}, f32[512,128]{1,0:T(8,128)}, u32[]{:S(2)}) copy-start(f32[512,128]{1,0:T(8,128)} %fusion.16) | copy-start | bytes 786436
  226.6 12.4 %collective-permute-start.7 = (f32[655,128]{1,0:T(8,128)S(1)}, f32[655,128]{1,0:T(8,128)S(1)}, u32[]{:S(2)}, u32[]{:S(2)}) collective-permute-start(f32[655,128]{1,0:T(8,128)S(1)} %collective-permute-done.5), channel_id=1, source_target_pairs={{1,0},{2,1},{3,2},{4,3},{5,4},{6,5},{7,6},{8,7},{9,8},{10,9},{11,1... | collective-permute-start | bytes 1006088 | tf_op jit(solution)/shard_map/ppermute | solution.py:32
  234.0 12.9 %collective-permute-start.6 = (f32[655,128]{1,0:T(8,128)S(1)}, f32[655,128]{1,0:T(8,128)S(1)}, u32[]{:S(2)}, u32[]{:S(2)}) collective-permute-start(f32[655,128]{1,0:T(8,128)S(1)} %collective-permute-done.4), channel_id=1, source_target_pairs={{0,1},{1,2},{2,3},{3,4},{4,5},{5,6},{6,7},{7,8},{8,9},{9,10},{10,1... | collective-permute-start | bytes 1006088 | tf_op jit(solution)/shard_map/ppermute | solution.py:32
  239.0 12.9 %collective-permute-start.9 = (f32[655,128]{1,0:T(8,128)S(1)}, f32[655,128]{1,0:T(8,128)S(1)}, u32[]{:S(2)}, u32[]{:S(2)}) collective-permute-start(f32[655,128]{1,0:T(8,128)S(1)} %collective-permute-done.7), channel_id=1, source_target_pairs={{1,0},{2,1},{3,2},{4,3},{5,4},{6,5},{7,6},{8,7},{9,8},{10,9},{11,1... | collective-permute-start | bytes 1006088 | tf_op jit(solution)/shard_map/ppermute | solution.py:32
  246.9 12.9 %collective-permute-start.8 = (f32[655,128]{1,0:T(8,128)S(1)}, f32[655,128]{1,0:T(8,128)S(1)}, u32[]{:S(2)}, u32[]{:S(2)}) collective-permute-start(f32[655,128]{1,0:T(8,128)S(1)} %collective-permute-done.6), channel_id=1, source_target_pairs={{0,1},{1,2},{2,3},{3,4},{4,5},{5,6},{6,7},{7,8},{8,9},{9,10},{10,1... | collective-permute-start | bytes 1006088 | tf_op jit(solution)/shard_map/ppermute | solution.py:32
  252.0 12.9 %collective-permute-start.11 = (f32[655,128]{1,0:T(8,128)S(1)}, f32[655,128]{1,0:T(8,128)S(1)}, u32[]{:S(2)}, u32[]{:S(2)}) collective-permute-start(f32[655,128]{1,0:T(8,128)S(1)} %collective-permute-done.9), channel_id=1, source_target_pairs={{1,0},{2,1},{3,2},{4,3},{5,4},{6,5},{7,6},{8,7},{9,8},{10,9},{11,1... | collective-permute-start | bytes 1006088 | tf_op jit(solution)/shard_map/ppermute | solution.py:32
  259.9 12.9 %collective-permute-start.10 = (f32[655,128]{1,0:T(8,128)S(1)}, f32[655,128]{1,0:T(8,128)S(1)}, u32[]{:S(2)}, u32[]{:S(2)}) collective-permute-start(f32[655,128]{1,0:T(8,128)S(1)} %collective-permute-done.8), channel_id=1, source_target_pairs={{0,1},{1,2},{2,3},{3,4},{4,5},{5,6},{6,7},{7,8},{8,9},{9,10},{10,1... | collective-permute-start | bytes 1006088 | tf_op jit(solution)/shard_map/ppermute | solution.py:32
  264.9 12.9 %collective-permute-start.13 = (f32[655,128]{1,0:T(8,128)S(1)}, f32[655,128]{1,0:T(8,128)S(1)}, u32[]{:S(2)}, u32[]{:S(2)}) collective-permute-start(f32[655,128]{1,0:T(8,128)S(1)} %collective-permute-done.11), channel_id=1, source_target_pairs={{1,0},{2,1},{3,2},{4,3},{5,4},{6,5},{7,6},{8,7},{9,8},{10,9},{11,1... | collective-permute-start | bytes 1006088 | tf_op jit(solution)/shard_map/ppermute | solution.py:32
  272.8 12.9 %collective-permute-start.12 = (f32[655,128]{1,0:T(8,128)S(1)}, f32[655,128]{1,0:T(8,128)S(1)}, u32[]{:S(2)}, u32[]{:S(2)}) collective-permute-start(f32[655,128]{1,0:T(8,128)S(1)} %collective-permute-done.10), channel_id=1, source_target_pairs={{0,1},{1,2},{2,3},{3,4},{4,5},{5,6},{6,7},{7,8},{8,9},{9,10},{10,1... | collective-permute-start | bytes 1006088 | tf_op jit(solution)/shard_map/ppermute | solution.py:32
  277.8 23.5 %collective-permute-start.15 = (f32[655,128]{1,0:T(8,128)S(1)}, f32[655,128]{1,0:T(8,128)S(1)}, u32[]{:S(2)}, u32[]{:S(2)}) collective-permute-start(f32[655,128]{1,0:T(8,128)S(1)} %collective-permute-done.13), channel_id=1, source_target_pairs={{1,0},{2,1},{3,2},{4,3},{5,4},{6,5},{7,6},{8,7},{9,8},{10,9},{11,1... | collective-permute-start | bytes 1006088 | tf_op jit(solution)/shard_map/ppermute | solution.py:32
  285.7 12.7 %collective-permute-start.14 = (f32[655,128]{1,0:T(8,128)S(1)}, f32[655,128]{1,0:T(8,128)S(1)}, u32[]{:S(2)}, u32[]{:S(2)}) collective-permute-start(f32[655,128]{1,0:T(8,128)S(1)} %collective-permute-done.12), channel_id=1, source_target_pairs={{0,1},{1,2},{2,3},{3,4},{4,5},{5,6},{6,7},{7,8},{8,9},{9,10},{10,1... | collective-permute-start | bytes 1006088 | tf_op jit(solution)/shard_map/ppermute | solution.py:32
  298.4 2.9 copy-start.9
  301.4 0.7 copy-start.7
  303.4 1.0 copy-start.24
  303.4 1.0 copy-start.25
  303.4 1.0 copy-start.26
  304.4 1.5 copy-start.8
  304.4 1.5 copy-start.10
  305.9 1.5 copy-start.27
  (3 other events, 2.0 us)
where the time goes:
time: 315 us; the launch traced here: 310 us
  starting transfers between devices  159 us (50%)
  matrix products  38.3 us (12%)
  waiting for transfers between devices  38.3 us (12%)
  Pallas kernels  32.3 us (10%)
  local copies, waits for them, and re-layouts  18.5 us (6%)
  blocking collectives  16.6 us (5%)
  other arithmetic  4.71 us (1%)
    ppermute x32, starting transfers between devices, from_behind(): return lax.ppermute(block, axis, route)  147 us
    pallas_call x1, Pallas kernels, cluster_gather_kernel(): pl.pallas_call(functools.partial(gather_kernel, clusters), out_shape=jax....  32.3 us
    dot_general x17, matrix products, contribution(): jnp.dot(kernel_block(own_points, coords), block[:leaf_points], precision=...  31.4 us
    ppermute x32, waiting for transfers between devices, from_behind(): return lax.ppermute(block, axis, route)  30.5 us
    all_gather x1, blocking collectives, per_device(): local_top = lax.all_gather(top_cols, MEMBERS, axis=1, tiled=True)  16.6 us
    ppermute x6, starting transfers between devices, from_partner(): return lax.ppermute(value, axis, pairs)  12 us
    ppermute x6, waiting for transfers between devices, from_partner(): return lax.ppermute(value, axis, pairs)  7.81 us
  transfers between devices with their start and end apart: 38, of which 7 were waited for; matrix products, arithmetic and copies ran while one was open for 16% of the time, Pallas kernels for 10%

commit v1 on v0

--- a/solution.py
+++ b/solution.py
@@ -160,10 +160,13 @@
     return total, jnp.stack(rim)
 
 
-def middle_full(coefs, skeletons, lists, transfer, above, stride, device):
+def slot_of(distance):
+    return distance + FAR_REACH - (distance > 0).astype(jnp.int32)
+
+
+def middle_full(stacked, skeletons, lists, transfer, above, stride, device):
     cluster = device // stride
     own_coords = lax.dynamic_index_in_dim(skeletons, cluster, 0, keepdims=False)
-    stacked, slot_of = partner_stack(coefs, stride)
     entries = lax.dynamic_index_in_dim(lists, cluster, 0, keepdims=False)
     chosen = jnp.maximum(entries, 0)
     coords = jnp.take(skeletons, chosen, axis=0)
@@ -174,10 +177,42 @@
     )
 
 
-def gather_kernel(clusters, block_ref, out_ref, landing, send_sem, recv_sem):
+OFFSETS = tuple(range(-FAR_REACH, 0)) + tuple(range(1, FAR_REACH + 1))
+
+
+def device_coords(linear):
+    return (linear // 8, linear // 4 % 2, linear // 2 % 2, linear % 2)
+
+
+def exchange_kernel(
+    clusters,
+    top_ref,
+    pair_ref,
+    quad_ref,
+    top_out,
+    pair_out,
+    quad_out,
+    top_land,
+    pair_land,
+    quad_land,
+    top_send,
+    top_recv,
+    pair_send,
+    pair_recv,
+    quad_send,
+    quad_recv,
+):
     me = lax.axis_index("cl")
+    dev = lax.axis_index(AX)
+    count = clusters * 8
     mesh_id = pl.DeviceIdType.MESH
+    pair_land[...] = jnp.zeros(pair_land.shape, jnp.float32)
+    quad_land[...] = jnp.zeros(quad_land.shape, jnp.float32)
     barrier = pltpu.get_barrier_semaphore()
+    extra = (-12, -6, -4, -2, 2, 4, 6, 12)
+
+    def inside(delta):
+        return jnp.logical_and(dev + delta >= 0, dev + delta < count)
 
     def greet(step, carry):
         peer = lax.rem(me + step, clusters)
@@ -185,15 +220,22 @@
         return carry
 
     lax.fori_loop(1, clusters, greet, 0)
-    pl.semaphore_wait(barrier, clusters - 1)
+    for delta in extra:
+        pl.semaphore_signal(
+            barrier,
+            inc=1,
+            device_id=device_coords(lax.rem(dev + delta + count, count)),
+            device_id_type=mesh_id,
+        )
+    pl.semaphore_wait(barrier, clusters - 1 + len(extra))
 
     def outgoing(step):
         peer = lax.rem(me + step, clusters)
         return pltpu.make_async_remote_copy(
-            src_ref=block_ref,
-            dst_ref=landing.at[me],
-            send_sem=send_sem.at[step],
-            recv_sem=recv_sem.at[me],
+            src_ref=top_ref,
+            dst_ref=top_land.at[me],
+            send_sem=top_send.at[step],
+            recv_sem=top_recv.at[me],
             device_id={"cl": peer},
             device_id_type=mesh_id,
         )
@@ -201,20 +243,41 @@
     def incoming(step):
         source = lax.rem(me - step + clusters, clusters)
         return pltpu.make_async_remote_copy(
-            src_ref=block_ref,
-            dst_ref=landing.at[source],
-            send_sem=send_sem.at[step],
-            recv_sem=recv_sem.at[source],
+            src_ref=top_ref,
+            dst_ref=top_land.at[source],
+            send_sem=top_send.at[step],
+            recv_sem=top_recv.at[source],
             device_id={"cl": source},
             device_id_type=mesh_id,
         )
+
+    def partner_copy(src, land, send_sem, recv_sem, slot, target):
+        return pltpu.make_async_remote_copy(
+            src_ref=src,
+            dst_ref=land.at[slot],
+            send_sem=send_sem.at[slot],
+            recv_sem=recv_sem.at[slot],
+            device_id=device_coords(target),
+            device_id_type=mesh_id,
+        )
+
+    partners = (
+        (pair_ref, pair_land, pair_send, pair_recv, 2),
+        (quad_ref, quad_land, quad_send, quad_recv, 4),
+    )
+    for src, land, send_sem, recv_sem, stride in partners:
+        for slot, offset in enumerate(OFFSETS):
+
+            @pl.when(inside(-offset * stride))
+            def _():
+                partner_copy(src, land, send_sem, recv_sem, slot, dev - offset * stride).start()
 
     def send(step, carry):
         outgoing(step).start()
         return carry
 
     lax.fori_loop(1, clusters, send, 0)
-    landing[me] = block_ref[...]
+    top_land[me] = top_ref[...]
 
     def finish(step, carry):
         outgoing(step).wait_send()
@@ -222,24 +285,49 @@
         return carry
 
     lax.fori_loop(1, clusters, finish, 0)
-    out_ref[...] = landing[...]
-
-
-def cluster_gather_kernel(block):
+    for src, land, send_sem, recv_sem, stride in partners:
+        for slot, offset in enumerate(OFFSETS):
+
+            @pl.when(inside(-offset * stride))
+            def _():
+                partner_copy(src, land, send_sem, recv_sem, slot, dev - offset * stride).wait_send()
+
+            @pl.when(inside(offset * stride))
+            def _():
+                partner_copy(src, land, send_sem, recv_sem, slot, dev + offset * stride).wait_recv()
+
+    top_out[...] = top_land[...]
+    pair_out[...] = pair_land[...]
+    quad_out[...] = quad_land[...]
+
+
+def exchange(top_block, coef_pair, coef_quad):
     clusters = lax.axis_size("cl")
-    rows, cols = block.shape
+    rows, cols = top_block.shape
+    stack = (len(OFFSETS),) + coef_pair.shape
+    vmem = pl.BlockSpec(memory_space=pltpu.VMEM)
     return pl.pallas_call(
-        functools.partial(gather_kernel, clusters),
-        out_shape=jax.ShapeDtypeStruct((clusters, rows, cols), jnp.float32),
-        in_specs=[pl.BlockSpec(memory_space=pltpu.VMEM)],
-        out_specs=pl.BlockSpec(memory_space=pltpu.VMEM),
+        functools.partial(exchange_kernel, clusters),
+        out_shape=(
+            jax.ShapeDtypeStruct((clusters, rows, cols), jnp.float32),
+            jax.ShapeDtypeStruct(stack, jnp.float32),
+            jax.ShapeDtypeStruct(stack, jnp.float32),
+        ),
+        in_specs=[vmem] * 3,
+        out_specs=(vmem, vmem, vmem),
         scratch_shapes=[
             pltpu.VMEM((clusters, rows, cols), jnp.float32),
+            pltpu.VMEM(stack, jnp.float32),
+            pltpu.VMEM(stack, jnp.float32),
             pltpu.SemaphoreType.DMA((clusters,)),
             pltpu.SemaphoreType.DMA((clusters,)),
+            pltpu.SemaphoreType.DMA((len(OFFSETS),)),
+            pltpu.SemaphoreType.DMA((len(OFFSETS),)),
+            pltpu.SemaphoreType.DMA((len(OFFSETS),)),
+            pltpu.SemaphoreType.DMA((len(OFFSETS),)),
         ],
         compiler_params=pltpu.CompilerParams(collective_id=0, has_side_effects=True),
-    )(block)
+    )(top_block, coef_pair, coef_quad)
 
 
 def per_device(
@@ -281,12 +369,12 @@
         axis=0,
     )
     near_field, leaf_rim = near_sum(own_points, near_list[0], shipped, device)
-    coef_top, coef_pair, coef_quad = lax.optimization_barrier((coef_top, coef_pair, coef_quad))
     top_cluster = device // 8
     top_member = device % 8
     share = width // 8
     top_cols_own = lax.dynamic_slice_in_dim(coef_top.T, top_member * share, share, 0)
-    all_top = jnp.swapaxes(cluster_gather_kernel(top_cols_own), 1, 2)
+    top_t, pair_stack, quad_stack = exchange(top_cols_own, coef_pair, coef_quad)
+    all_top = jnp.swapaxes(top_t, 1, 2)
     top_coords = lax.dynamic_index_in_dim(skel_top, top_cluster, 0, keepdims=False)
     top_entries = lax.dynamic_index_in_dim(far_top, top_cluster, 0, keepdims=False)
     top_chosen = jnp.maximum(top_entries, 0)
@@ -297,8 +385,8 @@
         top_entries >= 0,
     )
     local_top = lax.all_gather(top_cols, MEMBERS, axis=1, tiled=True)
-    local_quad = middle_full(coef_quad, skel_quad, far_quad, quad_matrix, local_top, 4, device)
-    local_pair = middle_full(coef_pair, skel_pair, far_pair, pair_matrix, local_quad, 2, device)
+    local_quad = middle_full(quad_stack, skel_quad, far_quad, quad_matrix, local_top, 4, device)
+    local_pair = middle_full(pair_stack, skel_pair, far_pair, pair_matrix, local_quad, 2, device)
     leaf_entries = far_leaf[0]
     positions = jnp.clip(jnp.maximum(leaf_entries, 0) - device + REACH, 0, 2 * REACH)
     leaf_blocks = jnp.take(leaf_rim, positions, axis=0)

time: 315 us -> 263 us (0.83); the launches traced: 310 us -> 261 us
  starting transfers between devices: 159 us -> 95.6 us
  Pallas kernels: 32.3 us -> 79.1 us
  waiting for transfers between devices: 38.3 us -> 14.6 us
  local copies, waits for them, and re-layouts: 18.5 us -> 14.4 us
    ppermute x32 -> x16, starting transfers between devices: 147 us -> 83.6 us  [from_behind(): return lax.ppermute(block, axis, route)]
    pallas_call x1, Pallas kernels: 32.3 us -> 79.1 us  [exchange(): pl.pallas_call(functools.partial(exchange_kernel, clusters), out_shape=(j...]
    ppermute x32 -> x16, waiting for transfers between devices: 30.5 us -> 6.83 us  [from_behind(): return lax.ppermute(block, axis, route)]
  transfers between devices with their start and end apart: 38 -> 22, of which waited for: 7 -> 4; matrix products, arithmetic and copies ran while one was open for 16% -> 17% of each run, Pallas kernels for 10% -> 30%
where the time goes in v1:
time: 263 us; the launch traced here: 261 us
  starting transfers between devices  95.6 us (36%)
  Pallas kernels  79.1 us (30%)
  matrix products  37.4 us (14%)
  waiting for transfers between devices  14.6 us (6%)
  local copies, waits for them, and re-layouts  14.4 us (5%)
  blocking collectives  14 us (5%)
  other arithmetic  4.63 us (2%)
    ppermute x16, starting transfers between devices, from_behind(): return lax.ppermute(block, axis, route)  83.6 us
    pallas_call x1, Pallas kernels, exchange(): pl.pallas_call(functools.partial(exchange_kernel, clusters), out_shape=(j...  79.1 us
    dot_general x17, matrix products, contribution(): jnp.dot(kernel_block(own_points, coords), block[:leaf_points], precision=...  30.5 us
    all_gather x1, blocking collectives, per_device(): local_top = lax.all_gather(top_cols, MEMBERS, axis=1, tiled=True)  14 us
    ppermute x6, starting transfers between devices, from_partner(): return lax.ppermute(value, axis, pairs)  12 us
    ppermute x6, waiting for transfers between devices, from_partner(): return lax.ppermute(value, axis, pairs)  7.76 us
    ppermute x16, waiting for transfers between devices, from_behind(): return lax.ppermute(block, axis, route)  6.83 us
  transfers between devices with their start and end apart: 22, of which 4 were waited for; matrix products, arithmetic and copies ran while one was open for 17% of the time, Pallas kernels for 30%

profile of v1, /device:TPU:24, one launch (start us, length us, event | category | flops | bytes accessed | tf_op | source)
XLA Modules:
  0.0 261.0 jit_solution(8166709615926346341)
XLA Ops:
  0.1 0.8 copy.50
  0.9 0.7 reduce.17
  1.7 1.6 fusion.407
  3.3 1.0 pad_maximum_fusion
  4.3 1.9 collective-permute-start
  6.2 13.2 %collective-permute-start.1 = (f32[655,128]{1,0:T(8,128)S(1)}, f32[655,128]{1,0:T(8,128)S(1)}, u32[]{:S(2)}, u32[]{:S(2)}) collective-permute-start(f32[655,128]{1,0:T(8,128)S(1)} %pad_maximum_fusion), channel_id=1, source_target_pairs={{1,0},{2,1},{3,2},{4,3},{5,4},{6,5},{7,6},{8,7},{9,8},{10,9},{11,1... | collective-permute-start | bytes 1006088 | tf_op jit(solution)/shard_map/ppermute | solution.py:32
  19.5 1.9 collective-permute-start.16
  21.4 2.4 collective-permute-start.17
  25.4 1.6 gather_fusion.1
  28.6 1.0 compare_reduce_fusion.8
  29.6 1.6 convolution_select_fusion.16
  31.2 0.7 fusion.478
  32.1 1.9 collective-permute-start.18
  34.3 3.6 %collective-permute-done.18 = f32[64,128]{1,0:T(8,128)S(1)} collective-permute-done((f32[64,128]{1,0:T(8,128)S(1)}, f32[64,128]{1,0:T(8,128)S(1)}, u32[]{:S(2)}, u32[]{:S(2)}) %collective-permute-start.18) | collective-permute-done | bytes 32800 | tf_op jit(solution)/shard_map/ppermute | solution.py:26
  38.2 1.9 collective-permute-start.19
  40.2 1.4 collective-permute-done.19
  42.2 1.9 collective-permute-start.20
  44.2 2.0 collective-permute-start.2
  46.2 7.7 %collective-permute-start.3 = (f32[655,128]{1,0:T(8,128)S(1)}, f32[655,128]{1,0:T(8,128)}, u32[]{:S(2)}, u32[]{:S(2)}) collective-permute-start(f32[655,128]{1,0:T(8,128)S(1)} %collective-permute-done.1), channel_id=1, source_target_pairs={{1,0},{2,1},{3,2},{4,3},{5,4},{6,5},{7,6},{8,7},{9,8},{10,9},{11,1... | collective-permute-start | bytes 1006088 | tf_op jit(solution)/shard_map/ppermute | solution.py:32
  54.0 1.6 fusion.17
  55.6 0.6 slice_bitcast_fusion.16
  56.2 1.9 collective-permute-start.21
  58.2 2.3 fusion.16
  60.5 2.8 %collective-permute-done.21 = f32[128,128]{1,0:T(8,128)S(1)} collective-permute-done((f32[128,128]{1,0:T(8,128)S(1)}, f32[128,128]{1,0:T(8,128)S(1)}, u32[]{:S(2)}, u32[]{:S(2)}) %collective-permute-start.21) | collective-permute-done | bytes 65568 | tf_op jit(solution)/shard_map/ppermute | solution.py:26
  63.4 0.7 copy.36.top_ref
  64.1 79.1 %shard_map.145 = (f32[64,16,128]{2,1,0:T(8,128)}, f32[8,128,128]{2,1,0:T(8,128)}, f32[8,128,128]{2,1,0:T(8,128)}) custom-call(f32[16,128]{1,0:T(8,128)} %copy.36.top_ref, f32[128,128]{1,0:T(8,128)} %slice_bitcast_fusion.17.pair_ref, f32[128,128]{1,0:T(8,128)} %get-tuple-element.93.quad_ref), custom_call_target="tpu_custom_call" | custom-call | tf_op jit(solution)/shard_map/pallas_call | solution.py:309
  143.2 1.6 gather_fusion.4
  144.8 0.8 fusion.206
  145.6 14.0 %all_gather.3 = f32[128,128]{0,1:T(8,128)S(1)} all-gather(f32[128,16]{0,1:T(8,128)S(1)} %fusion.206), channel_id=1, replica_groups=mesh['cl'=64,'q'=2,'p'=2,'c'=2] {'q','p','c'}, dimensions={1}, use_global_device_ids=true | all-gather | bytes 73728 | tf_op jit(solution)/shard_map/all_gather | solution.py:387
  161.0 0.9 fusion.230
  161.9 0.9 fusion.218
  163.3 7.5 %collective-permute-start.5 = (f32[655,128]{1,0:T(8,128)}, f32[655,128]{1,0:T(8,128)S(1)}, u32[]{:S(2)}, u32[]{:S(2)}) collective-permute-start(f32[655,128]{1,0:T(8,128)} %collective-permute-done.3), channel_id=1, source_target_pairs={{1,0},{2,1},{3,2},{4,3},{5,4},{6,5},{7,6},{8,7},{9,8},{10,9},{11,1... | collective-permute-start | bytes 1006088 | tf_op jit(solution)/shard_map/ppermute | solution.py:32
  170.8 0.7 slice_bitcast_fusion.67
  171.6 2.1 collective-permute-start.4
  173.7 2.6 %convolution_select_fusion.12 = f32[512,128]{1,0:T(8,128)S(1)} fusion(f32[512]{0:T(512)S(1)} %get-tuple-element.70, f32[512]{0:T(512)S(1)} %get-tuple-element.71, f32[512]{0:T(512)S(1)} %get-tuple-element.69, f32[512]{0:T(512)S(1)} %bitcast.342, f32[512]{0:T(512)S(1)} %bitcast.325, f32[512]{0:T(512)S(1)} %bitcast.308, ...), kind=kOutput, calls=%fused_computation.34 | convolution fusion | flops 204013568 | bytes 537088 | tf_op jit(solution)/shard_map/dot_general | solution.py:144
  176.3 0.8 slice_bitcast_fusion.70
  177.1 2.5 fusion.15
  179.6 7.9 %collective-permute-start.7 = (f32[655,128]{1,0:T(8,128)S(1)}, f32[655,128]{1,0:T(8,128)S(1)}, u32[]{:S(2)}, u32[]{:S(2)}) collective-permute-start(f32[655,128]{1,0:T(8,128)S(1)} %collective-permute-done.5), channel_id=1, source_target_pairs={{1,0},{2,1},{3,2},{4,3},{5,4},{6,5},{7,6},{8,7},{9,8},{10,9},{11,1... | collective-permute-start | bytes 1006088 | tf_op jit(solution)/shard_map/ppermute | solution.py:32
  187.5 1.9 collective-permute-start.6
  189.4 1.5 convolution_select_fusion.10
  191.0 1.5 fusion.13
  192.5 7.9 %collective-permute-start.9 = (f32[655,128]{1,0:T(8,128)S(1)}, f32[655,128]{1,0:T(8,128)S(1)}, u32[]{:S(2)}, u32[]{:S(2)}) collective-permute-start(f32[655,128]{1,0:T(8,128)S(1)} %collective-permute-done.7), channel_id=1, source_target_pairs={{1,0},{2,1},{3,2},{4,3},{5,4},{6,5},{7,6},{8,7},{9,8},{10,9},{11,1... | collective-permute-start | bytes 1006088 | tf_op jit(solution)/shard_map/ppermute | solution.py:32
  200.3 1.9 collective-permute-start.8
  202.3 1.6 convolution_select_fusion.8
  203.8 1.5 fusion.11
  205.4 7.9 %collective-permute-start.11 = (f32[655,128]{1,0:T(8,128)S(1)}, f32[655,128]{1,0:T(8,128)S(1)}, u32[]{:S(2)}, u32[]{:S(2)}) collective-permute-start(f32[655,128]{1,0:T(8,128)S(1)} %collective-permute-done.9), channel_id=1, source_target_pairs={{1,0},{2,1},{3,2},{4,3},{5,4},{6,5},{7,6},{8,7},{9,8},{10,9},{11,1... | collective-permute-start | bytes 1006088 | tf_op jit(solution)/shard_map/ppermute | solution.py:32
  213.3 1.9 collective-permute-start.10
  215.2 1.6 convolution_select_fusion.6
  216.8 1.6 fusion.9
  218.4 7.9 %collective-permute-start.13 = (f32[655,128]{1,0:T(8,128)S(1)}, f32[655,128]{1,0:T(8,128)S(1)}, u32[]{:S(2)}, u32[]{:S(2)}) collective-permute-start(f32[655,128]{1,0:T(8,128)S(1)} %collective-permute-done.11), channel_id=1, source_target_pairs={{1,0},{2,1},{3,2},{4,3},{5,4},{6,5},{7,6},{8,7},{9,8},{10,9},{11,1... | collective-permute-start | bytes 1006088 | tf_op jit(solution)/shard_map/ppermute | solution.py:32
  226.3 1.9 collective-permute-start.12
  228.2 1.5 convolution_select_fusion.4
  229.8 1.5 fusion.7
  231.3 7.9 %collective-permute-start.15 = (f32[655,128]{1,0:T(8,128)S(1)}, f32[655,128]{1,0:T(8,128)S(1)}, u32[]{:S(2)}, u32[]{:S(2)}) collective-permute-start(f32[655,128]{1,0:T(8,128)S(1)} %collective-permute-done.13), channel_id=1, source_target_pairs={{1,0},{2,1},{3,2},{4,3},{5,4},{6,5},{7,6},{8,7},{9,8},{10,9},{11,1... | collective-permute-start | bytes 1006088 | tf_op jit(solution)/shard_map/ppermute | solution.py:32
  239.2 2.1 collective-permute-start.14
  241.4 1.5 convolution_select_fusion.2
  242.9 2.3 fusion.5
  245.1 6.8 %collective-permute-done.14 = f32[655,128]{1,0:T(8,128)S(1)} collective-permute-done((f32[655,128]{1,0:T(8,128)S(1)}, f32[655,128]{1,0:T(8,128)S(1)}, u32[]{:S(2)}, u32[]{:S(2)}) %collective-permute-start.14) | collective-permute-done | bytes 335392 | tf_op jit(solution)/shard_map/ppermute | solution.py:32
  252.0 0.9 fusion.450
  253.0 0.9 fusion.447
  254.0 0.7 copy-done.9
  255.6 0.9 fusion.242
  257.1 1.6 convolution_select_fusion
  258.8 2.2 fusion.3
  (147 shorter events, 8.1 us)
Async XLA Ops:
  0.0 1.7 copy-start
  0.0 24.1 %copy-start.17 = (f32[1,3,128]{2,0,1:T(1,128)S(1)}, f32[1,3,128]{2,0,1:T(1,128)}, u32[]{:S(2)}) copy-start(f32[1,3,128]{2,0,1:T(1,128)} %param.23) | copy-start | bytes 4612
  0.0 25.0 %copy-start.8 = (f32[1,3,512]{2,0,1:T(1,128)S(1)}, f32[1,3,512]{2,0,1:T(1,128)}, u32[]{:S(2)}) copy-start(f32[1,3,512]{2,0,1:T(1,128)} %param.18) | copy-start | bytes 18436
  0.0 19.4 %copy-start.6 = (f32[64,128]{1,0:T(8,128)S(1)}, f32[64,128]{1,0:T(8,128)}, u32[]{:S(2)}) copy-start(f32[64,128]{1,0:T(8,128)} %param.21) | copy-start | bytes 98308
  0.0 21.4 %copy-start.13 = (f32[32,128]{1,0:T(8,128)S(1)}, f32[32,128]{1,0:T(8,128)}, u32[]{:S(2)}) copy-start(f32[32,128]{1,0:T(8,128)} %param.22) | copy-start | bytes 49156
  0.0 23.8 %copy-start.18 = (s32[1,8]{1,0:T(1,128)S(1)}, s32[1,8]{1,0:T(1,128)}, u32[]{:S(2)}) copy-start(s32[1,8]{1,0:T(1,128)} %param.28) | copy-start | bytes 100
  0.0 24.1 %copy-start.16 = (s32[256,8]{0,1:T(8,128)S(1)}, s32[256,8]{0,1:T(8,128)}, u32[]{:S(2)}) copy-start(s32[256,8]{0,1:T(8,128)} %param.29) | copy-start | bytes 24580
  0.1 24.5 %copy-start.14 = (s32[128,8]{0,1:T(8,128)S(1)}, s32[128,8]{0,1:T(8,128)}, u32[]{:S(2)}) copy-start(s32[128,8]{0,1:T(8,128)} %param.30) | copy-start | bytes 12292
  0.1 24.5 %copy-start.15 = (s32[64,8]{0,1:T(8,128)S(1)}, s32[64,8]{0,1:T(8,128)}, u32[]{:S(2)}) copy-start(s32[64,8]{0,1:T(8,128)} %param.31) | copy-start | bytes 6148
  0.1 25.0 %copy-start.4 = (f32[1,128,128]{2,1,0:T(8,128)S(1)}, f32[1,128,128]{2,1,0:T(8,128)}, u32[]{:S(2)}) copy-start(f32[1,128,128]{2,1,0:T(8,128)} %param.20) | copy-start | bytes 196612
  0.1 27.0 %copy-start.7 = (f32[128,3,128]{2,0,1:T(8,128)S(1)}, f32[128,3,128]{2,0,1:T(8,128)}, u32[]{:S(2)}) copy-start(f32[128,3,128]{2,0,1:T(8,128)} %param.25) | copy-start | bytes 589828
  0.1 27.7 %copy-start.5 = (f32[64,3,128]{2,0,1:T(8,128)S(1)}, f32[64,3,128]{2,0,1:T(8,128)}, u32[]{:S(2)}) copy-start(f32[64,3,128]{2,0,1:T(8,128)} %param.26) | copy-start | bytes 294916
  1.7 26.9 %copy-start.19 = (s32[1,16]{1,0:T(1,128)S(1)}, s32[1,16]{1,0:T(1,128)}, u32[]{:S(2)}) copy-start(s32[1,16]{1,0:T(1,128)} %param.27) | copy-start | bytes 196
  1.7 27.9 %copy-start.1 = (f32[1,512,128]{2,1,0:T(8,128)S(1)}, f32[1,512,128]{2,1,0:T(8,128)}, u32[]{:S(2)}) copy-start(f32[1,512,128]{2,1,0:T(8,128)} %param.17) | copy-start | bytes 786436
  4.3 39.9 %collective-permute-start = (f32[655,128]{1,0:T(8,128)S(1)}, f32[655,128]{1,0:T(8,128)S(1)}, u32[]{:S(2)}, u32[]{:S(2)}) collective-permute-start(f32[655,128]{1,0:T(8,128)S(1)} %pad_maximum_fusion), channel_id=1, source_target_pairs={{0,1},{1,2},{2,3},{3,4},{4,5},{5,6},{6,7},{7,8},{8,9},{9,10},{10,1... | collective-permute-start | bytes 1006088 | tf_op jit(solution)/shard_map/ppermute | solution.py:32
  6.2 40.0 %collective-permute-start.1 = (f32[655,128]{1,0:T(8,128)S(1)}, f32[655,128]{1,0:T(8,128)S(1)}, u32[]{:S(2)}, u32[]{:S(2)}) collective-permute-start(f32[655,128]{1,0:T(8,128)S(1)} %pad_maximum_fusion), channel_id=1, source_target_pairs={{1,0},{2,1},{3,2},{4,3},{5,4},{6,5},{7,6},{8,7},{9,8},{10,9},{11,1... | collective-permute-start | bytes 1006088 | tf_op jit(solution)/shard_map/ppermute | solution.py:32
  19.5 14.6 %collective-permute-start.16 = (f32[64,128]{1,0:T(8,128)S(1)}, f32[64,128]{1,0:T(8,128)S(1)}, u32[]{:S(2)}, u32[]{:S(2)}) collective-permute-start(f32[64,128]{1,0:T(8,128)S(1)} %copy-done.6), channel_id=1, source_target_pairs={{0,1},{1,0},{2,3},{3,2},{4,5},{5,4},{6,7},{7,6},{8,9},{9,8},{10,11... | collective-permute-start | bytes 98312 | tf_op jit(solution)/shard_map/ppermute | solution.py:26
  21.4 10.7 %collective-permute-start.17 = (f32[32,128]{1,0:T(8,128)S(1)}, f32[32,128]{1,0:T(8,128)S(1)}, u32[]{:S(2)}, u32[]{:S(2)}) collective-permute-start(f32[32,128]{1,0:T(8,128)S(1)} %copy-done.13), channel_id=1, source_target_pairs={{0,1},{1,0},{2,3},{3,2},{4,5},{5,4},{6,7},{7,6},{8,9},{9,8},{10,11... | collective-permute-start | bytes 49160 | tf_op jit(solution)/shard_map/ppermute | solution.py:26
  32.1 5.8 %collective-permute-start.18 = (f32[64,128]{1,0:T(8,128)S(1)}, f32[64,128]{1,0:T(8,128)S(1)}, u32[]{:S(2)}, u32[]{:S(2)}) collective-permute-start(f32[64,128]{1,0:T(8,128)S(1)} %maximum_select_fusion.6), channel_id=1, source_target_pairs={{0,2},{1,3},{2,0},{3,1},{4,6},{5,7},{6,4},{7,5},{8,10},{9,11},{10,... | collective-permute-start | bytes 98312 | tf_op jit(solution)/shard_map/ppermute | solution.py:26
  38.2 3.3 %collective-permute-start.19 = (f32[3,128,128]{2,1,0:T(8,128)S(1)}, f32[3,128,128]{2,1,0:T(8,128)S(1)}, u32[]{:S(2)}, u32[]{:S(2)}) collective-permute-start(f32[3,128,128]{2,1,0:T(8,128)S(1)} %pad_maximum_fusion.1), channel_id=1, source_target_pairs={{0,1},{1,0},{2,3},{3,2},{4,5},{5,4},{6,7},{7,6},{8,9},{9,8},{10,11... | collective-permute-start | bytes 589832 | tf_op jit(solution)/shard_map/ppermute | solution.py:26
  42.2 13.3 %collective-permute-start.20 = (f32[2,128,128]{2,1,0:T(8,128)S(1)}, f32[2,128,128]{2,1,0:T(8,128)S(1)}, u32[]{:S(2)}, u32[]{:S(2)}) collective-permute-start(f32[2,128,128]{2,1,0:T(8,128)S(1)} %slice.748), channel_id=1, source_target_pairs={{0,2},{1,3},{2,0},{3,1},{4,6},{5,7},{6,4},{7,5},{8,10},{9,11},{10,... | collective-permute-start | bytes 393224 | tf_op jit(solution)/shard_map/ppermute | solution.py:26
  44.2 127.4 %collective-permute-start.2 = (f32[655,128]{1,0:T(8,128)S(1)}, f32[655,128]{1,0:T(8,128)}, u32[]{:S(2)}, u32[]{:S(2)}) collective-permute-start(f32[655,128]{1,0:T(8,128)S(1)} %collective-permute-done), channel_id=1, source_target_pairs={{0,1},{1,2},{2,3},{3,4},{4,5},{5,6},{6,7},{7,8},{8,9},{9,10},{10,1... | collective-permute-start | bytes 1006088 | tf_op jit(solution)/shard_map/ppermute | solution.py:32
  46.2 117.1 %collective-permute-start.3 = (f32[655,128]{1,0:T(8,128)S(1)}, f32[655,128]{1,0:T(8,128)}, u32[]{:S(2)}, u32[]{:S(2)}) collective-permute-start(f32[655,128]{1,0:T(8,128)S(1)} %collective-permute-done.1), channel_id=1, source_target_pairs={{1,0},{2,1},{3,2},{4,3},{5,4},{6,5},{7,6},{8,7},{9,8},{10,9},{11,1... | collective-permute-start | bytes 1006088 | tf_op jit(solution)/shard_map/ppermute | solution.py:32
  56.2 7.0 %collective-permute-start.21 = (f32[128,128]{1,0:T(8,128)S(1)}, f32[128,128]{1,0:T(8,128)S(1)}, u32[]{:S(2)}, u32[]{:S(2)}) collective-permute-start(f32[128,128]{1,0:T(8,128)S(1)} %get-tuple-element.94), channel_id=1, source_target_pairs={{0,4},{1,5},{2,6},{3,7},{4,0},{5,1},{6,2},{7,3},{8,12},{9,13},{10,... | collective-permute-start | bytes 196616 | tf_op jit(solution)/shard_map/ppermute | solution.py:26
  143.2 16.4 %copy-start.3 = (f32[8,128,128]{2,1,0:T(8,128)S(1)}, f32[8,128,128]{2,1,0:T(8,128)}, u32[]{:S(2)}) copy-start(f32[8,128,128]{2,1,0:T(8,128)} %get-tuple-element.9) | copy-start | bytes 1572868
  144.8 15.3 %copy-start.2 = (f32[8,128,128]{2,1,0:T(8,128)S(1)}, f32[8,128,128]{2,1,0:T(8,128)}, u32[]{:S(2)}) copy-start(f32[8,128,128]{2,1,0:T(8,128)} %get-tuple-element.10) | copy-start | bytes 1572868
  163.3 16.2 %collective-permute-start.5 = (f32[655,128]{1,0:T(8,128)}, f32[655,128]{1,0:T(8,128)S(1)}, u32[]{:S(2)}, u32[]{:S(2)}) collective-permute-start(f32[655,128]{1,0:T(8,128)} %collective-permute-done.3), channel_id=1, source_target_pairs={{1,0},{2,1},{3,2},{4,3},{5,4},{6,5},{7,6},{8,7},{9,8},{10,9},{11,1... | collective-permute-start | bytes 1006088 | tf_op jit(solution)/shard_map/ppermute | solution.py:32
  171.6 15.9 %collective-permute-start.4 = (f32[655,128]{1,0:T(8,128)}, f32[655,128]{1,0:T(8,128)S(1)}, u32[]{:S(2)}, u32[]{:S(2)}) collective-permute-start(f32[655,128]{1,0:T(8,128)} %collective-permute-done.2), channel_id=1, source_target_pairs={{0,1},{1,2},{2,3},{3,4},{4,5},{5,6},{6,7},{7,8},{8,9},{9,10},{10,1... | collective-permute-start | bytes 1006088 | tf_op jit(solution)/shard_map/ppermute | solution.py:32
  173.7 3.4 %copy-start.21 = (f32[512,128]{1,0:T(8,128)S(1)}, f32[512,128]{1,0:T(8,128)}, u32[]{:S(2)}) copy-start(f32[512,128]{1,0:T(8,128)} %fusion.16) | copy-start | bytes 786436
  179.6 12.9 %collective-permute-start.7 = (f32[655,128]{1,0:T(8,128)S(1)}, f32[655,128]{1,0:T(8,128)S(1)}, u32[]{:S(2)}, u32[]{:S(2)}) collective-permute-start(f32[655,128]{1,0:T(8,128)S(1)} %collective-permute-done.5), channel_id=1, source_target_pairs={{1,0},{2,1},{3,2},{4,3},{5,4},{6,5},{7,6},{8,7},{9,8},{10,9},{11,1... | collective-permute-start | bytes 1006088 | tf_op jit(solution)/shard_map/ppermute | solution.py:32
  187.5 12.9 %collective-permute-start.6 = (f32[655,128]{1,0:T(8,128)S(1)}, f32[655,128]{1,0:T(8,128)S(1)}, u32[]{:S(2)}, u32[]{:S(2)}) collective-permute-start(f32[655,128]{1,0:T(8,128)S(1)} %collective-permute-done.4), channel_id=1, source_target_pairs={{0,1},{1,2},{2,3},{3,4},{4,5},{5,6},{6,7},{7,8},{8,9},{9,10},{10,1... | collective-permute-start | bytes 1006088 | tf_op jit(solution)/shard_map/ppermute | solution.py:32
  192.5 12.9 %collective-permute-start.9 = (f32[655,128]{1,0:T(8,128)S(1)}, f32[655,128]{1,0:T(8,128)S(1)}, u32[]{:S(2)}, u32[]{:S(2)}) collective-permute-start(f32[655,128]{1,0:T(8,128)S(1)} %collective-permute-done.7), channel_id=1, source_target_pairs={{1,0},{2,1},{3,2},{4,3},{5,4},{6,5},{7,6},{8,7},{9,8},{10,9},{11,1... | collective-permute-start | bytes 1006088 | tf_op jit(solution)/shard_map/ppermute | solution.py:32
  200.3 12.9 %collective-permute-start.8 = (f32[655,128]{1,0:T(8,128)S(1)}, f32[655,128]{1,0:T(8,128)S(1)}, u32[]{:S(2)}, u32[]{:S(2)}) collective-permute-start(f32[655,128]{1,0:T(8,128)S(1)} %collective-permute-done.6), channel_id=1, source_target_pairs={{0,1},{1,2},{2,3},{3,4},{4,5},{5,6},{6,7},{7,8},{8,9},{9,10},{10,1... | collective-permute-start | bytes 1006088 | tf_op jit(solution)/shard_map/ppermute | solution.py:32
  205.4 13.0 %collective-permute-start.11 = (f32[655,128]{1,0:T(8,128)S(1)}, f32[655,128]{1,0:T(8,128)S(1)}, u32[]{:S(2)}, u32[]{:S(2)}) collective-permute-start(f32[655,128]{1,0:T(8,128)S(1)} %collective-permute-done.9), channel_id=1, source_target_pairs={{1,0},{2,1},{3,2},{4,3},{5,4},{6,5},{7,6},{8,7},{9,8},{10,9},{11,1... | collective-permute-start | bytes 1006088 | tf_op jit(solution)/shard_map/ppermute | solution.py:32
  213.3 13.0 %collective-permute-start.10 = (f32[655,128]{1,0:T(8,128)S(1)}, f32[655,128]{1,0:T(8,128)S(1)}, u32[]{:S(2)}, u32[]{:S(2)}) collective-permute-start(f32[655,128]{1,0:T(8,128)S(1)} %collective-permute-done.8), channel_id=1, source_target_pairs={{0,1},{1,2},{2,3},{3,4},{4,5},{5,6},{6,7},{7,8},{8,9},{9,10},{10,1... | collective-permute-start | bytes 1006088 | tf_op jit(solution)/shard_map/ppermute | solution.py:32
  218.4 12.9 %collective-permute-start.13 = (f32[655,128]{1,0:T(8,128)S(1)}, f32[655,128]{1,0:T(8,128)S(1)}, u32[]{:S(2)}, u32[]{:S(2)}) collective-permute-start(f32[655,128]{1,0:T(8,128)S(1)} %collective-permute-done.11), channel_id=1, source_target_pairs={{1,0},{2,1},{3,2},{4,3},{5,4},{6,5},{7,6},{8,7},{9,8},{10,9},{11,1... | collective-permute-start | bytes 1006088 | tf_op jit(solution)/shard_map/ppermute | solution.py:32
  226.3 12.9 %collective-permute-start.12 = (f32[655,128]{1,0:T(8,128)S(1)}, f32[655,128]{1,0:T(8,128)S(1)}, u32[]{:S(2)}, u32[]{:S(2)}) collective-permute-start(f32[655,128]{1,0:T(8,128)S(1)} %collective-permute-done.10), channel_id=1, source_target_pairs={{0,1},{1,2},{2,3},{3,4},{4,5},{5,6},{6,7},{7,8},{8,9},{9,10},{10,1... | collective-permute-start | bytes 1006088 | tf_op jit(solution)/shard_map/ppermute | solution.py:32
  231.3 22.6 %collective-permute-start.15 = (f32[655,128]{1,0:T(8,128)S(1)}, f32[655,128]{1,0:T(8,128)S(1)}, u32[]{:S(2)}, u32[]{:S(2)}) collective-permute-start(f32[655,128]{1,0:T(8,128)S(1)} %collective-permute-done.13), channel_id=1, source_target_pairs={{1,0},{2,1},{3,2},{4,3},{5,4},{6,5},{7,6},{8,7},{9,8},{10,9},{11,1... | collective-permute-start | bytes 1006088 | tf_op jit(solution)/shard_map/ppermute | solution.py:32
  239.2 12.7 %collective-permute-start.14 = (f32[655,128]{1,0:T(8,128)S(1)}, f32[655,128]{1,0:T(8,128)S(1)}, u32[]{:S(2)}, u32[]{:S(2)}) collective-permute-start(f32[655,128]{1,0:T(8,128)S(1)} %collective-permute-done.12), channel_id=1, source_target_pairs={{0,1},{1,2},{2,3},{3,4},{4,5},{5,6},{6,7},{7,8},{8,9},{9,10},{10,1... | collective-permute-start | bytes 1006088 | tf_op jit(solution)/shard_map/ppermute | solution.py:32
  251.9 2.1 copy-start.11
  254.0 0.7 copy-start.9
  255.6 1.5 copy-start.10
  255.6 1.5 copy-start.12
  257.1 1.7 copy-start.20

commit v2 on v1

--- a/solution.py
+++ b/solution.py
@@ -188,28 +188,22 @@
     clusters,
     top_ref,
     pair_ref,
-    quad_ref,
     top_out,
     pair_out,
-    quad_out,
     top_land,
     pair_land,
-    quad_land,
     top_send,
     top_recv,
     pair_send,
     pair_recv,
-    quad_send,
-    quad_recv,
 ):
     me = lax.axis_index("cl")
     dev = lax.axis_index(AX)
     count = clusters * 8
     mesh_id = pl.DeviceIdType.MESH
     pair_land[...] = jnp.zeros(pair_land.shape, jnp.float32)
-    quad_land[...] = jnp.zeros(quad_land.shape, jnp.float32)
     barrier = pltpu.get_barrier_semaphore()
-    extra = (-12, -6, -4, -2, 2, 4, 6, 12)
+    extra = (-6, -4, -2, 2, 4, 6)
 
     def inside(delta):
         return jnp.logical_and(dev + delta >= 0, dev + delta < count)
@@ -261,10 +255,7 @@
             device_id_type=mesh_id,
         )
 
-    partners = (
-        (pair_ref, pair_land, pair_send, pair_recv, 2),
-        (quad_ref, quad_land, quad_send, quad_recv, 4),
-    )
+    partners = ((pair_ref, pair_land, pair_send, pair_recv, 2),)
     for src, land, send_sem, recv_sem, stride in partners:
         for slot, offset in enumerate(OFFSETS):
 
@@ -298,10 +289,9 @@
 
     top_out[...] = top_land[...]
     pair_out[...] = pair_land[...]
-    quad_out[...] = quad_land[...]
-
-
-def exchange(top_block, coef_pair, coef_quad):
+
+
+def exchange(top_block, coef_pair):
     clusters = lax.axis_size("cl")
     rows, cols = top_block.shape
     stack = (len(OFFSETS),) + coef_pair.shape
@@ -311,23 +301,19 @@
         out_shape=(
             jax.ShapeDtypeStruct((clusters, rows, cols), jnp.float32),
             jax.ShapeDtypeStruct(stack, jnp.float32),
-            jax.ShapeDtypeStruct(stack, jnp.float32),
         ),
-        in_specs=[vmem] * 3,
-        out_specs=(vmem, vmem, vmem),
+        in_specs=[vmem] * 2,
+        out_specs=(vmem, vmem),
         scratch_shapes=[
             pltpu.VMEM((clusters, rows, cols), jnp.float32),
-            pltpu.VMEM(stack, jnp.float32),
             pltpu.VMEM(stack, jnp.float32),
             pltpu.SemaphoreType.DMA((clusters,)),
             pltpu.SemaphoreType.DMA((clusters,)),
             pltpu.SemaphoreType.DMA((len(OFFSETS),)),
             pltpu.SemaphoreType.DMA((len(OFFSETS),)),
-            pltpu.SemaphoreType.DMA((len(OFFSETS),)),
-            pltpu.SemaphoreType.DMA((len(OFFSETS),)),
         ],
         compiler_params=pltpu.CompilerParams(collective_id=0, has_side_effects=True),
-    )(top_block, coef_pair, coef_quad)
+    )(top_block, coef_pair)
 
 
 def per_device(
@@ -373,7 +359,8 @@
     top_member = device % 8
     share = width // 8
     top_cols_own = lax.dynamic_slice_in_dim(coef_top.T, top_member * share, share, 0)
-    top_t, pair_stack, quad_stack = exchange(top_cols_own, coef_pair, coef_quad)
+    quad_stack, _ = partner_stack(coef_quad, 4)
+    top_t, pair_stack = exchange(top_cols_own, coef_pair)
     all_top = jnp.swapaxes(top_t, 1, 2)
     top_coords = lax.dynamic_index_in_dim(skel_top, top_cluster, 0, keepdims=False)
     top_entries = lax.dynamic_index_in_dim(far_top, top_cluster, 0, keepdims=False)

time: 263 us -> 285 us (1.084)
  starting transfers between devices: 95.6 us -> 128 us
  Pallas kernels: 79.1 us -> 50.4 us
  waiting for transfers between devices: 14.6 us -> 33.1 us
    ppermute x16 -> x24, starting transfers between devices: 83.6 us -> 115 us  [from_behind(): return lax.ppermute(block, axis, route)]
    pallas_call x1, Pallas kernels: 79.1 us -> 50.4 us  [exchange(): pl.pallas_call(functools.partial(exchange_kernel, clusters), out_shape=(j...]
    ppermute x16 -> x24, waiting for transfers between devices: 6.83 us -> 20.6 us  [from_behind(): return lax.ppermute(block, axis, route)]
    ppermute x6, waiting for transfers between devices: 7.76 us -> 12.6 us  [from_partner(): return lax.ppermute(value, axis, pairs)]
  transfers between devices with their start and end apart: 22 -> 30, of which waited for: 4 -> 7; matrix products, arithmetic and copies ran while one was open for 17% -> 16% of each run, Pallas kernels for 30% -> 18%
where the time goes in v2:
time: 285 us; the launch traced here: 284 us
  starting transfers between devices  128 us (45%)
  Pallas kernels  50.4 us (18%)
  matrix products  37.4 us (13%)
  waiting for transfers between devices  33.1 us (12%)
  blocking collectives  14.6 us (5%)
  local copies, waits for them, and re-layouts  13.9 us (5%)
  other arithmetic  4.69 us (2%)
    ppermute x24, starting transfers between devices, from_behind(): return lax.ppermute(block, axis, route)  115 us
    pallas_call x1, Pallas kernels, exchange(): pl.pallas_call(functools.partial(exchange_kernel, clusters), out_shape=(j...  50.4 us
    dot_general x17, matrix products, contribution(): jnp.dot(kernel_block(own_points, coords), block[:leaf_points], precision=...  30.6 us
    ppermute x24, waiting for transfers between devices, from_behind(): return lax.ppermute(block, axis, route)  20.6 us
    all_gather x1, blocking collectives, per_device(): local_top = lax.all_gather(top_cols, MEMBERS, axis=1, tiled=True)  14.6 us
    ppermute x6, starting transfers between devices, from_partner(): return lax.ppermute(value, axis, pairs)  13.4 us
    ppermute x6, waiting for transfers between devices, from_partner(): return lax.ppermute(value, axis, pairs)  12.6 us
  transfers between devices with their start and end apart: 30, of which 7 were waited for; matrix products, arithmetic and copies ran while one was open for 16% of the time, Pallas kernels for 18%

profile of v2, /device:TPU:24, one launch (start us, length us, event | category | flops | bytes accessed | tf_op | source)
XLA Modules:
  0.0 283.9 jit_solution(7593163559791210570)
XLA Ops:
  1.7 1.6 fusion.407
  3.3 1.0 pad_maximum_fusion
  4.3 1.9 collective-permute-start
  6.2 13.2 %collective-permute-start.1 = (f32[655,128]{1,0:T(8,128)S(1)}, f32[655,128]{1,0:T(8,128)S(1)}, u32[]{:S(2)}, u32[]{:S(2)}) collective-permute-start(f32[655,128]{1,0:T(8,128)S(1)} %pad_maximum_fusion), channel_id=1, source_target_pairs={{1,0},{2,1},{3,2},{4,3},{5,4},{6,5},{7,6},{8,7},{9,8},{10,9},{11,1... | collective-permute-start | bytes 1006088 | tf_op jit(solution)/shard_map/ppermute | solution.py:32
  19.5 1.9 collective-permute-start.16
  21.4 2.4 collective-permute-start.17
  25.5 1.6 gather_fusion.1
  28.7 1.0 compare_reduce_fusion.8
  29.7 1.6 convolution_select_fusion.16
  32.1 1.9 collective-permute-start.18
  34.4 3.6 %collective-permute-done.18 = f32[64,128]{1,0:T(8,128)S(1)} collective-permute-done((f32[64,128]{1,0:T(8,128)S(1)}, f32[64,128]{1,0:T(8,128)S(1)}, u32[]{:S(2)}, u32[]{:S(2)}) %collective-permute-start.18) | collective-permute-done | bytes 32800 | tf_op jit(solution)/shard_map/ppermute | solution.py:26
  38.3 1.9 collective-permute-start.19
  40.2 1.4 collective-permute-done.19
  42.3 1.9 collective-permute-start.20
  44.2 2.0 collective-permute-start.2
  46.3 7.7 %collective-permute-start.3 = (f32[655,128]{1,0:T(8,128)S(1)}, f32[655,128]{1,0:T(8,128)}, u32[]{:S(2)}, u32[]{:S(2)}) collective-permute-start(f32[655,128]{1,0:T(8,128)S(1)} %collective-permute-done.1), channel_id=1, source_target_pairs={{1,0},{2,1},{3,2},{4,3},{5,4},{6,5},{7,6},{8,7},{9,8},{10,9},{11,1... | collective-permute-start | bytes 1006088 | tf_op jit(solution)/shard_map/ppermute | solution.py:32
  54.0 1.6 fusion.17
  55.7 4.3 %collective-permute-start.22 = (f32[128,128]{1,0:T(8,128)S(1)}, f32[128,128]{1,0:T(8,128)S(1)}, u32[]{:S(2)}, u32[]{:S(2)}) collective-permute-start(f32[128,128]{1,0:T(8,128)S(1)} %get-tuple-element.91), channel_id=1, source_target_pairs={{0,16},{1,17},{2,18},{3,19},{4,20},{5,21},{6,22},{7,23},{8,24},{9,... | collective-permute-start | bytes 196616 | tf_op jit(solution)/shard_map/ppermute | solution.py:32
  60.0 2.3 fusion.16
  62.4 3.8 %collective-permute-start.23 = (f32[128,128]{1,0:T(8,128)S(1)}, f32[128,128]{1,0:T(8,128)S(1)}, u32[]{:S(2)}, u32[]{:S(2)}) collective-permute-start(f32[128,128]{1,0:T(8,128)S(1)} %get-tuple-element.91), channel_id=1, source_target_pairs={{0,12},{1,13},{2,14},{3,15},{4,16},{5,17},{6,18},{7,19},{8,20},{9,... | collective-permute-start | bytes 196616 | tf_op jit(solution)/shard_map/ppermute | solution.py:32
  66.2 3.8 %collective-permute-start.24 = (f32[128,128]{1,0:T(8,128)S(1)}, f32[128,128]{1,0:T(8,128)S(1)}, u32[]{:S(2)}, u32[]{:S(2)}) collective-permute-start(f32[128,128]{1,0:T(8,128)S(1)} %get-tuple-element.91), channel_id=1, source_target_pairs={{0,8},{1,9},{2,10},{3,11},{4,12},{5,13},{6,14},{7,15},{8,16},{9,17... | collective-permute-start | bytes 196616 | tf_op jit(solution)/shard_map/ppermute | solution.py:32
  70.0 4.0 %collective-permute-done.22 = f32[128,128]{1,0:T(8,128)S(1)} collective-permute-done((f32[128,128]{1,0:T(8,128)S(1)}, f32[128,128]{1,0:T(8,128)S(1)}, u32[]{:S(2)}, u32[]{:S(2)}) %collective-permute-start.22) | collective-permute-done | bytes 65568 | tf_op jit(solution)/shard_map/ppermute | solution.py:32
  74.0 1.9 collective-permute-start.25
  75.9 8.7 %collective-permute-done.23 = f32[128,128]{1,0:T(8,128)S(1)} collective-permute-done((f32[128,128]{1,0:T(8,128)S(1)}, f32[128,128]{1,0:T(8,128)S(1)}, u32[]{:S(2)}, u32[]{:S(2)}) %collective-permute-start.23) | collective-permute-done | bytes 65568 | tf_op jit(solution)/shard_map/ppermute | solution.py:32
  84.6 1.9 collective-permute-start.26
  86.6 1.2 collective-permute-done.24
  87.8 2.5 collective-permute-start.27
  90.3 9.7 %collective-permute-start.28 = (f32[128,128]{1,0:T(8,128)S(1)}, f32[128,128]{1,0:T(8,128)S(1)}, u32[]{:S(2)}, u32[]{:S(2)}) collective-permute-start(f32[128,128]{1,0:T(8,128)S(1)} %get-tuple-element.91), channel_id=1, source_target_pairs={{12,0},{13,1},{14,2},{15,3},{16,4},{17,5},{18,6},{19,7},{20,8},{21... | collective-permute-start | bytes 196616 | tf_op jit(solution)/shard_map/ppermute | solution.py:32
  100.1 7.1 %collective-permute-start.29 = (f32[128,128]{1,0:T(8,128)S(1)}, f32[128,128]{1,0:T(8,128)S(1)}, u32[]{:S(2)}, u32[]{:S(2)}) collective-permute-start(f32[128,128]{1,0:T(8,128)S(1)} %get-tuple-element.91), channel_id=1, source_target_pairs={{16,0},{17,1},{18,2},{19,3},{20,4},{21,5},{22,6},{23,7},{24,8},{25... | collective-permute-start | bytes 196616 | tf_op jit(solution)/shard_map/ppermute | solution.py:32
  107.2 3.3 %collective-permute-start.21 = (f32[128,128]{1,0:T(8,128)S(1)}, f32[128,128]{1,0:T(8,128)S(1)}, u32[]{:S(2)}, u32[]{:S(2)}) collective-permute-start(f32[128,128]{1,0:T(8,128)S(1)} %get-tuple-element.92), channel_id=1, source_target_pairs={{0,4},{1,5},{2,6},{3,7},{4,0},{5,1},{6,2},{7,3},{8,12},{9,13},{10,... | collective-permute-start | bytes 196616 | tf_op jit(solution)/shard_map/ppermute | solution.py:26
  110.5 7.6 %collective-permute-done.21 = f32[128,128]{1,0:T(8,128)S(1)} collective-permute-done((f32[128,128]{1,0:T(8,128)S(1)}, f32[128,128]{1,0:T(8,128)S(1)}, u32[]{:S(2)}, u32[]{:S(2)}) %collective-permute-start.21) | collective-permute-done | bytes 65568 | tf_op jit(solution)/shard_map/ppermute | solution.py:26
  118.9 50.4 %shard_map.145 = (f32[64,16,128]{2,1,0:T(8,128)}, f32[8,128,128]{2,1,0:T(8,128)}) custom-call(f32[16,128]{1,0:T(8,128)} %copy.36.top_ref, f32[128,128]{1,0:T(8,128)} %slice_bitcast_fusion.17.pair_ref), custom_call_target="tpu_custom_call" | custom-call | tf_op jit(solution)/shard_map/pallas_call | solution.py:299
  169.3 1.6 gather_fusion.4
  172.3 14.6 %all_gather.3 = f32[128,128]{0,1:T(8,128)S(1)} all-gather(f32[128,16]{0,1:T(8,128)S(1)} %fusion.206), channel_id=1, replica_groups=mesh['cl'=64,'q'=2,'p'=2,'c'=2] {'q','p','c'}, dimensions={1}, use_global_device_ids=true | all-gather | bytes 73728 | tf_op jit(solution)/shard_map/all_gather | solution.py:374
  190.1 3.7 %collective-permute-start.5 = (f32[655,128]{1,0:T(8,128)}, f32[655,128]{1,0:T(8,128)S(1)}, u32[]{:S(2)}, u32[]{:S(2)}) collective-permute-start(f32[655,128]{1,0:T(8,128)} %collective-permute-done.3), channel_id=1, source_target_pairs={{1,0},{2,1},{3,2},{4,3},{5,4},{6,5},{7,6},{8,7},{9,8},{10,9},{11,1... | collective-permute-start | bytes 1006088 | tf_op jit(solution)/shard_map/ppermute | solution.py:32
  194.6 2.1 collective-permute-start.4
  196.7 2.6 convolution_select_fusion.12
  200.0 2.5 fusion.15
  202.6 7.9 %collective-permute-start.7 = (f32[655,128]{1,0:T(8,128)S(1)}, f32[655,128]{1,0:T(8,128)S(1)}, u32[]{:S(2)}, u32[]{:S(2)}) collective-permute-start(f32[655,128]{1,0:T(8,128)S(1)} %collective-permute-done.5), channel_id=1, source_target_pairs={{1,0},{2,1},{3,2},{4,3},{5,4},{6,5},{7,6},{8,7},{9,8},{10,9},{11,1... | collective-permute-start | bytes 1006088 | tf_op jit(solution)/shard_map/ppermute | solution.py:32
  210.5 1.9 collective-permute-start.6
  212.4 1.5 convolution_select_fusion.10
  213.9 1.5 fusion.13
  215.5 7.9 %collective-permute-start.9 = (f32[655,128]{1,0:T(8,128)S(1)}, f32[655,128]{1,0:T(8,128)S(1)}, u32[]{:S(2)}, u32[]{:S(2)}) collective-permute-start(f32[655,128]{1,0:T(8,128)S(1)} %collective-permute-done.7), channel_id=1, source_target_pairs={{1,0},{2,1},{3,2},{4,3},{5,4},{6,5},{7,6},{8,7},{9,8},{10,9},{11,1... | collective-permute-start | bytes 1006088 | tf_op jit(solution)/shard_map/ppermute | solution.py:32
  223.4 1.9 collective-permute-start.8
  225.3 1.6 convolution_select_fusion.8
  226.9 1.6 fusion.11
  228.5 7.9 %collective-permute-start.11 = (f32[655,128]{1,0:T(8,128)S(1)}, f32[655,128]{1,0:T(8,128)S(1)}, u32[]{:S(2)}, u32[]{:S(2)}) collective-permute-start(f32[655,128]{1,0:T(8,128)S(1)} %collective-permute-done.9), channel_id=1, source_target_pairs={{1,0},{2,1},{3,2},{4,3},{5,4},{6,5},{7,6},{8,7},{9,8},{10,9},{11,1... | collective-permute-start | bytes 1006088 | tf_op jit(solution)/shard_map/ppermute | solution.py:32
  236.3 1.9 collective-permute-start.10
  238.3 1.5 convolution_select_fusion.6
  239.8 1.5 fusion.9
  241.3 7.9 %collective-permute-start.13 = (f32[655,128]{1,0:T(8,128)S(1)}, f32[655,128]{1,0:T(8,128)S(1)}, u32[]{:S(2)}, u32[]{:S(2)}) collective-permute-start(f32[655,128]{1,0:T(8,128)S(1)} %collective-permute-done.11), channel_id=1, source_target_pairs={{1,0},{2,1},{3,2},{4,3},{5,4},{6,5},{7,6},{8,7},{9,8},{10,9},{11,1... | collective-permute-start | bytes 1006088 | tf_op jit(solution)/shard_map/ppermute | solution.py:32
  249.2 1.9 collective-permute-start.12
  251.1 1.5 convolution_select_fusion.4
  252.7 1.6 fusion.7
  254.3 7.9 %collective-permute-start.15 = (f32[655,128]{1,0:T(8,128)S(1)}, f32[655,128]{1,0:T(8,128)S(1)}, u32[]{:S(2)}, u32[]{:S(2)}) collective-permute-start(f32[655,128]{1,0:T(8,128)S(1)} %collective-permute-done.13), channel_id=1, source_target_pairs={{1,0},{2,1},{3,2},{4,3},{5,4},{6,5},{7,6},{8,7},{9,8},{10,9},{11,1... | collective-permute-start | bytes 1006088 | tf_op jit(solution)/shard_map/ppermute | solution.py:32
  262.2 2.1 collective-permute-start.14
  264.3 1.6 convolution_select_fusion.2
  266.0 2.3 fusion.5
  268.3 6.6 %collective-permute-done.14 = f32[655,128]{1,0:T(8,128)S(1)} collective-permute-done((f32[655,128]{1,0:T(8,128)S(1)}, f32[655,128]{1,0:T(8,128)S(1)}, u32[]{:S(2)}, u32[]{:S(2)}) %collective-permute-start.14) | collective-permute-done | bytes 335392 | tf_op jit(solution)/shard_map/ppermute | solution.py:32
  275.0 0.9 fusion.450
  276.0 0.9 fusion.447
  278.6 0.9 fusion.242
  280.1 1.5 convolution_select_fusion
  281.6 2.2 fusion.3
  (170 shorter events, 15.9 us)
Async XLA Ops:
  0.0 1.7 copy-start
  0.0 24.2 %copy-start.16 = (f32[1,3,128]{2,0,1:T(1,128)S(1)}, f32[1,3,128]{2,0,1:T(1,128)}, u32[]{:S(2)}) copy-start(f32[1,3,128]{2,0,1:T(1,128)} %param.23) | copy-start | bytes 4612
  0.0 25.1 %copy-start.7 = (f32[1,3,512]{2,0,1:T(1,128)S(1)}, f32[1,3,512]{2,0,1:T(1,128)}, u32[]{:S(2)}) copy-start(f32[1,3,512]{2,0,1:T(1,128)} %param.18) | copy-start | bytes 18436
  0.0 19.4 %copy-start.5 = (f32[64,128]{1,0:T(8,128)S(1)}, f32[64,128]{1,0:T(8,128)}, u32[]{:S(2)}) copy-start(f32[64,128]{1,0:T(8,128)} %param.21) | copy-start | bytes 98308
  0.0 21.4 %copy-start.13 = (f32[32,128]{1,0:T(8,128)S(1)}, f32[32,128]{1,0:T(8,128)}, u32[]{:S(2)}) copy-start(f32[32,128]{1,0:T(8,128)} %param.22) | copy-start | bytes 49156
  0.0 23.8 %copy-start.17 = (s32[1,8]{1,0:T(1,128)S(1)}, s32[1,8]{1,0:T(1,128)}, u32[]{:S(2)}) copy-start(s32[1,8]{1,0:T(1,128)} %param.28) | copy-start | bytes 100
  0.0 24.2 %copy-start.15 = (s32[256,8]{0,1:T(8,128)S(1)}, s32[256,8]{0,1:T(8,128)}, u32[]{:S(2)}) copy-start(s32[256,8]{0,1:T(8,128)} %param.29) | copy-start | bytes 24580
  0.1 24.4 %copy-start.14 = (s32[64,8]{0,1:T(8,128)S(1)}, s32[64,8]{0,1:T(8,128)}, u32[]{:S(2)}) copy-start(s32[64,8]{0,1:T(8,128)} %param.31) | copy-start | bytes 6148
  0.1 24.6 %copy-start.12 = (s32[128,8]{0,1:T(8,128)S(1)}, s32[128,8]{0,1:T(8,128)}, u32[]{:S(2)}) copy-start(s32[128,8]{0,1:T(8,128)} %param.30) | copy-start | bytes 12292
  0.1 25.1 %copy-start.3 = (f32[1,128,128]{2,1,0:T(8,128)S(1)}, f32[1,128,128]{2,1,0:T(8,128)}, u32[]{:S(2)}) copy-start(f32[1,128,128]{2,1,0:T(8,128)} %param.20) | copy-start | bytes 196612
  0.1 27.1 %copy-start.6 = (f32[128,3,128]{2,0,1:T(8,128)S(1)}, f32[128,3,128]{2,0,1:T(8,128)}, u32[]{:S(2)}) copy-start(f32[128,3,128]{2,0,1:T(8,128)} %param.25) | copy-start | bytes 589828
  0.1 27.8 %copy-start.4 = (f32[64,3,128]{2,0,1:T(8,128)S(1)}, f32[64,3,128]{2,0,1:T(8,128)}, u32[]{:S(2)}) copy-start(f32[64,3,128]{2,0,1:T(8,128)} %param.26) | copy-start | bytes 294916
  1.7 27.0 %copy-start.18 = (s32[1,16]{1,0:T(1,128)S(1)}, s32[1,16]{1,0:T(1,128)}, u32[]{:S(2)}) copy-start(s32[1,16]{1,0:T(1,128)} %param.27) | copy-start | bytes 196
  1.7 28.0 %copy-start.1 = (f32[1,512,128]{2,1,0:T(8,128)S(1)}, f32[1,512,128]{2,1,0:T(8,128)}, u32[]{:S(2)}) copy-start(f32[1,512,128]{2,1,0:T(8,128)} %param.17) | copy-start | bytes 786436
  4.3 39.9 %collective-permute-start = (f32[655,128]{1,0:T(8,128)S(1)}, f32[655,128]{1,0:T(8,128)S(1)}, u32[]{:S(2)}, u32[]{:S(2)}) collective-permute-start(f32[655,128]{1,0:T(8,128)S(1)} %pad_maximum_fusion), channel_id=1, source_target_pairs={{0,1},{1,2},{2,3},{3,4},{4,5},{5,6},{6,7},{7,8},{8,9},{9,10},{10,1... | collective-permute-start | bytes 1006088 | tf_op jit(solution)/shard_map/ppermute | solution.py:32
  6.2 40.0 %collective-permute-start.1 = (f32[655,128]{1,0:T(8,128)S(1)}, f32[655,128]{1,0:T(8,128)S(1)}, u32[]{:S(2)}, u32[]{:S(2)}) collective-permute-start(f32[655,128]{1,0:T(8,128)S(1)} %pad_maximum_fusion), channel_id=1, source_target_pairs={{1,0},{2,1},{3,2},{4,3},{5,4},{6,5},{7,6},{8,7},{9,8},{10,9},{11,1... | collective-permute-start | bytes 1006088 | tf_op jit(solution)/shard_map/ppermute | solution.py:32
  19.5 14.6 %collective-permute-start.16 = (f32[64,128]{1,0:T(8,128)S(1)}, f32[64,128]{1,0:T(8,128)S(1)}, u32[]{:S(2)}, u32[]{:S(2)}) collective-permute-start(f32[64,128]{1,0:T(8,128)S(1)} %copy-done.5), channel_id=1, source_target_pairs={{0,1},{1,0},{2,3},{3,2},{4,5},{5,4},{6,7},{7,6},{8,9},{9,8},{10,11... | collective-permute-start | bytes 98312 | tf_op jit(solution)/shard_map/ppermute | solution.py:26
  21.4 10.7 %collective-permute-start.17 = (f32[32,128]{1,0:T(8,128)S(1)}, f32[32,128]{1,0:T(8,128)S(1)}, u32[]{:S(2)}, u32[]{:S(2)}) collective-permute-start(f32[32,128]{1,0:T(8,128)S(1)} %copy-done.13), channel_id=1, source_target_pairs={{0,1},{1,0},{2,3},{3,2},{4,5},{5,4},{6,7},{7,6},{8,9},{9,8},{10,11... | collective-permute-start | bytes 49160 | tf_op jit(solution)/shard_map/ppermute | solution.py:26
  32.1 5.8 %collective-permute-start.18 = (f32[64,128]{1,0:T(8,128)S(1)}, f32[64,128]{1,0:T(8,128)S(1)}, u32[]{:S(2)}, u32[]{:S(2)}) collective-permute-start(f32[64,128]{1,0:T(8,128)S(1)} %maximum_select_fusion.6), channel_id=1, source_target_pairs={{0,2},{1,3},{2,0},{3,1},{4,6},{5,7},{6,4},{7,5},{8,10},{9,11},{10,... | collective-permute-start | bytes 98312 | tf_op jit(solution)/shard_map/ppermute | solution.py:26
  38.3 3.3 %collective-permute-start.19 = (f32[3,128,128]{2,1,0:T(8,128)S(1)}, f32[3,128,128]{2,1,0:T(8,128)S(1)}, u32[]{:S(2)}, u32[]{:S(2)}) collective-permute-start(f32[3,128,128]{2,1,0:T(8,128)S(1)} %pad_maximum_fusion.1), channel_id=1, source_target_pairs={{0,1},{1,0},{2,3},{3,2},{4,5},{5,4},{6,7},{7,6},{8,9},{9,8},{10,11... | collective-permute-start | bytes 589832 | tf_op jit(solution)/shard_map/ppermute | solution.py:26
  42.3 13.4 %collective-permute-start.20 = (f32[2,128,128]{2,1,0:T(8,128)S(1)}, f32[2,128,128]{2,1,0:T(8,128)S(1)}, u32[]{:S(2)}, u32[]{:S(2)}) collective-permute-start(f32[2,128,128]{2,1,0:T(8,128)S(1)} %slice.748), channel_id=1, source_target_pairs={{0,2},{1,3},{2,0},{3,1},{4,6},{5,7},{6,4},{7,5},{8,10},{9,11},{10,... | collective-permute-start | bytes 393224 | tf_op jit(solution)/shard_map/ppermute | solution.py:26
  44.2 150.4 %collective-permute-start.2 = (f32[655,128]{1,0:T(8,128)S(1)}, f32[655,128]{1,0:T(8,128)}, u32[]{:S(2)}, u32[]{:S(2)}) collective-permute-start(f32[655,128]{1,0:T(8,128)S(1)} %collective-permute-done), channel_id=1, source_target_pairs={{0,1},{1,2},{2,3},{3,4},{4,5},{5,6},{6,7},{7,8},{8,9},{9,10},{10,1... | collective-permute-start | bytes 1006088 | tf_op jit(solution)/shard_map/ppermute | solution.py:32
  46.3 143.8 %collective-permute-start.3 = (f32[655,128]{1,0:T(8,128)S(1)}, f32[655,128]{1,0:T(8,128)}, u32[]{:S(2)}, u32[]{:S(2)}) collective-permute-start(f32[655,128]{1,0:T(8,128)S(1)} %collective-permute-done.1), channel_id=1, source_target_pairs={{1,0},{2,1},{3,2},{4,3},{5,4},{6,5},{7,6},{8,7},{9,8},{10,9},{11,1... | collective-permute-start | bytes 1006088 | tf_op jit(solution)/shard_map/ppermute | solution.py:32
  55.7 18.3 %collective-permute-start.22 = (f32[128,128]{1,0:T(8,128)S(1)}, f32[128,128]{1,0:T(8,128)S(1)}, u32[]{:S(2)}, u32[]{:S(2)}) collective-permute-start(f32[128,128]{1,0:T(8,128)S(1)} %get-tuple-element.91), channel_id=1, source_target_pairs={{0,16},{1,17},{2,18},{3,19},{4,20},{5,21},{6,22},{7,23},{8,24},{9,... | collective-permute-start | bytes 196616 | tf_op jit(solution)/shard_map/ppermute | solution.py:32
  62.4 22.3 %collective-permute-start.23 = (f32[128,128]{1,0:T(8,128)S(1)}, f32[128,128]{1,0:T(8,128)S(1)}, u32[]{:S(2)}, u32[]{:S(2)}) collective-permute-start(f32[128,128]{1,0:T(8,128)S(1)} %get-tuple-element.91), channel_id=1, source_target_pairs={{0,12},{1,13},{2,14},{3,15},{4,16},{5,17},{6,18},{7,19},{8,20},{9,... | collective-permute-start | bytes 196616 | tf_op jit(solution)/shard_map/ppermute | solution.py:32
  66.2 21.6 %collective-permute-start.24 = (f32[128,128]{1,0:T(8,128)S(1)}, f32[128,128]{1,0:T(8,128)S(1)}, u32[]{:S(2)}, u32[]{:S(2)}) collective-permute-start(f32[128,128]{1,0:T(8,128)S(1)} %get-tuple-element.91), channel_id=1, source_target_pairs={{0,8},{1,9},{2,10},{3,11},{4,12},{5,13},{6,14},{7,15},{8,16},{9,17... | collective-permute-start | bytes 196616 | tf_op jit(solution)/shard_map/ppermute | solution.py:32
  74.0 16.3 %collective-permute-start.25 = (f32[128,128]{1,0:T(8,128)S(1)}, f32[128,128]{1,0:T(8,128)S(1)}, u32[]{:S(2)}, u32[]{:S(2)}) collective-permute-start(f32[128,128]{1,0:T(8,128)S(1)} %get-tuple-element.91), channel_id=1, source_target_pairs={{0,4},{1,5},{2,6},{3,7},{4,8},{5,9},{6,10},{7,11},{8,12},{9,13},{1... | collective-permute-start | bytes 196616 | tf_op jit(solution)/shard_map/ppermute | solution.py:32
  84.6 15.4 %collective-permute-start.26 = (f32[128,128]{1,0:T(8,128)S(1)}, f32[128,128]{1,0:T(8,128)S(1)}, u32[]{:S(2)}, u32[]{:S(2)}) collective-permute-start(f32[128,128]{1,0:T(8,128)S(1)} %get-tuple-element.91), channel_id=1, source_target_pairs={{4,0},{5,1},{6,2},{7,3},{8,4},{9,5},{10,6},{11,7},{12,8},{13,9},{1... | collective-permute-start | bytes 196616 | tf_op jit(solution)/shard_map/ppermute | solution.py:32
  87.8 19.4 %collective-permute-start.27 = (f32[128,128]{1,0:T(8,128)S(1)}, f32[128,128]{1,0:T(8,128)S(1)}, u32[]{:S(2)}, u32[]{:S(2)}) collective-permute-start(f32[128,128]{1,0:T(8,128)S(1)} %get-tuple-element.91), channel_id=1, source_target_pairs={{8,0},{9,1},{10,2},{11,3},{12,4},{13,5},{14,6},{15,7},{16,8},{17,9... | collective-permute-start | bytes 196616 | tf_op jit(solution)/shard_map/ppermute | solution.py:32
  90.3 80.6 %collective-permute-start.28 = (f32[128,128]{1,0:T(8,128)S(1)}, f32[128,128]{1,0:T(8,128)S(1)}, u32[]{:S(2)}, u32[]{:S(2)}) collective-permute-start(f32[128,128]{1,0:T(8,128)S(1)} %get-tuple-element.91), channel_id=1, source_target_pairs={{12,0},{13,1},{14,2},{15,3},{16,4},{17,5},{18,6},{19,7},{20,8},{21... | collective-permute-start | bytes 196616 | tf_op jit(solution)/shard_map/ppermute | solution.py:32
  100.1 86.9 %collective-permute-start.29 = (f32[128,128]{1,0:T(8,128)S(1)}, f32[128,128]{1,0:T(8,128)S(1)}, u32[]{:S(2)}, u32[]{:S(2)}) collective-permute-start(f32[128,128]{1,0:T(8,128)S(1)} %get-tuple-element.91), channel_id=1, source_target_pairs={{16,0},{17,1},{18,2},{19,3},{20,4},{21,5},{22,6},{23,7},{24,8},{25... | collective-permute-start | bytes 196616 | tf_op jit(solution)/shard_map/ppermute | solution.py:32
  107.2 10.9 %collective-permute-start.21 = (f32[128,128]{1,0:T(8,128)S(1)}, f32[128,128]{1,0:T(8,128)S(1)}, u32[]{:S(2)}, u32[]{:S(2)}) collective-permute-start(f32[128,128]{1,0:T(8,128)S(1)} %get-tuple-element.92), channel_id=1, source_target_pairs={{0,4},{1,5},{2,6},{3,7},{4,0},{5,1},{6,2},{7,3},{8,12},{9,13},{10,... | collective-permute-start | bytes 196616 | tf_op jit(solution)/shard_map/ppermute | solution.py:26
  169.2 2.5 copy-start.2
  190.1 12.5 %collective-permute-start.5 = (f32[655,128]{1,0:T(8,128)}, f32[655,128]{1,0:T(8,128)S(1)}, u32[]{:S(2)}, u32[]{:S(2)}) collective-permute-start(f32[655,128]{1,0:T(8,128)} %collective-permute-done.3), channel_id=1, source_target_pairs={{1,0},{2,1},{3,2},{4,3},{5,4},{6,5},{7,6},{8,7},{9,8},{10,9},{11,1... | collective-permute-start | bytes 1006088 | tf_op jit(solution)/shard_map/ppermute | solution.py:32
  194.6 15.9 %collective-permute-start.4 = (f32[655,128]{1,0:T(8,128)}, f32[655,128]{1,0:T(8,128)S(1)}, u32[]{:S(2)}, u32[]{:S(2)}) collective-permute-start(f32[655,128]{1,0:T(8,128)} %collective-permute-done.2), channel_id=1, source_target_pairs={{0,1},{1,2},{2,3},{3,4},{4,5},{5,6},{6,7},{7,8},{8,9},{9,10},{10,1... | collective-permute-start | bytes 1006088 | tf_op jit(solution)/shard_map/ppermute | solution.py:32
  196.7 3.3 %copy-start.20 = (f32[512,128]{1,0:T(8,128)S(1)}, f32[512,128]{1,0:T(8,128)}, u32[]{:S(2)}) copy-start(f32[512,128]{1,0:T(8,128)} %fusion.16) | copy-start | bytes 786436
  202.6 12.9 %collective-permute-start.7 = (f32[655,128]{1,0:T(8,128)S(1)}, f32[655,128]{1,0:T(8,128)S(1)}, u32[]{:S(2)}, u32[]{:S(2)}) collective-permute-start(f32[655,128]{1,0:T(8,128)S(1)} %collective-permute-done.5), channel_id=1, source_target_pairs={{1,0},{2,1},{3,2},{4,3},{5,4},{6,5},{7,6},{8,7},{9,8},{10,9},{11,1... | collective-permute-start | bytes 1006088 | tf_op jit(solution)/shard_map/ppermute | solution.py:32
  210.5 12.9 %collective-permute-start.6 = (f32[655,128]{1,0:T(8,128)S(1)}, f32[655,128]{1,0:T(8,128)S(1)}, u32[]{:S(2)}, u32[]{:S(2)}) collective-permute-start(f32[655,128]{1,0:T(8,128)S(1)} %collective-permute-done.4), channel_id=1, source_target_pairs={{0,1},{1,2},{2,3},{3,4},{4,5},{5,6},{6,7},{7,8},{8,9},{9,10},{10,1... | collective-permute-start | bytes 1006088 | tf_op jit(solution)/shard_map/ppermute | solution.py:32
  215.5 13.0 %collective-permute-start.9 = (f32[655,128]{1,0:T(8,128)S(1)}, f32[655,128]{1,0:T(8,128)S(1)}, u32[]{:S(2)}, u32[]{:S(2)}) collective-permute-start(f32[655,128]{1,0:T(8,128)S(1)} %collective-permute-done.7), channel_id=1, source_target_pairs={{1,0},{2,1},{3,2},{4,3},{5,4},{6,5},{7,6},{8,7},{9,8},{10,9},{11,1... | collective-permute-start | bytes 1006088 | tf_op jit(solution)/shard_map/ppermute | solution.py:32
  223.4 13.0 %collective-permute-start.8 = (f32[655,128]{1,0:T(8,128)S(1)}, f32[655,128]{1,0:T(8,128)S(1)}, u32[]{:S(2)}, u32[]{:S(2)}) collective-permute-start(f32[655,128]{1,0:T(8,128)S(1)} %collective-permute-done.6), channel_id=1, source_target_pairs={{0,1},{1,2},{2,3},{3,4},{4,5},{5,6},{6,7},{7,8},{8,9},{9,10},{10,1... | collective-permute-start | bytes 1006088 | tf_op jit(solution)/shard_map/ppermute | solution.py:32
  228.5 12.8 %collective-permute-start.11 = (f32[655,128]{1,0:T(8,128)S(1)}, f32[655,128]{1,0:T(8,128)S(1)}, u32[]{:S(2)}, u32[]{:S(2)}) collective-permute-start(f32[655,128]{1,0:T(8,128)S(1)} %collective-permute-done.9), channel_id=1, source_target_pairs={{1,0},{2,1},{3,2},{4,3},{5,4},{6,5},{7,6},{8,7},{9,8},{10,9},{11,1... | collective-permute-start | bytes 1006088 | tf_op jit(solution)/shard_map/ppermute | solution.py:32
  236.3 12.8 %collective-permute-start.10 = (f32[655,128]{1,0:T(8,128)S(1)}, f32[655,128]{1,0:T(8,128)S(1)}, u32[]{:S(2)}, u32[]{:S(2)}) collective-permute-start(f32[655,128]{1,0:T(8,128)S(1)} %collective-permute-done.8), channel_id=1, source_target_pairs={{0,1},{1,2},{2,3},{3,4},{4,5},{5,6},{6,7},{7,8},{8,9},{9,10},{10,1... | collective-permute-start | bytes 1006088 | tf_op jit(solution)/shard_map/ppermute | solution.py:32
  241.3 13.0 %collective-permute-start.13 = (f32[655,128]{1,0:T(8,128)S(1)}, f32[655,128]{1,0:T(8,128)S(1)}, u32[]{:S(2)}, u32[]{:S(2)}) collective-permute-start(f32[655,128]{1,0:T(8,128)S(1)} %collective-permute-done.11), channel_id=1, source_target_pairs={{1,0},{2,1},{3,2},{4,3},{5,4},{6,5},{7,6},{8,7},{9,8},{10,9},{11,1... | collective-permute-start | bytes 1006088 | tf_op jit(solution)/shard_map/ppermute | solution.py:32
  249.2 13.0 %collective-permute-start.12 = (f32[655,128]{1,0:T(8,128)S(1)}, f32[655,128]{1,0:T(8,128)S(1)}, u32[]{:S(2)}, u32[]{:S(2)}) collective-permute-start(f32[655,128]{1,0:T(8,128)S(1)} %collective-permute-done.10), channel_id=1, source_target_pairs={{0,1},{1,2},{2,3},{3,4},{4,5},{5,6},{6,7},{7,8},{8,9},{9,10},{10,1... | collective-permute-start | bytes 1006088 | tf_op jit(solution)/shard_map/ppermute | solution.py:32
  254.3 22.6 %collective-permute-start.15 = (f32[655,128]{1,0:T(8,128)S(1)}, f32[655,128]{1,0:T(8,128)S(1)}, u32[]{:S(2)}, u32[]{:S(2)}) collective-permute-start(f32[655,128]{1,0:T(8,128)S(1)} %collective-permute-done.13), channel_id=1, source_target_pairs={{1,0},{2,1},{3,2},{4,3},{5,4},{6,5},{7,6},{8,7},{9,8},{10,9},{11,1... | collective-permute-start | bytes 1006088 | tf_op jit(solution)/shard_map/ppermute | solution.py:32
  262.2 12.7 %collective-permute-start.14 = (f32[655,128]{1,0:T(8,128)S(1)}, f32[655,128]{1,0:T(8,128)S(1)}, u32[]{:S(2)}, u32[]{:S(2)}) collective-permute-start(f32[655,128]{1,0:T(8,128)S(1)} %collective-permute-done.12), channel_id=1, source_target_pairs={{0,1},{1,2},{2,3},{3,4},{4,5},{5,6},{6,7},{7,8},{8,9},{9,10},{10,1... | collective-permute-start | bytes 1006088 | tf_op jit(solution)/shard_map/ppermute | solution.py:32
  274.9 2.1 copy-start.10
  276.9 0.7 copy-start.8
  278.5 1.5 copy-start.9
  278.5 1.5 copy-start.11
  280.1 1.6 copy-start.19

commit v3 on v1

--- a/solution.py
+++ b/solution.py
@@ -373,6 +373,7 @@
     top_member = device % 8
     share = width // 8
     top_cols_own = lax.dynamic_slice_in_dim(coef_top.T, top_member * share, share, 0)
+    top_cols_own, near_field = lax.optimization_barrier((top_cols_own, near_field))
     top_t, pair_stack, quad_stack = exchange(top_cols_own, coef_pair, coef_quad)
     all_top = jnp.swapaxes(top_t, 1, 2)
     top_coords = lax.dynamic_index_in_dim(skel_top, top_cluster, 0, keepdims=False)

time: 263 us -> 258 us (0.981)
  Pallas kernels: 79.1 us -> 69.7 us
  local copies, waits for them, and re-layouts: 14.4 us -> 22.6 us
  starting transfers between devices: 95.6 us -> 91.2 us
  matrix products: 37.4 us -> 33.6 us
    pallas_call x1, Pallas kernels: 79.1 us -> 69.7 us  [exchange(): pl.pallas_call(functools.partial(exchange_kernel, clusters), out_shape=(j...]
    unnamed x61 -> x75, local copies, waits for them, and re-layouts: 3.68 us -> 12.5 us
    dot_general x17, matrix products: 30.5 us -> 26 us  [contribution(): jnp.dot(kernel_block(own_points, coords), block[:leaf_points], precision=...]
    ppermute x16, starting transfers between devices: 83.6 us -> 79.2 us  [from_behind(): return lax.ppermute(block, axis, route)]
  transfers between devices with their start and end apart: 22 -> 22, of which waited for: 4 -> 4; matrix products, arithmetic and copies ran while one was open for 17% -> 12% of each run, Pallas kernels for 30% -> 0%
where the time goes in v3:
time: 258 us; the launch traced here: 254 us
  starting transfers between devices  91.2 us (35%)
  Pallas kernels  69.7 us (27%)
  matrix products  33.6 us (13%)
  local copies, waits for them, and re-layouts  22.6 us (9%)
  waiting for transfers between devices  16.2 us (6%)
  blocking collectives  14.5 us (6%)
  other arithmetic  4.61 us (2%)
    ppermute x16, starting transfers between devices, from_behind(): return lax.ppermute(block, axis, route)  79.2 us
    pallas_call x1, Pallas kernels, exchange(): pl.pallas_call(functools.partial(exchange_kernel, clusters), out_shape=(j...  69.7 us
    dot_general x17, matrix products, contribution(): jnp.dot(kernel_block(own_points, coords), block[:leaf_points], precision=...  26 us
    all_gather x1, blocking collectives, per_device(): local_top = lax.all_gather(top_cols, MEMBERS, axis=1, tiled=True)  14.5 us
    unnamed x75, local copies, waits for them, and re-layouts  12.5 us
    ppermute x6, starting transfers between devices, from_partner(): return lax.ppermute(value, axis, pairs)  12 us
    ppermute x6, waiting for transfers between devices, from_partner(): return lax.ppermute(value, axis, pairs)  8.61 us
    ppermute x16, waiting for transfers between devices, from_behind(): return lax.ppermute(block, axis, route)  7.58 us
  transfers between devices with their start and end apart: 22, of which 4 were waited for; matrix products, arithmetic and copies ran while one was open for 12% of the time, Pallas kernels for 0%

profile of v3, /device:TPU:24, one launch (start us, length us, event | category | flops | bytes accessed | tf_op | source)
XLA Modules:
  0.0 253.7 jit_solution(5811858681881519077)
XLA Ops:
  1.7 1.6 fusion.407
  3.3 1.0 pad_maximum_fusion
  4.3 1.9 collective-permute-start.6
  6.2 13.2 %collective-permute-start.7 = (f32[655,128]{1,0:T(8,128)S(1)}, f32[655,128]{1,0:T(8,128)S(1)}, u32[]{:S(2)}, u32[]{:S(2)}) collective-permute-start(f32[655,128]{1,0:T(8,128)S(1)} %pad_maximum_fusion), channel_id=1, source_target_pairs={{1,0},{2,1},{3,2},{4,3},{5,4},{6,5},{7,6},{8,7},{9,8},{10,9},{11,1... | collective-permute-start | bytes 1006088 | tf_op jit(solution)/shard_map/ppermute | solution.py:32
  19.5 1.9 collective-permute-start.1
  21.4 2.4 collective-permute-start
  26.9 1.6 gather_fusion.1
  28.6 1.0 compare_reduce_fusion.8
  29.6 1.6 convolution_select_fusion.16
  32.1 1.9 collective-permute-start.2
  34.3 3.6 %collective-permute-done.2 = f32[64,128]{1,0:T(8,128)S(1)} collective-permute-done((f32[64,128]{1,0:T(8,128)S(1)}, f32[64,128]{1,0:T(8,128)S(1)}, u32[]{:S(2)}, u32[]{:S(2)}) %collective-permute-start.2) | collective-permute-done | bytes 32800 | tf_op jit(solution)/shard_map/ppermute | solution.py:26
  38.2 1.9 collective-permute-start.3
  40.1 1.4 collective-permute-done.3
  42.2 1.9 collective-permute-start.4
  44.1 2.0 collective-permute-start.8
  46.2 7.7 %collective-permute-start.9 = (f32[655,128]{1,0:T(8,128)S(1)}, f32[655,128]{1,0:T(8,128)S(1)}, u32[]{:S(2)}, u32[]{:S(2)}) collective-permute-start(f32[655,128]{1,0:T(8,128)S(1)} %collective-permute-done.7), channel_id=1, source_target_pairs={{1,0},{2,1},{3,2},{4,3},{5,4},{6,5},{7,6},{8,7},{9,8},{10,9},{11,1... | collective-permute-start | bytes 1006088 | tf_op jit(solution)/shard_map/ppermute | solution.py:32
  54.0 1.6 fusion.17
  56.2 1.9 collective-permute-start.5
  58.1 1.5 fusion.16
  59.6 3.6 %collective-permute-done.5 = f32[128,128]{1,0:T(8,128)S(1)} collective-permute-done((f32[128,128]{1,0:T(8,128)S(1)}, f32[128,128]{1,0:T(8,128)S(1)}, u32[]{:S(2)}, u32[]{:S(2)}) %collective-permute-start.5) | collective-permute-done | bytes 65568 | tf_op jit(solution)/shard_map/ppermute | solution.py:26
  63.4 3.2 %collective-permute-start.11 = (f32[655,128]{1,0:T(8,128)S(1)}, f32[655,128]{1,0:T(8,128)S(1)}, u32[]{:S(2)}, u32[]{:S(2)}) collective-permute-start(f32[655,128]{1,0:T(8,128)S(1)} %collective-permute-done.9), channel_id=1, source_target_pairs={{1,0},{2,1},{3,2},{4,3},{5,4},{6,5},{7,6},{8,7},{9,8},{10,9},{11,1... | collective-permute-start | bytes 1006088 | tf_op jit(solution)/shard_map/ppermute | solution.py:32
  66.7 1.9 collective-permute-start.10
  68.6 1.5 convolution_select_fusion.12
  70.2 1.5 fusion.15
  71.8 7.9 %collective-permute-start.13 = (f32[655,128]{1,0:T(8,128)S(1)}, f32[655,128]{1,0:T(8,128)S(1)}, u32[]{:S(2)}, u32[]{:S(2)}) collective-permute-start(f32[655,128]{1,0:T(8,128)S(1)} %collective-permute-done.11), channel_id=1, source_target_pairs={{1,0},{2,1},{3,2},{4,3},{5,4},{6,5},{7,6},{8,7},{9,8},{10,9},{11,1... | collective-permute-start | bytes 1006088 | tf_op jit(solution)/shard_map/ppermute | solution.py:32
  79.7 1.9 collective-permute-start.12
  81.6 1.5 convolution_select_fusion.10
  83.1 1.5 fusion.13
  84.6 7.9 %collective-permute-start.15 = (f32[655,128]{1,0:T(8,128)S(1)}, f32[655,128]{1,0:T(8,128)S(1)}, u32[]{:S(2)}, u32[]{:S(2)}) collective-permute-start(f32[655,128]{1,0:T(8,128)S(1)} %collective-permute-done.13), channel_id=1, source_target_pairs={{1,0},{2,1},{3,2},{4,3},{5,4},{6,5},{7,6},{8,7},{9,8},{10,9},{11,1... | collective-permute-start | bytes 1006088 | tf_op jit(solution)/shard_map/ppermute | solution.py:32
  92.5 2.1 collective-permute-start.14
  94.7 1.5 convolution_select_fusion.8
  96.2 1.6 fusion.11
  97.7 7.9 %collective-permute-start.17 = (f32[655,128]{1,0:T(8,128)S(1)}, f32[655,128]{1,0:T(8,128)S(1)}, u32[]{:S(2)}, u32[]{:S(2)}) collective-permute-start(f32[655,128]{1,0:T(8,128)S(1)} %collective-permute-done.15), channel_id=1, source_target_pairs={{1,0},{2,1},{3,2},{4,3},{5,4},{6,5},{7,6},{8,7},{9,8},{10,9},{11,1... | collective-permute-start | bytes 1006088 | tf_op jit(solution)/shard_map/ppermute | solution.py:32
  105.6 1.9 collective-permute-start.16
  107.6 1.5 convolution_select_fusion.6
  109.1 1.6 fusion.9
  110.7 7.9 %collective-permute-start.19 = (f32[655,128]{1,0:T(8,128)S(1)}, f32[655,128]{1,0:T(8,128)S(1)}, u32[]{:S(2)}, u32[]{:S(2)}) collective-permute-start(f32[655,128]{1,0:T(8,128)S(1)} %collective-permute-done.17), channel_id=1, source_target_pairs={{1,0},{2,1},{3,2},{4,3},{5,4},{6,5},{7,6},{8,7},{9,8},{10,9},{11,1... | collective-permute-start | bytes 1006088 | tf_op jit(solution)/shard_map/ppermute | solution.py:32
  118.6 1.9 collective-permute-start.18
  120.6 1.5 convolution_select_fusion.4
  122.1 1.5 fusion.7
  123.6 7.9 %collective-permute-start.21 = (f32[655,128]{1,0:T(8,128)S(1)}, f32[655,128]{1,0:T(8,128)S(1)}, u32[]{:S(2)}, u32[]{:S(2)}) collective-permute-start(f32[655,128]{1,0:T(8,128)S(1)} %collective-permute-done.19), channel_id=1, source_target_pairs={{1,0},{2,1},{3,2},{4,3},{5,4},{6,5},{7,6},{8,7},{9,8},{10,9},{11,1... | collective-permute-start | bytes 1006088 | tf_op jit(solution)/shard_map/ppermute | solution.py:32
  131.5 1.9 collective-permute-start.20
  133.4 1.6 convolution_select_fusion.2
  135.0 1.6 fusion.5
  136.6 7.5 %collective-permute-done.20 = f32[655,128]{1,0:T(8,128)S(1)} collective-permute-done((f32[655,128]{1,0:T(8,128)S(1)}, f32[655,128]{1,0:T(8,128)S(1)}, u32[]{:S(2)}, u32[]{:S(2)}) %collective-permute-start.20) | collective-permute-done | bytes 335392 | tf_op jit(solution)/shard_map/ppermute | solution.py:32
  144.2 1.5 convolution_select_fusion
  145.7 1.6 fusion.3
  148.0 69.7 %shard_map.145 = (f32[64,16,128]{2,1,0:T(8,128)}, f32[8,128,128]{2,1,0:T(8,128)}, f32[8,128,128]{2,1,0:T(8,128)}) custom-call(f32[16,128]{1,0:T(8,128)} %copy.36.top_ref, f32[128,128]{1,0:T(8,128)} %slice_bitcast_fusion.17.pair_ref, f32[128,128]{1,0:T(8,128)} %get-tuple-element.97.quad_ref), custom_call_target="tpu_custom_call" | custom-call | tf_op jit(solution)/shard_map/pallas_call | solution.py:309
  217.6 1.6 gather_fusion.4
  220.0 14.5 %all_gather.3 = f32[128,128]{0,1:T(8,128)S(1)} all-gather(f32[128,16]{0,1:T(8,128)S(1)} %fusion.206), channel_id=1, replica_groups=mesh['cl'=64,'q'=2,'p'=2,'c'=2] {'q','p','c'}, dimensions={1}, use_global_device_ids=true | all-gather | bytes 73728 | tf_op jit(solution)/shard_map/all_gather | solution.py:388
  234.5 0.9 fusion.456
  235.4 0.9 fusion.455
  236.3 0.9 fusion.454
  237.2 0.9 fusion.453
  238.1 0.9 fusion.452
  238.9 0.9 fusion.451
  239.8 0.9 fusion.450
  240.8 0.9 fusion.447
  241.7 0.9 fusion.446
  242.6 0.9 fusion.444
  243.5 0.9 fusion.443
  244.3 0.9 fusion.442
  245.2 0.9 fusion.441
  252.6 1.1 fusion.1
  (161 shorter events, 15.4 us)
Async XLA Ops:
  0.0 1.7 copy-start
  0.0 25.0 %copy-start.26 = (f32[1,3,128]{2,0,1:T(1,128)S(1)}, f32[1,3,128]{2,0,1:T(1,128)}, u32[]{:S(2)}) copy-start(f32[1,3,128]{2,0,1:T(1,128)} %param.23) | copy-start | bytes 4612
  0.0 23.8 %copy-start.8 = (f32[1,3,512]{2,0,1:T(1,128)S(1)}, f32[1,3,512]{2,0,1:T(1,128)}, u32[]{:S(2)}) copy-start(f32[1,3,512]{2,0,1:T(1,128)} %param.18) | copy-start | bytes 18436
  0.0 19.4 %copy-start.22 = (f32[32,128]{1,0:T(8,128)S(1)}, f32[32,128]{1,0:T(8,128)}, u32[]{:S(2)}) copy-start(f32[32,128]{1,0:T(8,128)} %param.22) | copy-start | bytes 49156
  0.0 21.4 %copy-start.6 = (f32[64,128]{1,0:T(8,128)S(1)}, f32[64,128]{1,0:T(8,128)}, u32[]{:S(2)}) copy-start(f32[64,128]{1,0:T(8,128)} %param.21) | copy-start | bytes 98308
  0.0 23.8 %copy-start.23 = (s32[128,8]{0,1:T(8,128)S(1)}, s32[128,8]{0,1:T(8,128)}, u32[]{:S(2)}) copy-start(s32[128,8]{0,1:T(8,128)} %param.30) | copy-start | bytes 12292
  0.0 23.8 %copy-start.24 = (s32[64,8]{0,1:T(8,128)S(1)}, s32[64,8]{0,1:T(8,128)}, u32[]{:S(2)}) copy-start(s32[64,8]{0,1:T(8,128)} %param.31) | copy-start | bytes 6148
  0.1 24.3 %copy-start.25 = (s32[256,8]{0,1:T(8,128)S(1)}, s32[256,8]{0,1:T(8,128)}, u32[]{:S(2)}) copy-start(s32[256,8]{0,1:T(8,128)} %param.29) | copy-start | bytes 24580
  0.1 24.6 %copy-start.27 = (s32[1,8]{1,0:T(1,128)S(1)}, s32[1,8]{1,0:T(1,128)}, u32[]{:S(2)}) copy-start(s32[1,8]{1,0:T(1,128)} %param.28) | copy-start | bytes 100
  0.1 25.0 %copy-start.4 = (f32[1,128,128]{2,1,0:T(8,128)S(1)}, f32[1,128,128]{2,1,0:T(8,128)}, u32[]{:S(2)}) copy-start(f32[1,128,128]{2,1,0:T(8,128)} %param.20) | copy-start | bytes 196612
  0.1 25.3 %copy-start.7 = (f32[128,3,128]{2,0,1:T(8,128)S(1)}, f32[128,3,128]{2,0,1:T(8,128)}, u32[]{:S(2)}) copy-start(f32[128,3,128]{2,0,1:T(8,128)} %param.25) | copy-start | bytes 589828
  0.1 26.0 %copy-start.5 = (f32[64,3,128]{2,0,1:T(8,128)S(1)}, f32[64,3,128]{2,0,1:T(8,128)}, u32[]{:S(2)}) copy-start(f32[64,3,128]{2,0,1:T(8,128)} %param.26) | copy-start | bytes 294916
  1.7 26.9 %copy-start.28 = (s32[1,16]{1,0:T(1,128)S(1)}, s32[1,16]{1,0:T(1,128)}, u32[]{:S(2)}) copy-start(s32[1,16]{1,0:T(1,128)} %param.27) | copy-start | bytes 196
  1.7 27.9 %copy-start.1 = (f32[1,512,128]{2,1,0:T(8,128)S(1)}, f32[1,512,128]{2,1,0:T(8,128)}, u32[]{:S(2)}) copy-start(f32[1,512,128]{2,1,0:T(8,128)} %param.17) | copy-start | bytes 786436
  4.3 39.8 %collective-permute-start.6 = (f32[655,128]{1,0:T(8,128)S(1)}, f32[655,128]{1,0:T(8,128)S(1)}, u32[]{:S(2)}, u32[]{:S(2)}) collective-permute-start(f32[655,128]{1,0:T(8,128)S(1)} %pad_maximum_fusion), channel_id=1, source_target_pairs={{0,1},{1,2},{2,3},{3,4},{4,5},{5,6},{6,7},{7,8},{8,9},{9,10},{10,1... | collective-permute-start | bytes 1006088 | tf_op jit(solution)/shard_map/ppermute | solution.py:32
  6.2 40.0 %collective-permute-start.7 = (f32[655,128]{1,0:T(8,128)S(1)}, f32[655,128]{1,0:T(8,128)S(1)}, u32[]{:S(2)}, u32[]{:S(2)}) collective-permute-start(f32[655,128]{1,0:T(8,128)S(1)} %pad_maximum_fusion), channel_id=1, source_target_pairs={{1,0},{2,1},{3,2},{4,3},{5,4},{6,5},{7,6},{8,7},{9,8},{10,9},{11,1... | collective-permute-start | bytes 1006088 | tf_op jit(solution)/shard_map/ppermute | solution.py:32
  19.5 12.6 %collective-permute-start.1 = (f32[32,128]{1,0:T(8,128)S(1)}, f32[32,128]{1,0:T(8,128)S(1)}, u32[]{:S(2)}, u32[]{:S(2)}) collective-permute-start(f32[32,128]{1,0:T(8,128)S(1)} %copy-done.22), channel_id=1, source_target_pairs={{0,1},{1,0},{2,3},{3,2},{4,5},{5,4},{6,7},{7,6},{8,9},{9,8},{10,11... | collective-permute-start | bytes 49160 | tf_op jit(solution)/shard_map/ppermute | solution.py:26
  21.4 12.6 %collective-permute-start = (f32[64,128]{1,0:T(8,128)S(1)}, f32[64,128]{1,0:T(8,128)S(1)}, u32[]{:S(2)}, u32[]{:S(2)}) collective-permute-start(f32[64,128]{1,0:T(8,128)S(1)} %copy-done.6), channel_id=1, source_target_pairs={{0,1},{1,0},{2,3},{3,2},{4,5},{5,4},{6,7},{7,6},{8,9},{9,8},{10,11... | collective-permute-start | bytes 98312 | tf_op jit(solution)/shard_map/ppermute | solution.py:26
  32.1 5.8 %collective-permute-start.2 = (f32[64,128]{1,0:T(8,128)S(1)}, f32[64,128]{1,0:T(8,128)S(1)}, u32[]{:S(2)}, u32[]{:S(2)}) collective-permute-start(f32[64,128]{1,0:T(8,128)S(1)} %maximum_select_fusion.6), channel_id=1, source_target_pairs={{0,2},{1,3},{2,0},{3,1},{4,6},{5,7},{6,4},{7,5},{8,10},{9,11},{10,... | collective-permute-start | bytes 98312 | tf_op jit(solution)/shard_map/ppermute | solution.py:26
  38.2 3.3 %collective-permute-start.3 = (f32[3,128,128]{2,1,0:T(8,128)S(1)}, f32[3,128,128]{2,1,0:T(8,128)S(1)}, u32[]{:S(2)}, u32[]{:S(2)}) collective-permute-start(f32[3,128,128]{2,1,0:T(8,128)S(1)} %pad_maximum_fusion.1), channel_id=1, source_target_pairs={{0,1},{1,0},{2,3},{3,2},{4,5},{5,4},{6,7},{7,6},{8,9},{9,8},{10,11... | collective-permute-start | bytes 589832 | tf_op jit(solution)/shard_map/ppermute | solution.py:26
  42.2 13.3 %collective-permute-start.4 = (f32[2,128,128]{2,1,0:T(8,128)S(1)}, f32[2,128,128]{2,1,0:T(8,128)S(1)}, u32[]{:S(2)}, u32[]{:S(2)}) collective-permute-start(f32[2,128,128]{2,1,0:T(8,128)S(1)} %slice.660), channel_id=1, source_target_pairs={{0,2},{1,3},{2,0},{3,1},{4,6},{5,7},{6,4},{7,5},{8,10},{9,11},{10,... | collective-permute-start | bytes 393224 | tf_op jit(solution)/shard_map/ppermute | solution.py:26
  44.1 22.5 %collective-permute-start.8 = (f32[655,128]{1,0:T(8,128)S(1)}, f32[655,128]{1,0:T(8,128)S(1)}, u32[]{:S(2)}, u32[]{:S(2)}) collective-permute-start(f32[655,128]{1,0:T(8,128)S(1)} %collective-permute-done.6), channel_id=1, source_target_pairs={{0,1},{1,2},{2,3},{3,4},{4,5},{5,6},{6,7},{7,8},{8,9},{9,10},{10,1... | collective-permute-start | bytes 1006088 | tf_op jit(solution)/shard_map/ppermute | solution.py:32
  46.2 17.2 %collective-permute-start.9 = (f32[655,128]{1,0:T(8,128)S(1)}, f32[655,128]{1,0:T(8,128)S(1)}, u32[]{:S(2)}, u32[]{:S(2)}) collective-permute-start(f32[655,128]{1,0:T(8,128)S(1)} %collective-permute-done.7), channel_id=1, source_target_pairs={{1,0},{2,1},{3,2},{4,3},{5,4},{6,5},{7,6},{8,7},{9,8},{10,9},{11,1... | collective-permute-start | bytes 1006088 | tf_op jit(solution)/shard_map/ppermute | solution.py:32
  56.2 7.0 %collective-permute-start.5 = (f32[128,128]{1,0:T(8,128)S(1)}, f32[128,128]{1,0:T(8,128)S(1)}, u32[]{:S(2)}, u32[]{:S(2)}) collective-permute-start(f32[128,128]{1,0:T(8,128)S(1)} %get-tuple-element.98), channel_id=1, source_target_pairs={{0,4},{1,5},{2,6},{3,7},{4,0},{5,1},{6,2},{7,3},{8,12},{9,13},{10,... | collective-permute-start | bytes 196616 | tf_op jit(solution)/shard_map/ppermute | solution.py:26
  63.4 6.8 %copy-start.9 = (f32[655,128]{1,0:T(8,128)}, f32[655,128]{1,0:T(8,128)S(1)}, u32[]{:S(2)}) copy-start(f32[655,128]{1,0:T(8,128)S(1)} %collective-permute-done.9) | copy-start | bytes 1006084
  63.4 8.3 %collective-permute-start.11 = (f32[655,128]{1,0:T(8,128)S(1)}, f32[655,128]{1,0:T(8,128)S(1)}, u32[]{:S(2)}, u32[]{:S(2)}) collective-permute-start(f32[655,128]{1,0:T(8,128)S(1)} %collective-permute-done.9), channel_id=1, source_target_pairs={{1,0},{2,1},{3,2},{4,3},{5,4},{6,5},{7,6},{8,7},{9,8},{10,9},{11,1... | collective-permute-start | bytes 1006088 | tf_op jit(solution)/shard_map/ppermute | solution.py:32
  66.7 3.5 %copy-start.10 = (f32[655,128]{1,0:T(8,128)}, f32[655,128]{1,0:T(8,128)S(1)}, u32[]{:S(2)}) copy-start(f32[655,128]{1,0:T(8,128)S(1)} %collective-permute-done.8) | copy-start | bytes 1006084
  66.7 13.0 %collective-permute-start.10 = (f32[655,128]{1,0:T(8,128)S(1)}, f32[655,128]{1,0:T(8,128)S(1)}, u32[]{:S(2)}, u32[]{:S(2)}) collective-permute-start(f32[655,128]{1,0:T(8,128)S(1)} %collective-permute-done.8), channel_id=1, source_target_pairs={{0,1},{1,2},{2,3},{3,4},{4,5},{5,6},{6,7},{7,8},{8,9},{9,10},{10,1... | collective-permute-start | bytes 1006088 | tf_op jit(solution)/shard_map/ppermute | solution.py:32
  71.7 11.3 %copy-start.11 = (f32[655,128]{1,0:T(8,128)}, f32[655,128]{1,0:T(8,128)S(1)}, u32[]{:S(2)}) copy-start(f32[655,128]{1,0:T(8,128)S(1)} %collective-permute-done.11) | copy-start | bytes 1006084
  71.8 12.9 %collective-permute-start.13 = (f32[655,128]{1,0:T(8,128)S(1)}, f32[655,128]{1,0:T(8,128)S(1)}, u32[]{:S(2)}, u32[]{:S(2)}) collective-permute-start(f32[655,128]{1,0:T(8,128)S(1)} %collective-permute-done.11), channel_id=1, source_target_pairs={{1,0},{2,1},{3,2},{4,3},{5,4},{6,5},{7,6},{8,7},{9,8},{10,9},{11,1... | collective-permute-start | bytes 1006088 | tf_op jit(solution)/shard_map/ppermute | solution.py:32
  79.6 3.4 %copy-start.12 = (f32[655,128]{1,0:T(8,128)}, f32[655,128]{1,0:T(8,128)S(1)}, u32[]{:S(2)}) copy-start(f32[655,128]{1,0:T(8,128)S(1)} %collective-permute-done.10) | copy-start | bytes 1006084
  79.7 12.9 %collective-permute-start.12 = (f32[655,128]{1,0:T(8,128)S(1)}, f32[655,128]{1,0:T(8,128)S(1)}, u32[]{:S(2)}, u32[]{:S(2)}) collective-permute-start(f32[655,128]{1,0:T(8,128)S(1)} %collective-permute-done.10), channel_id=1, source_target_pairs={{0,1},{1,2},{2,3},{3,4},{4,5},{5,6},{6,7},{7,8},{8,9},{9,10},{10,1... | collective-permute-start | bytes 1006088 | tf_op jit(solution)/shard_map/ppermute | solution.py:32
  84.6 13.1 %collective-permute-start.15 = (f32[655,128]{1,0:T(8,128)S(1)}, f32[655,128]{1,0:T(8,128)S(1)}, u32[]{:S(2)}, u32[]{:S(2)}) collective-permute-start(f32[655,128]{1,0:T(8,128)S(1)} %collective-permute-done.13), channel_id=1, source_target_pairs={{1,0},{2,1},{3,2},{4,3},{5,4},{6,5},{7,6},{8,7},{9,8},{10,9},{11,1... | collective-permute-start | bytes 1006088 | tf_op jit(solution)/shard_map/ppermute | solution.py:32
  92.5 3.6 %copy-start.14 = (f32[655,128]{1,0:T(8,128)}, f32[655,128]{1,0:T(8,128)S(1)}, u32[]{:S(2)}) copy-start(f32[655,128]{1,0:T(8,128)S(1)} %collective-permute-done.12) | copy-start | bytes 1006084
  92.5 13.1 %collective-permute-start.14 = (f32[655,128]{1,0:T(8,128)S(1)}, f32[655,128]{1,0:T(8,128)S(1)}, u32[]{:S(2)}, u32[]{:S(2)}) collective-permute-start(f32[655,128]{1,0:T(8,128)S(1)} %collective-permute-done.12), channel_id=1, source_target_pairs={{0,1},{1,2},{2,3},{3,4},{4,5},{5,6},{6,7},{7,8},{8,9},{9,10},{10,1... | collective-permute-start | bytes 1006088 | tf_op jit(solution)/shard_map/ppermute | solution.py:32
  97.7 11.3 %copy-start.13 = (f32[655,128]{1,0:T(8,128)}, f32[655,128]{1,0:T(8,128)S(1)}, u32[]{:S(2)}) copy-start(f32[655,128]{1,0:T(8,128)S(1)} %collective-permute-done.15) | copy-start | bytes 1006084
  97.7 13.0 %collective-permute-start.17 = (f32[655,128]{1,0:T(8,128)S(1)}, f32[655,128]{1,0:T(8,128)S(1)}, u32[]{:S(2)}, u32[]{:S(2)}) collective-permute-start(f32[655,128]{1,0:T(8,128)S(1)} %collective-permute-done.15), channel_id=1, source_target_pairs={{1,0},{2,1},{3,2},{4,3},{5,4},{6,5},{7,6},{8,7},{9,8},{10,9},{11,1... | collective-permute-start | bytes 1006088 | tf_op jit(solution)/shard_map/ppermute | solution.py:32
  105.6 3.5 %copy-start.16 = (f32[655,128]{1,0:T(8,128)}, f32[655,128]{1,0:T(8,128)S(1)}, u32[]{:S(2)}) copy-start(f32[655,128]{1,0:T(8,128)S(1)} %collective-permute-done.14) | copy-start | bytes 1006084
  105.6 13.0 %collective-permute-start.16 = (f32[655,128]{1,0:T(8,128)S(1)}, f32[655,128]{1,0:T(8,128)S(1)}, u32[]{:S(2)}, u32[]{:S(2)}) collective-permute-start(f32[655,128]{1,0:T(8,128)S(1)} %collective-permute-done.14), channel_id=1, source_target_pairs={{0,1},{1,2},{2,3},{3,4},{4,5},{5,6},{6,7},{7,8},{8,9},{9,10},{10,1... | collective-permute-start | bytes 1006088 | tf_op jit(solution)/shard_map/ppermute | solution.py:32
  110.7 11.3 %copy-start.15 = (f32[655,128]{1,0:T(8,128)}, f32[655,128]{1,0:T(8,128)S(1)}, u32[]{:S(2)}) copy-start(f32[655,128]{1,0:T(8,128)S(1)} %collective-permute-done.17) | copy-start | bytes 1006084
  110.7 12.8 %collective-permute-start.19 = (f32[655,128]{1,0:T(8,128)S(1)}, f32[655,128]{1,0:T(8,128)S(1)}, u32[]{:S(2)}, u32[]{:S(2)}) collective-permute-start(f32[655,128]{1,0:T(8,128)S(1)} %collective-permute-done.17), channel_id=1, source_target_pairs={{1,0},{2,1},{3,2},{4,3},{5,4},{6,5},{7,6},{8,7},{9,8},{10,9},{11,1... | collective-permute-start | bytes 1006088 | tf_op jit(solution)/shard_map/ppermute | solution.py:32
  118.6 3.4 %copy-start.18 = (f32[655,128]{1,0:T(8,128)}, f32[655,128]{1,0:T(8,128)S(1)}, u32[]{:S(2)}) copy-start(f32[655,128]{1,0:T(8,128)S(1)} %collective-permute-done.16) | copy-start | bytes 1006084
  118.6 12.8 %collective-permute-start.18 = (f32[655,128]{1,0:T(8,128)S(1)}, f32[655,128]{1,0:T(8,128)S(1)}, u32[]{:S(2)}, u32[]{:S(2)}) collective-permute-start(f32[655,128]{1,0:T(8,128)S(1)} %collective-permute-done.16), channel_id=1, source_target_pairs={{0,1},{1,2},{2,3},{3,4},{4,5},{5,6},{6,7},{7,8},{8,9},{9,10},{10,1... | collective-permute-start | bytes 1006088 | tf_op jit(solution)/shard_map/ppermute | solution.py:32
  123.6 11.4 %copy-start.17 = (f32[655,128]{1,0:T(8,128)}, f32[655,128]{1,0:T(8,128)S(1)}, u32[]{:S(2)}) copy-start(f32[655,128]{1,0:T(8,128)S(1)} %collective-permute-done.19) | copy-start | bytes 1006084
  123.6 13.0 %collective-permute-start.21 = (f32[655,128]{1,0:T(8,128)S(1)}, f32[655,128]{1,0:T(8,128)S(1)}, u32[]{:S(2)}, u32[]{:S(2)}) collective-permute-start(f32[655,128]{1,0:T(8,128)S(1)} %collective-permute-done.19), channel_id=1, source_target_pairs={{1,0},{2,1},{3,2},{4,3},{5,4},{6,5},{7,6},{8,7},{9,8},{10,9},{11,1... | collective-permute-start | bytes 1006088 | tf_op jit(solution)/shard_map/ppermute | solution.py:32
  131.5 3.5 %copy-start.20 = (f32[655,128]{1,0:T(8,128)}, f32[655,128]{1,0:T(8,128)S(1)}, u32[]{:S(2)}) copy-start(f32[655,128]{1,0:T(8,128)S(1)} %collective-permute-done.18) | copy-start | bytes 1006084
  131.5 12.7 %collective-permute-start.20 = (f32[655,128]{1,0:T(8,128)S(1)}, f32[655,128]{1,0:T(8,128)S(1)}, u32[]{:S(2)}, u32[]{:S(2)}) collective-permute-start(f32[655,128]{1,0:T(8,128)S(1)} %collective-permute-done.18), channel_id=1, source_target_pairs={{0,1},{1,2},{2,3},{3,4},{4,5},{5,6},{6,7},{7,8},{8,9},{9,10},{10,1... | collective-permute-start | bytes 1006088 | tf_op jit(solution)/shard_map/ppermute | solution.py:32
  136.6 9.1 %copy-start.19 = (f32[655,128]{1,0:T(8,128)}, f32[655,128]{1,0:T(8,128)S(1)}, u32[]{:S(2)}) copy-start(f32[655,128]{1,0:T(8,128)S(1)} %collective-permute-done.21) | copy-start | bytes 1006084
  144.2 1.5 copy-start.21
  246.7 1.0 copy-start.3
  246.8 1.5 copy-start.2

commit v4 on v3

--- a/solution.py
+++ b/solution.py
@@ -209,17 +209,21 @@
     pair_land[...] = jnp.zeros(pair_land.shape, jnp.float32)
     quad_land[...] = jnp.zeros(quad_land.shape, jnp.float32)
     barrier = pltpu.get_barrier_semaphore()
-    extra = (-12, -6, -4, -2, 2, 4, 6, 12)
+    extra = (-16, -12, -8, -6, -4, -2, 2, 4, 6, 8, 12, 16)
 
     def inside(delta):
         return jnp.logical_and(dev + delta >= 0, dev + delta < count)
 
-    def greet(step, carry):
-        peer = lax.rem(me + step, clusters)
-        pl.semaphore_signal(barrier, inc=1, device_id={"cl": peer}, device_id_type=mesh_id)
-        return carry
-
-    lax.fori_loop(1, clusters, greet, 0)
+    rounds = clusters.bit_length() - 1
+
+    def partner_of(level):
+        bit = 2**level
+        return me + bit - 2 * (me // bit % 2) * bit
+
+    for level in range(rounds):
+        pl.semaphore_signal(
+            barrier, inc=1, device_id={"cl": partner_of(level)}, device_id_type=mesh_id
+        )
     for delta in extra:
         pl.semaphore_signal(
             barrier,
@@ -227,27 +231,17 @@
             device_id=device_coords(lax.rem(dev + delta + count, count)),
             device_id_type=mesh_id,
         )
-    pl.semaphore_wait(barrier, clusters - 1 + len(extra))
-
-    def outgoing(step):
-        peer = lax.rem(me + step, clusters)
+    pl.semaphore_wait(barrier, rounds + len(extra))
+
+    def doubling(level):
+        width = 2**level
+        base = me // width * width
         return pltpu.make_async_remote_copy(
-            src_ref=top_ref,
-            dst_ref=top_land.at[me],
-            send_sem=top_send.at[step],
-            recv_sem=top_recv.at[me],
-            device_id={"cl": peer},
-            device_id_type=mesh_id,
-        )
-
-    def incoming(step):
-        source = lax.rem(me - step + clusters, clusters)
-        return pltpu.make_async_remote_copy(
-            src_ref=top_ref,
-            dst_ref=top_land.at[source],
-            send_sem=top_send.at[step],
-            recv_sem=top_recv.at[source],
-            device_id={"cl": source},
+            src_ref=top_land.at[pl.ds(base, width)],
+            dst_ref=top_land.at[pl.ds(base, width)],
+            send_sem=top_send.at[level],
+            recv_sem=top_recv.at[level],
+            device_id={"cl": partner_of(level)},
             device_id_type=mesh_id,
         )
 
@@ -272,19 +266,13 @@
             def _():
                 partner_copy(src, land, send_sem, recv_sem, slot, dev - offset * stride).start()
 
-    def send(step, carry):
-        outgoing(step).start()
-        return carry
-
-    lax.fori_loop(1, clusters, send, 0)
-    top_land[me] = top_ref[...]
-
-    def finish(step, carry):
-        outgoing(step).wait_send()
-        incoming(step).wait_recv()
-        return carry
-
-    lax.fori_loop(1, clusters, finish, 0)
+    own = pltpu.make_async_copy(top_ref, top_land.at[me], top_send.at[rounds])
+    own.start()
+    own.wait()
+    for level in range(rounds):
+        doubling(level).start()
+        doubling(level).wait_send()
+        doubling(level).wait_recv()
     for src, land, send_sem, recv_sem, stride in partners:
         for slot, offset in enumerate(OFFSETS):
 

time: 258 us -> 261 us (1.012)
  Pallas kernels: 69.7 us -> 73.3 us
    pallas_call x1, Pallas kernels: 69.7 us -> 73.3 us  [exchange(): pl.pallas_call(functools.partial(exchange_kernel, clusters), out_shape=(j...]
where the time goes in v4:
time: 261 us; the launch traced here: 257 us
  starting transfers between devices  91.2 us (35%)
  Pallas kernels  73.3 us (28%)
  matrix products  33.6 us (13%)
  local copies, waits for them, and re-layouts  22.6 us (9%)
  waiting for transfers between devices  16.2 us (6%)
  blocking collectives  14.2 us (5%)
  other arithmetic  4.61 us (2%)
    ppermute x16, starting transfers between devices, from_behind(): return lax.ppermute(block, axis, route)  79.2 us
    pallas_call x1, Pallas kernels, exchange(): pl.pallas_call(functools.partial(exchange_kernel, clusters), out_shape=(j...  73.3 us
    dot_general x17, matrix products, contribution(): jnp.dot(kernel_block(own_points, coords), block[:leaf_points], precision=...  26 us
    all_gather x1, blocking collectives, per_device(): local_top = lax.all_gather(top_cols, MEMBERS, axis=1, tiled=True)  14.2 us
    unnamed x75, local copies, waits for them, and re-layouts  12.5 us
    ppermute x6, starting transfers between devices, from_partner(): return lax.ppermute(value, axis, pairs)  12 us
    ppermute x6, waiting for transfers between devices, from_partner(): return lax.ppermute(value, axis, pairs)  8.61 us
    ppermute x16, waiting for transfers between devices, from_behind(): return lax.ppermute(block, axis, route)  7.58 us
  transfers between devices with their start and end apart: 22, of which 4 were waited for; matrix products, arithmetic and copies ran while one was open for 12% of the time, Pallas kernels for 0%

profile of v4, /device:TPU:24, one launch (start us, length us, event | category | flops | bytes accessed | tf_op | source)
XLA Modules:
  0.0 257.0 jit_solution(16552074626939446752)
XLA Ops:
  1.7 1.6 fusion.407
  3.3 1.0 pad_maximum_fusion
  4.3 1.9 collective-permute-start.6
  6.2 13.2 %collective-permute-start.7 = (f32[655,128]{1,0:T(8,128)S(1)}, f32[655,128]{1,0:T(8,128)S(1)}, u32[]{:S(2)}, u32[]{:S(2)}) collective-permute-start(f32[655,128]{1,0:T(8,128)S(1)} %pad_maximum_fusion), channel_id=1, source_target_pairs={{1,0},{2,1},{3,2},{4,3},{5,4},{6,5},{7,6},{8,7},{9,8},{10,9},{11,1... | collective-permute-start | bytes 1006088 | tf_op jit(solution)/shard_map/ppermute | solution.py:32
  19.5 1.9 collective-permute-start.1
  21.4 2.4 collective-permute-start
  26.9 1.6 gather_fusion.1
  28.6 1.0 compare_reduce_fusion.8
  29.6 1.6 convolution_select_fusion.16
  32.1 1.9 collective-permute-start.2
  34.3 3.6 %collective-permute-done.2 = f32[64,128]{1,0:T(8,128)S(1)} collective-permute-done((f32[64,128]{1,0:T(8,128)S(1)}, f32[64,128]{1,0:T(8,128)S(1)}, u32[]{:S(2)}, u32[]{:S(2)}) %collective-permute-start.2) | collective-permute-done | bytes 32800 | tf_op jit(solution)/shard_map/ppermute | solution.py:26
  38.2 1.9 collective-permute-start.3
  40.1 1.4 collective-permute-done.3
  42.2 1.9 collective-permute-start.4
  44.1 2.0 collective-permute-start.8
  46.2 7.7 %collective-permute-start.9 = (f32[655,128]{1,0:T(8,128)S(1)}, f32[655,128]{1,0:T(8,128)S(1)}, u32[]{:S(2)}, u32[]{:S(2)}) collective-permute-start(f32[655,128]{1,0:T(8,128)S(1)} %collective-permute-done.7), channel_id=1, source_target_pairs={{1,0},{2,1},{3,2},{4,3},{5,4},{6,5},{7,6},{8,7},{9,8},{10,9},{11,1... | collective-permute-start | bytes 1006088 | tf_op jit(solution)/shard_map/ppermute | solution.py:32
  54.0 1.6 fusion.17
  56.2 1.9 collective-permute-start.5
  58.1 1.5 fusion.16
  59.6 3.6 %collective-permute-done.5 = f32[128,128]{1,0:T(8,128)S(1)} collective-permute-done((f32[128,128]{1,0:T(8,128)S(1)}, f32[128,128]{1,0:T(8,128)S(1)}, u32[]{:S(2)}, u32[]{:S(2)}) %collective-permute-start.5) | collective-permute-done | bytes 65568 | tf_op jit(solution)/shard_map/ppermute | solution.py:26
  63.4 3.2 %collective-permute-start.11 = (f32[655,128]{1,0:T(8,128)S(1)}, f32[655,128]{1,0:T(8,128)S(1)}, u32[]{:S(2)}, u32[]{:S(2)}) collective-permute-start(f32[655,128]{1,0:T(8,128)S(1)} %collective-permute-done.9), channel_id=1, source_target_pairs={{1,0},{2,1},{3,2},{4,3},{5,4},{6,5},{7,6},{8,7},{9,8},{10,9},{11,1... | collective-permute-start | bytes 1006088 | tf_op jit(solution)/shard_map/ppermute | solution.py:32
  66.7 1.9 collective-permute-start.10
  68.6 1.5 convolution_select_fusion.12
  70.2 1.5 fusion.15
  71.8 7.9 %collective-permute-start.13 = (f32[655,128]{1,0:T(8,128)S(1)}, f32[655,128]{1,0:T(8,128)S(1)}, u32[]{:S(2)}, u32[]{:S(2)}) collective-permute-start(f32[655,128]{1,0:T(8,128)S(1)} %collective-permute-done.11), channel_id=1, source_target_pairs={{1,0},{2,1},{3,2},{4,3},{5,4},{6,5},{7,6},{8,7},{9,8},{10,9},{11,1... | collective-permute-start | bytes 1006088 | tf_op jit(solution)/shard_map/ppermute | solution.py:32
  79.7 1.9 collective-permute-start.12
  81.6 1.5 convolution_select_fusion.10
  83.1 1.5 fusion.13
  84.6 7.9 %collective-permute-start.15 = (f32[655,128]{1,0:T(8,128)S(1)}, f32[655,128]{1,0:T(8,128)S(1)}, u32[]{:S(2)}, u32[]{:S(2)}) collective-permute-start(f32[655,128]{1,0:T(8,128)S(1)} %collective-permute-done.13), channel_id=1, source_target_pairs={{1,0},{2,1},{3,2},{4,3},{5,4},{6,5},{7,6},{8,7},{9,8},{10,9},{11,1... | collective-permute-start | bytes 1006088 | tf_op jit(solution)/shard_map/ppermute | solution.py:32
  92.5 2.1 collective-permute-start.14
  94.7 1.5 convolution_select_fusion.8
  96.2 1.6 fusion.11
  97.7 7.9 %collective-permute-start.17 = (f32[655,128]{1,0:T(8,128)S(1)}, f32[655,128]{1,0:T(8,128)S(1)}, u32[]{:S(2)}, u32[]{:S(2)}) collective-permute-start(f32[655,128]{1,0:T(8,128)S(1)} %collective-permute-done.15), channel_id=1, source_target_pairs={{1,0},{2,1},{3,2},{4,3},{5,4},{6,5},{7,6},{8,7},{9,8},{10,9},{11,1... | collective-permute-start | bytes 1006088 | tf_op jit(solution)/shard_map/ppermute | solution.py:32
  105.6 1.9 collective-permute-start.16
  107.6 1.5 convolution_select_fusion.6
  109.1 1.6 fusion.9
  110.7 7.9 %collective-permute-start.19 = (f32[655,128]{1,0:T(8,128)S(1)}, f32[655,128]{1,0:T(8,128)S(1)}, u32[]{:S(2)}, u32[]{:S(2)}) collective-permute-start(f32[655,128]{1,0:T(8,128)S(1)} %collective-permute-done.17), channel_id=1, source_target_pairs={{1,0},{2,1},{3,2},{4,3},{5,4},{6,5},{7,6},{8,7},{9,8},{10,9},{11,1... | collective-permute-start | bytes 1006088 | tf_op jit(solution)/shard_map/ppermute | solution.py:32
  118.6 1.9 collective-permute-start.18
  120.6 1.5 convolution_select_fusion.4
  122.1 1.5 fusion.7
  123.6 7.9 %collective-permute-start.21 = (f32[655,128]{1,0:T(8,128)S(1)}, f32[655,128]{1,0:T(8,128)S(1)}, u32[]{:S(2)}, u32[]{:S(2)}) collective-permute-start(f32[655,128]{1,0:T(8,128)S(1)} %collective-permute-done.19), channel_id=1, source_target_pairs={{1,0},{2,1},{3,2},{4,3},{5,4},{6,5},{7,6},{8,7},{9,8},{10,9},{11,1... | collective-permute-start | bytes 1006088 | tf_op jit(solution)/shard_map/ppermute | solution.py:32
  131.5 1.9 collective-permute-start.20
  133.4 1.6 convolution_select_fusion.2
  135.0 1.6 fusion.5
  136.6 7.5 %collective-permute-done.20 = f32[655,128]{1,0:T(8,128)S(1)} collective-permute-done((f32[655,128]{1,0:T(8,128)S(1)}, f32[655,128]{1,0:T(8,128)S(1)}, u32[]{:S(2)}, u32[]{:S(2)}) %collective-permute-start.20) | collective-permute-done | bytes 335392 | tf_op jit(solution)/shard_map/ppermute | solution.py:32
  144.2 1.5 convolution_select_fusion
  145.7 1.6 fusion.3
  148.0 73.3 %shard_map.145 = (f32[64,16,128]{2,1,0:T(8,128)}, f32[8,128,128]{2,1,0:T(8,128)}, f32[8,128,128]{2,1,0:T(8,128)}) custom-call(f32[16,128]{1,0:T(8,128)} %copy.36.top_ref, f32[128,128]{1,0:T(8,128)} %slice_bitcast_fusion.17.pair_ref, f32[128,128]{1,0:T(8,128)} %get-tuple-element.97.quad_ref), custom_call_target="tpu_custom_call" | custom-call | tf_op jit(solution)/shard_map/pallas_call | solution.py:297
  221.3 1.6 gather_fusion.4
  223.6 14.2 %all_gather.3 = f32[128,128]{0,1:T(8,128)S(1)} all-gather(f32[128,16]{0,1:T(8,128)S(1)} %fusion.206), channel_id=1, replica_groups=mesh['cl'=64,'q'=2,'p'=2,'c'=2] {'q','p','c'}, dimensions={1}, use_global_device_ids=true | all-gather | bytes 73728 | tf_op jit(solution)/shard_map/all_gather | solution.py:376
  237.8 0.9 fusion.456
  238.7 0.9 fusion.455
  239.6 0.9 fusion.454
  240.5 0.9 fusion.453
  241.4 0.9 fusion.452
  242.3 0.9 fusion.451
  243.2 0.9 fusion.450
  244.1 0.9 fusion.447
  245.0 0.9 fusion.446
  245.9 0.9 fusion.444
  246.8 0.9 fusion.443
  247.7 0.9 fusion.442
  248.6 0.9 fusion.441
  255.9 1.1 fusion.1
  (161 shorter events, 15.4 us)
Async XLA Ops:
  0.0 1.7 copy-start
  0.0 25.0 %copy-start.26 = (f32[1,3,128]{2,0,1:T(1,128)S(1)}, f32[1,3,128]{2,0,1:T(1,128)}, u32[]{:S(2)}) copy-start(f32[1,3,128]{2,0,1:T(1,128)} %param.23) | copy-start | bytes 4612
  0.0 23.8 %copy-start.8 = (f32[1,3,512]{2,0,1:T(1,128)S(1)}, f32[1,3,512]{2,0,1:T(1,128)}, u32[]{:S(2)}) copy-start(f32[1,3,512]{2,0,1:T(1,128)} %param.18) | copy-start | bytes 18436
  0.0 19.4 %copy-start.22 = (f32[32,128]{1,0:T(8,128)S(1)}, f32[32,128]{1,0:T(8,128)}, u32[]{:S(2)}) copy-start(f32[32,128]{1,0:T(8,128)} %param.22) | copy-start | bytes 49156
  0.0 21.4 %copy-start.6 = (f32[64,128]{1,0:T(8,128)S(1)}, f32[64,128]{1,0:T(8,128)}, u32[]{:S(2)}) copy-start(f32[64,128]{1,0:T(8,128)} %param.21) | copy-start | bytes 98308
  0.0 23.8 %copy-start.23 = (s32[128,8]{0,1:T(8,128)S(1)}, s32[128,8]{0,1:T(8,128)}, u32[]{:S(2)}) copy-start(s32[128,8]{0,1:T(8,128)} %param.30) | copy-start | bytes 12292
  0.0 23.8 %copy-start.24 = (s32[64,8]{0,1:T(8,128)S(1)}, s32[64,8]{0,1:T(8,128)}, u32[]{:S(2)}) copy-start(s32[64,8]{0,1:T(8,128)} %param.31) | copy-start | bytes 6148
  0.1 24.3 %copy-start.25 = (s32[256,8]{0,1:T(8,128)S(1)}, s32[256,8]{0,1:T(8,128)}, u32[]{:S(2)}) copy-start(s32[256,8]{0,1:T(8,128)} %param.29) | copy-start | bytes 24580
  0.1 24.6 %copy-start.27 = (s32[1,8]{1,0:T(1,128)S(1)}, s32[1,8]{1,0:T(1,128)}, u32[]{:S(2)}) copy-start(s32[1,8]{1,0:T(1,128)} %param.28) | copy-start | bytes 100
  0.1 25.0 %copy-start.4 = (f32[1,128,128]{2,1,0:T(8,128)S(1)}, f32[1,128,128]{2,1,0:T(8,128)}, u32[]{:S(2)}) copy-start(f32[1,128,128]{2,1,0:T(8,128)} %param.20) | copy-start | bytes 196612
  0.1 25.3 %copy-start.7 = (f32[128,3,128]{2,0,1:T(8,128)S(1)}, f32[128,3,128]{2,0,1:T(8,128)}, u32[]{:S(2)}) copy-start(f32[128,3,128]{2,0,1:T(8,128)} %param.25) | copy-start | bytes 589828
  0.1 26.0 %copy-start.5 = (f32[64,3,128]{2,0,1:T(8,128)S(1)}, f32[64,3,128]{2,0,1:T(8,128)}, u32[]{:S(2)}) copy-start(f32[64,3,128]{2,0,1:T(8,128)} %param.26) | copy-start | bytes 294916
  1.7 26.9 %copy-start.28 = (s32[1,16]{1,0:T(1,128)S(1)}, s32[1,16]{1,0:T(1,128)}, u32[]{:S(2)}) copy-start(s32[1,16]{1,0:T(1,128)} %param.27) | copy-start | bytes 196
  1.7 27.9 %copy-start.1 = (f32[1,512,128]{2,1,0:T(8,128)S(1)}, f32[1,512,128]{2,1,0:T(8,128)}, u32[]{:S(2)}) copy-start(f32[1,512,128]{2,1,0:T(8,128)} %param.17) | copy-start | bytes 786436
  4.3 39.8 %collective-permute-start.6 = (f32[655,128]{1,0:T(8,128)S(1)}, f32[655,128]{1,0:T(8,128)S(1)}, u32[]{:S(2)}, u32[]{:S(2)}) collective-permute-start(f32[655,128]{1,0:T(8,128)S(1)} %pad_maximum_fusion), channel_id=1, source_target_pairs={{0,1},{1,2},{2,3},{3,4},{4,5},{5,6},{6,7},{7,8},{8,9},{9,10},{10,1... | collective-permute-start | bytes 1006088 | tf_op jit(solution)/shard_map/ppermute | solution.py:32
  6.2 40.0 %collective-permute-start.7 = (f32[655,128]{1,0:T(8,128)S(1)}, f32[655,128]{1,0:T(8,128)S(1)}, u32[]{:S(2)}, u32[]{:S(2)}) collective-permute-start(f32[655,128]{1,0:T(8,128)S(1)} %pad_maximum_fusion), channel_id=1, source_target_pairs={{1,0},{2,1},{3,2},{4,3},{5,4},{6,5},{7,6},{8,7},{9,8},{10,9},{11,1... | collective-permute-start | bytes 1006088 | tf_op jit(solution)/shard_map/ppermute | solution.py:32
  19.5 12.6 %collective-permute-start.1 = (f32[32,128]{1,0:T(8,128)S(1)}, f32[32,128]{1,0:T(8,128)S(1)}, u32[]{:S(2)}, u32[]{:S(2)}) collective-permute-start(f32[32,128]{1,0:T(8,128)S(1)} %copy-done.22), channel_id=1, source_target_pairs={{0,1},{1,0},{2,3},{3,2},{4,5},{5,4},{6,7},{7,6},{8,9},{9,8},{10,11... | collective-permute-start | bytes 49160 | tf_op jit(solution)/shard_map/ppermute | solution.py:26
  21.4 12.6 %collective-permute-start = (f32[64,128]{1,0:T(8,128)S(1)}, f32[64,128]{1,0:T(8,128)S(1)}, u32[]{:S(2)}, u32[]{:S(2)}) collective-permute-start(f32[64,128]{1,0:T(8,128)S(1)} %copy-done.6), channel_id=1, source_target_pairs={{0,1},{1,0},{2,3},{3,2},{4,5},{5,4},{6,7},{7,6},{8,9},{9,8},{10,11... | collective-permute-start | bytes 98312 | tf_op jit(solution)/shard_map/ppermute | solution.py:26
  32.1 5.8 %collective-permute-start.2 = (f32[64,128]{1,0:T(8,128)S(1)}, f32[64,128]{1,0:T(8,128)S(1)}, u32[]{:S(2)}, u32[]{:S(2)}) collective-permute-start(f32[64,128]{1,0:T(8,128)S(1)} %maximum_select_fusion.6), channel_id=1, source_target_pairs={{0,2},{1,3},{2,0},{3,1},{4,6},{5,7},{6,4},{7,5},{8,10},{9,11},{10,... | collective-permute-start | bytes 98312 | tf_op jit(solution)/shard_map/ppermute | solution.py:26
  38.2 3.3 %collective-permute-start.3 = (f32[3,128,128]{2,1,0:T(8,128)S(1)}, f32[3,128,128]{2,1,0:T(8,128)S(1)}, u32[]{:S(2)}, u32[]{:S(2)}) collective-permute-start(f32[3,128,128]{2,1,0:T(8,128)S(1)} %pad_maximum_fusion.1), channel_id=1, source_target_pairs={{0,1},{1,0},{2,3},{3,2},{4,5},{5,4},{6,7},{7,6},{8,9},{9,8},{10,11... | collective-permute-start | bytes 589832 | tf_op jit(solution)/shard_map/ppermute | solution.py:26
  42.2 13.3 %collective-permute-start.4 = (f32[2,128,128]{2,1,0:T(8,128)S(1)}, f32[2,128,128]{2,1,0:T(8,128)S(1)}, u32[]{:S(2)}, u32[]{:S(2)}) collective-permute-start(f32[2,128,128]{2,1,0:T(8,128)S(1)} %slice.660), channel_id=1, source_target_pairs={{0,2},{1,3},{2,0},{3,1},{4,6},{5,7},{6,4},{7,5},{8,10},{9,11},{10,... | collective-permute-start | bytes 393224 | tf_op jit(solution)/shard_map/ppermute | solution.py:26
  44.1 22.5 %collective-permute-start.8 = (f32[655,128]{1,0:T(8,128)S(1)}, f32[655,128]{1,0:T(8,128)S(1)}, u32[]{:S(2)}, u32[]{:S(2)}) collective-permute-start(f32[655,128]{1,0:T(8,128)S(1)} %collective-permute-done.6), channel_id=1, source_target_pairs={{0,1},{1,2},{2,3},{3,4},{4,5},{5,6},{6,7},{7,8},{8,9},{9,10},{10,1... | collective-permute-start | bytes 1006088 | tf_op jit(solution)/shard_map/ppermute | solution.py:32
  46.2 17.2 %collective-permute-start.9 = (f32[655,128]{1,0:T(8,128)S(1)}, f32[655,128]{1,0:T(8,128)S(1)}, u32[]{:S(2)}, u32[]{:S(2)}) collective-permute-start(f32[655,128]{1,0:T(8,128)S(1)} %collective-permute-done.7), channel_id=1, source_target_pairs={{1,0},{2,1},{3,2},{4,3},{5,4},{6,5},{7,6},{8,7},{9,8},{10,9},{11,1... | collective-permute-start | bytes 1006088 | tf_op jit(solution)/shard_map/ppermute | solution.py:32
  56.2 7.0 %collective-permute-start.5 = (f32[128,128]{1,0:T(8,128)S(1)}, f32[128,128]{1,0:T(8,128)S(1)}, u32[]{:S(2)}, u32[]{:S(2)}) collective-permute-start(f32[128,128]{1,0:T(8,128)S(1)} %get-tuple-element.98), channel_id=1, source_target_pairs={{0,4},{1,5},{2,6},{3,7},{4,0},{5,1},{6,2},{7,3},{8,12},{9,13},{10,... | collective-permute-start | bytes 196616 | tf_op jit(solution)/shard_map/ppermute | solution.py:26
  63.4 6.8 %copy-start.9 = (f32[655,128]{1,0:T(8,128)}, f32[655,128]{1,0:T(8,128)S(1)}, u32[]{:S(2)}) copy-start(f32[655,128]{1,0:T(8,128)S(1)} %collective-permute-done.9) | copy-start | bytes 1006084
  63.4 8.3 %collective-permute-start.11 = (f32[655,128]{1,0:T(8,128)S(1)}, f32[655,128]{1,0:T(8,128)S(1)}, u32[]{:S(2)}, u32[]{:S(2)}) collective-permute-start(f32[655,128]{1,0:T(8,128)S(1)} %collective-permute-done.9), channel_id=1, source_target_pairs={{1,0},{2,1},{3,2},{4,3},{5,4},{6,5},{7,6},{8,7},{9,8},{10,9},{11,1... | collective-permute-start | bytes 1006088 | tf_op jit(solution)/shard_map/ppermute | solution.py:32
  66.7 3.5 %copy-start.10 = (f32[655,128]{1,0:T(8,128)}, f32[655,128]{1,0:T(8,128)S(1)}, u32[]{:S(2)}) copy-start(f32[655,128]{1,0:T(8,128)S(1)} %collective-permute-done.8) | copy-start | bytes 1006084
  66.7 13.0 %collective-permute-start.10 = (f32[655,128]{1,0:T(8,128)S(1)}, f32[655,128]{1,0:T(8,128)S(1)}, u32[]{:S(2)}, u32[]{:S(2)}) collective-permute-start(f32[655,128]{1,0:T(8,128)S(1)} %collective-permute-done.8), channel_id=1, source_target_pairs={{0,1},{1,2},{2,3},{3,4},{4,5},{5,6},{6,7},{7,8},{8,9},{9,10},{10,1... | collective-permute-start | bytes 1006088 | tf_op jit(solution)/shard_map/ppermute | solution.py:32
  71.7 11.3 %copy-start.11 = (f32[655,128]{1,0:T(8,128)}, f32[655,128]{1,0:T(8,128)S(1)}, u32[]{:S(2)}) copy-start(f32[655,128]{1,0:T(8,128)S(1)} %collective-permute-done.11) | copy-start | bytes 1006084
  71.8 12.9 %collective-permute-start.13 = (f32[655,128]{1,0:T(8,128)S(1)}, f32[655,128]{1,0:T(8,128)S(1)}, u32[]{:S(2)}, u32[]{:S(2)}) collective-permute-start(f32[655,128]{1,0:T(8,128)S(1)} %collective-permute-done.11), channel_id=1, source_target_pairs={{1,0},{2,1},{3,2},{4,3},{5,4},{6,5},{7,6},{8,7},{9,8},{10,9},{11,1... | collective-permute-start | bytes 1006088 | tf_op jit(solution)/shard_map/ppermute | solution.py:32
  79.6 3.4 %copy-start.12 = (f32[655,128]{1,0:T(8,128)}, f32[655,128]{1,0:T(8,128)S(1)}, u32[]{:S(2)}) copy-start(f32[655,128]{1,0:T(8,128)S(1)} %collective-permute-done.10) | copy-start | bytes 1006084
  79.7 12.9 %collective-permute-start.12 = (f32[655,128]{1,0:T(8,128)S(1)}, f32[655,128]{1,0:T(8,128)S(1)}, u32[]{:S(2)}, u32[]{:S(2)}) collective-permute-start(f32[655,128]{1,0:T(8,128)S(1)} %collective-permute-done.10), channel_id=1, source_target_pairs={{0,1},{1,2},{2,3},{3,4},{4,5},{5,6},{6,7},{7,8},{8,9},{9,10},{10,1... | collective-permute-start | bytes 1006088 | tf_op jit(solution)/shard_map/ppermute | solution.py:32
  84.6 13.1 %collective-permute-start.15 = (f32[655,128]{1,0:T(8,128)S(1)}, f32[655,128]{1,0:T(8,128)S(1)}, u32[]{:S(2)}, u32[]{:S(2)}) collective-permute-start(f32[655,128]{1,0:T(8,128)S(1)} %collective-permute-done.13), channel_id=1, source_target_pairs={{1,0},{2,1},{3,2},{4,3},{5,4},{6,5},{7,6},{8,7},{9,8},{10,9},{11,1... | collective-permute-start | bytes 1006088 | tf_op jit(solution)/shard_map/ppermute | solution.py:32
  92.5 3.6 %copy-start.14 = (f32[655,128]{1,0:T(8,128)}, f32[655,128]{1,0:T(8,128)S(1)}, u32[]{:S(2)}) copy-start(f32[655,128]{1,0:T(8,128)S(1)} %collective-permute-done.12) | copy-start | bytes 1006084
  92.5 13.1 %collective-permute-start.14 = (f32[655,128]{1,0:T(8,128)S(1)}, f32[655,128]{1,0:T(8,128)S(1)}, u32[]{:S(2)}, u32[]{:S(2)}) collective-permute-start(f32[655,128]{1,0:T(8,128)S(1)} %collective-permute-done.12), channel_id=1, source_target_pairs={{0,1},{1,2},{2,3},{3,4},{4,5},{5,6},{6,7},{7,8},{8,9},{9,10},{10,1... | collective-permute-start | bytes 1006088 | tf_op jit(solution)/shard_map/ppermute | solution.py:32
  97.7 11.3 %copy-start.13 = (f32[655,128]{1,0:T(8,128)}, f32[655,128]{1,0:T(8,128)S(1)}, u32[]{:S(2)}) copy-start(f32[655,128]{1,0:T(8,128)S(1)} %collective-permute-done.15) | copy-start | bytes 1006084
  97.7 13.0 %collective-permute-start.17 = (f32[655,128]{1,0:T(8,128)S(1)}, f32[655,128]{1,0:T(8,128)S(1)}, u32[]{:S(2)}, u32[]{:S(2)}) collective-permute-start(f32[655,128]{1,0:T(8,128)S(1)} %collective-permute-done.15), channel_id=1, source_target_pairs={{1,0},{2,1},{3,2},{4,3},{5,4},{6,5},{7,6},{8,7},{9,8},{10,9},{11,1... | collective-permute-start | bytes 1006088 | tf_op jit(solution)/shard_map/ppermute | solution.py:32
  105.6 3.5 %copy-start.16 = (f32[655,128]{1,0:T(8,128)}, f32[655,128]{1,0:T(8,128)S(1)}, u32[]{:S(2)}) copy-start(f32[655,128]{1,0:T(8,128)S(1)} %collective-permute-done.14) | copy-start | bytes 1006084
  105.6 13.0 %collective-permute-start.16 = (f32[655,128]{1,0:T(8,128)S(1)}, f32[655,128]{1,0:T(8,128)S(1)}, u32[]{:S(2)}, u32[]{:S(2)}) collective-permute-start(f32[655,128]{1,0:T(8,128)S(1)} %collective-permute-done.14), channel_id=1, source_target_pairs={{0,1},{1,2},{2,3},{3,4},{4,5},{5,6},{6,7},{7,8},{8,9},{9,10},{10,1... | collective-permute-start | bytes 1006088 | tf_op jit(solution)/shard_map/ppermute | solution.py:32
  110.7 11.3 %copy-start.15 = (f32[655,128]{1,0:T(8,128)}, f32[655,128]{1,0:T(8,128)S(1)}, u32[]{:S(2)}) copy-start(f32[655,128]{1,0:T(8,128)S(1)} %collective-permute-done.17) | copy-start | bytes 1006084
  110.7 12.8 %collective-permute-start.19 = (f32[655,128]{1,0:T(8,128)S(1)}, f32[655,128]{1,0:T(8,128)S(1)}, u32[]{:S(2)}, u32[]{:S(2)}) collective-permute-start(f32[655,128]{1,0:T(8,128)S(1)} %collective-permute-done.17), channel_id=1, source_target_pairs={{1,0},{2,1},{3,2},{4,3},{5,4},{6,5},{7,6},{8,7},{9,8},{10,9},{11,1... | collective-permute-start | bytes 1006088 | tf_op jit(solution)/shard_map/ppermute | solution.py:32
  118.6 3.4 %copy-start.18 = (f32[655,128]{1,0:T(8,128)}, f32[655,128]{1,0:T(8,128)S(1)}, u32[]{:S(2)}) copy-start(f32[655,128]{1,0:T(8,128)S(1)} %collective-permute-done.16) | copy-start | bytes 1006084
  118.6 12.8 %collective-permute-start.18 = (f32[655,128]{1,0:T(8,128)S(1)}, f32[655,128]{1,0:T(8,128)S(1)}, u32[]{:S(2)}, u32[]{:S(2)}) collective-permute-start(f32[655,128]{1,0:T(8,128)S(1)} %collective-permute-done.16), channel_id=1, source_target_pairs={{0,1},{1,2},{2,3},{3,4},{4,5},{5,6},{6,7},{7,8},{8,9},{9,10},{10,1... | collective-permute-start | bytes 1006088 | tf_op jit(solution)/shard_map/ppermute | solution.py:32
  123.6 11.4 %copy-start.17 = (f32[655,128]{1,0:T(8,128)}, f32[655,128]{1,0:T(8,128)S(1)}, u32[]{:S(2)}) copy-start(f32[655,128]{1,0:T(8,128)S(1)} %collective-permute-done.19) | copy-start | bytes 1006084
  123.6 13.0 %collective-permute-start.21 = (f32[655,128]{1,0:T(8,128)S(1)}, f32[655,128]{1,0:T(8,128)S(1)}, u32[]{:S(2)}, u32[]{:S(2)}) collective-permute-start(f32[655,128]{1,0:T(8,128)S(1)} %collective-permute-done.19), channel_id=1, source_target_pairs={{1,0},{2,1},{3,2},{4,3},{5,4},{6,5},{7,6},{8,7},{9,8},{10,9},{11,1... | collective-permute-start | bytes 1006088 | tf_op jit(solution)/shard_map/ppermute | solution.py:32
  131.5 3.5 %copy-start.20 = (f32[655,128]{1,0:T(8,128)}, f32[655,128]{1,0:T(8,128)S(1)}, u32[]{:S(2)}) copy-start(f32[655,128]{1,0:T(8,128)S(1)} %collective-permute-done.18) | copy-start | bytes 1006084
  131.5 12.7 %collective-permute-start.20 = (f32[655,128]{1,0:T(8,128)S(1)}, f32[655,128]{1,0:T(8,128)S(1)}, u32[]{:S(2)}, u32[]{:S(2)}) collective-permute-start(f32[655,128]{1,0:T(8,128)S(1)} %collective-permute-done.18), channel_id=1, source_target_pairs={{0,1},{1,2},{2,3},{3,4},{4,5},{5,6},{6,7},{7,8},{8,9},{9,10},{10,1... | collective-permute-start | bytes 1006088 | tf_op jit(solution)/shard_map/ppermute | solution.py:32
  136.6 9.1 %copy-start.19 = (f32[655,128]{1,0:T(8,128)}, f32[655,128]{1,0:T(8,128)S(1)}, u32[]{:S(2)}) copy-start(f32[655,128]{1,0:T(8,128)S(1)} %collective-permute-done.21) | copy-start | bytes 1006084
  144.2 1.5 copy-start.21
  250.0 1.0 copy-start.3
  250.2 1.5 copy-start.2

commit v5 on v3

--- a/solution.py
+++ b/solution.py
@@ -61,7 +61,7 @@
     right = jnp.transpose(coords, (1, 0, 2)).reshape(3, count * span)
     masked = jnp.where(valid[:, None, None], values, 0.0)
     flat = masked.reshape(count * span, values.shape[2])
-    return jnp.dot(kernel_block(own_coords, right), flat, precision=HIGHEST)
+    return jnp.dot(kernel_block(own_coords, right), flat, precision=lax.Precision.HIGH)
 
 
 def pair_total(partial_value, levels):
@@ -394,7 +394,7 @@
     local_leaf = batched_far(
         skel_leaf[0], leaf_blocks[:, rank:], leaf_blocks[:, :rank], leaf_entries >= 0
     ) + jnp.dot(transfer_leaf[0], local_pair, precision=HIGHEST)
-    product = near_field + jnp.dot(leaf_basis[0], local_leaf, precision=HIGHEST)
+    product = near_field + jnp.dot(leaf_basis[0], local_leaf, precision=lax.Precision.HIGH)
     return product[None]
 
 

time: 258 us -> 257 us (level)
  no operation moved by 1% of the time
where the time goes in v5:
time: 257 us; the launch traced here: 252 us
  starting transfers between devices  91.2 us (35%)
  Pallas kernels  69.6 us (27%)
  matrix products  32.4 us (13%)
  local copies, waits for them, and re-layouts  22.6 us (9%)
  waiting for transfers between devices  16.2 us (6%)
  blocking collectives  14.5 us (6%)
  other arithmetic  4.61 us (2%)
    ppermute x16, starting transfers between devices, from_behind(): return lax.ppermute(block, axis, route)  79.2 us
    pallas_call x1, Pallas kernels, exchange(): pl.pallas_call(functools.partial(exchange_kernel, clusters), out_shape=(j...  69.6 us
    dot_general x17, matrix products, contribution(): jnp.dot(kernel_block(own_points, coords), block[:leaf_points], precision=...  26 us
    all_gather x1, blocking collectives, per_device(): local_top = lax.all_gather(top_cols, MEMBERS, axis=1, tiled=True)  14.5 us
    unnamed x75, local copies, waits for them, and re-layouts  12.5 us
    ppermute x6, starting transfers between devices, from_partner(): return lax.ppermute(value, axis, pairs)  12 us
    ppermute x6, waiting for transfers between devices, from_partner(): return lax.ppermute(value, axis, pairs)  8.61 us
    ppermute x16, waiting for transfers between devices, from_behind(): return lax.ppermute(block, axis, route)  7.58 us
  transfers between devices with their start and end apart: 22, of which 4 were waited for; matrix products, arithmetic and copies ran while one was open for 12% of the time, Pallas kernels for 0%

profile of v5, /device:TPU:24, one launch (start us, length us, event | category | flops | bytes accessed | tf_op | source)
XLA Modules:
  0.0 252.5 jit_solution(11303544846349922699)
XLA Ops:
  1.7 1.6 fusion.407
  3.3 1.0 pad_maximum_fusion
  4.3 1.9 collective-permute-start.6
  6.2 13.2 %collective-permute-start.7 = (f32[655,128]{1,0:T(8,128)S(1)}, f32[655,128]{1,0:T(8,128)S(1)}, u32[]{:S(2)}, u32[]{:S(2)}) collective-permute-start(f32[655,128]{1,0:T(8,128)S(1)} %pad_maximum_fusion), channel_id=1, source_target_pairs={{1,0},{2,1},{3,2},{4,3},{5,4},{6,5},{7,6},{8,7},{9,8},{10,9},{11,1... | collective-permute-start | bytes 1006088 | tf_op jit(solution)/shard_map/ppermute | solution.py:32
  19.5 1.9 collective-permute-start.1
  21.4 2.4 collective-permute-start
  26.9 1.6 gather_fusion.1
  28.6 1.0 compare_reduce_fusion.8
  29.6 1.6 convolution_select_fusion.16
  32.1 1.9 collective-permute-start.2
  34.3 3.6 %collective-permute-done.2 = f32[64,128]{1,0:T(8,128)S(1)} collective-permute-done((f32[64,128]{1,0:T(8,128)S(1)}, f32[64,128]{1,0:T(8,128)S(1)}, u32[]{:S(2)}, u32[]{:S(2)}) %collective-permute-start.2) | collective-permute-done | bytes 32800 | tf_op jit(solution)/shard_map/ppermute | solution.py:26
  38.2 1.9 collective-permute-start.3
  40.1 1.4 collective-permute-done.3
  42.2 1.9 collective-permute-start.4
  44.1 2.0 collective-permute-start.8
  46.2 7.7 %collective-permute-start.9 = (f32[655,128]{1,0:T(8,128)S(1)}, f32[655,128]{1,0:T(8,128)S(1)}, u32[]{:S(2)}, u32[]{:S(2)}) collective-permute-start(f32[655,128]{1,0:T(8,128)S(1)} %collective-permute-done.7), channel_id=1, source_target_pairs={{1,0},{2,1},{3,2},{4,3},{5,4},{6,5},{7,6},{8,7},{9,8},{10,9},{11,1... | collective-permute-start | bytes 1006088 | tf_op jit(solution)/shard_map/ppermute | solution.py:32
  54.0 1.6 fusion.17
  56.2 1.9 collective-permute-start.5
  58.1 1.5 fusion.16
  59.6 3.6 %collective-permute-done.5 = f32[128,128]{1,0:T(8,128)S(1)} collective-permute-done((f32[128,128]{1,0:T(8,128)S(1)}, f32[128,128]{1,0:T(8,128)S(1)}, u32[]{:S(2)}, u32[]{:S(2)}) %collective-permute-start.5) | collective-permute-done | bytes 65568 | tf_op jit(solution)/shard_map/ppermute | solution.py:26
  63.4 3.2 %collective-permute-start.11 = (f32[655,128]{1,0:T(8,128)S(1)}, f32[655,128]{1,0:T(8,128)S(1)}, u32[]{:S(2)}, u32[]{:S(2)}) collective-permute-start(f32[655,128]{1,0:T(8,128)S(1)} %collective-permute-done.9), channel_id=1, source_target_pairs={{1,0},{2,1},{3,2},{4,3},{5,4},{6,5},{7,6},{8,7},{9,8},{10,9},{11,1... | collective-permute-start | bytes 1006088 | tf_op jit(solution)/shard_map/ppermute | solution.py:32
  66.7 1.9 collective-permute-start.10
  68.6 1.5 convolution_select_fusion.12
  70.2 1.5 fusion.15
  71.8 7.9 %collective-permute-start.13 = (f32[655,128]{1,0:T(8,128)S(1)}, f32[655,128]{1,0:T(8,128)S(1)}, u32[]{:S(2)}, u32[]{:S(2)}) collective-permute-start(f32[655,128]{1,0:T(8,128)S(1)} %collective-permute-done.11), channel_id=1, source_target_pairs={{1,0},{2,1},{3,2},{4,3},{5,4},{6,5},{7,6},{8,7},{9,8},{10,9},{11,1... | collective-permute-start | bytes 1006088 | tf_op jit(solution)/shard_map/ppermute | solution.py:32
  79.7 1.9 collective-permute-start.12
  81.6 1.5 convolution_select_fusion.10
  83.1 1.5 fusion.13
  84.6 7.9 %collective-permute-start.15 = (f32[655,128]{1,0:T(8,128)S(1)}, f32[655,128]{1,0:T(8,128)S(1)}, u32[]{:S(2)}, u32[]{:S(2)}) collective-permute-start(f32[655,128]{1,0:T(8,128)S(1)} %collective-permute-done.13), channel_id=1, source_target_pairs={{1,0},{2,1},{3,2},{4,3},{5,4},{6,5},{7,6},{8,7},{9,8},{10,9},{11,1... | collective-permute-start | bytes 1006088 | tf_op jit(solution)/shard_map/ppermute | solution.py:32
  92.5 2.1 collective-permute-start.14
  94.7 1.5 convolution_select_fusion.8
  96.2 1.6 fusion.11
  97.7 7.9 %collective-permute-start.17 = (f32[655,128]{1,0:T(8,128)S(1)}, f32[655,128]{1,0:T(8,128)S(1)}, u32[]{:S(2)}, u32[]{:S(2)}) collective-permute-start(f32[655,128]{1,0:T(8,128)S(1)} %collective-permute-done.15), channel_id=1, source_target_pairs={{1,0},{2,1},{3,2},{4,3},{5,4},{6,5},{7,6},{8,7},{9,8},{10,9},{11,1... | collective-permute-start | bytes 1006088 | tf_op jit(solution)/shard_map/ppermute | solution.py:32
  105.6 1.9 collective-permute-start.16
  107.6 1.5 convolution_select_fusion.6
  109.1 1.6 fusion.9
  110.7 7.9 %collective-permute-start.19 = (f32[655,128]{1,0:T(8,128)S(1)}, f32[655,128]{1,0:T(8,128)S(1)}, u32[]{:S(2)}, u32[]{:S(2)}) collective-permute-start(f32[655,128]{1,0:T(8,128)S(1)} %collective-permute-done.17), channel_id=1, source_target_pairs={{1,0},{2,1},{3,2},{4,3},{5,4},{6,5},{7,6},{8,7},{9,8},{10,9},{11,1... | collective-permute-start | bytes 1006088 | tf_op jit(solution)/shard_map/ppermute | solution.py:32
  118.6 1.9 collective-permute-start.18
  120.6 1.5 convolution_select_fusion.4
  122.1 1.5 fusion.7
  123.6 7.9 %collective-permute-start.21 = (f32[655,128]{1,0:T(8,128)S(1)}, f32[655,128]{1,0:T(8,128)S(1)}, u32[]{:S(2)}, u32[]{:S(2)}) collective-permute-start(f32[655,128]{1,0:T(8,128)S(1)} %collective-permute-done.19), channel_id=1, source_target_pairs={{1,0},{2,1},{3,2},{4,3},{5,4},{6,5},{7,6},{8,7},{9,8},{10,9},{11,1... | collective-permute-start | bytes 1006088 | tf_op jit(solution)/shard_map/ppermute | solution.py:32
  131.5 1.9 collective-permute-start.20
  133.4 1.6 convolution_select_fusion.2
  135.0 1.6 fusion.5
  136.6 7.5 %collective-permute-done.20 = f32[655,128]{1,0:T(8,128)S(1)} collective-permute-done((f32[655,128]{1,0:T(8,128)S(1)}, f32[655,128]{1,0:T(8,128)S(1)}, u32[]{:S(2)}, u32[]{:S(2)}) %collective-permute-start.20) | collective-permute-done | bytes 335392 | tf_op jit(solution)/shard_map/ppermute | solution.py:32
  144.2 1.5 convolution_select_fusion
  145.7 1.6 fusion.3
  148.0 69.6 %shard_map.145 = (f32[64,16,128]{2,1,0:T(8,128)}, f32[8,128,128]{2,1,0:T(8,128)}, f32[8,128,128]{2,1,0:T(8,128)}) custom-call(f32[16,128]{1,0:T(8,128)} %copy.36.top_ref, f32[128,128]{1,0:T(8,128)} %slice_bitcast_fusion.17.pair_ref, f32[128,128]{1,0:T(8,128)} %get-tuple-element.97.quad_ref), custom_call_target="tpu_custom_call" | custom-call | tf_op jit(solution)/shard_map/pallas_call | solution.py:309
  217.6 1.6 gather_fusion.4
  219.8 14.5 %all_gather.3 = f32[128,128]{0,1:T(8,128)S(1)} all-gather(f32[128,16]{0,1:T(8,128)S(1)} %fusion.206), channel_id=1, replica_groups=mesh['cl'=64,'q'=2,'p'=2,'c'=2] {'q','p','c'}, dimensions={1}, use_global_device_ids=true | all-gather | bytes 73728 | tf_op jit(solution)/shard_map/all_gather | solution.py:388
  234.3 0.9 fusion.456
  235.2 0.9 fusion.455
  236.1 0.9 fusion.454
  237.0 0.9 fusion.453
  237.8 0.9 fusion.452
  238.7 0.9 fusion.451
  239.6 0.9 fusion.450
  240.6 0.9 fusion.447
  241.5 0.9 fusion.446
  242.4 0.9 fusion.444
  243.2 0.9 fusion.443
  244.1 0.9 fusion.442
  245.0 0.9 fusion.441
  251.5 1.0 fusion.1
  (161 shorter events, 14.4 us)
Async XLA Ops:
  0.0 1.7 copy-start
  0.0 25.0 %copy-start.26 = (f32[1,3,128]{2,0,1:T(1,128)S(1)}, f32[1,3,128]{2,0,1:T(1,128)}, u32[]{:S(2)}) copy-start(f32[1,3,128]{2,0,1:T(1,128)} %param.23) | copy-start | bytes 4612
  0.0 23.8 %copy-start.8 = (f32[1,3,512]{2,0,1:T(1,128)S(1)}, f32[1,3,512]{2,0,1:T(1,128)}, u32[]{:S(2)}) copy-start(f32[1,3,512]{2,0,1:T(1,128)} %param.18) | copy-start | bytes 18436
  0.0 19.4 %copy-start.22 = (f32[32,128]{1,0:T(8,128)S(1)}, f32[32,128]{1,0:T(8,128)}, u32[]{:S(2)}) copy-start(f32[32,128]{1,0:T(8,128)} %param.22) | copy-start | bytes 49156
  0.0 21.4 %copy-start.6 = (f32[64,128]{1,0:T(8,128)S(1)}, f32[64,128]{1,0:T(8,128)}, u32[]{:S(2)}) copy-start(f32[64,128]{1,0:T(8,128)} %param.21) | copy-start | bytes 98308
  0.0 23.8 %copy-start.23 = (s32[128,8]{0,1:T(8,128)S(1)}, s32[128,8]{0,1:T(8,128)}, u32[]{:S(2)}) copy-start(s32[128,8]{0,1:T(8,128)} %param.30) | copy-start | bytes 12292
  0.0 23.8 %copy-start.24 = (s32[64,8]{0,1:T(8,128)S(1)}, s32[64,8]{0,1:T(8,128)}, u32[]{:S(2)}) copy-start(s32[64,8]{0,1:T(8,128)} %param.31) | copy-start | bytes 6148
  0.1 24.3 %copy-start.25 = (s32[256,8]{0,1:T(8,128)S(1)}, s32[256,8]{0,1:T(8,128)}, u32[]{:S(2)}) copy-start(s32[256,8]{0,1:T(8,128)} %param.29) | copy-start | bytes 24580
  0.1 24.6 %copy-start.27 = (s32[1,8]{1,0:T(1,128)S(1)}, s32[1,8]{1,0:T(1,128)}, u32[]{:S(2)}) copy-start(s32[1,8]{1,0:T(1,128)} %param.28) | copy-start | bytes 100
  0.1 25.0 %copy-start.4 = (f32[1,128,128]{2,1,0:T(8,128)S(1)}, f32[1,128,128]{2,1,0:T(8,128)}, u32[]{:S(2)}) copy-start(f32[1,128,128]{2,1,0:T(8,128)} %param.20) | copy-start | bytes 196612
  0.1 25.3 %copy-start.7 = (f32[128,3,128]{2,0,1:T(8,128)S(1)}, f32[128,3,128]{2,0,1:T(8,128)}, u32[]{:S(2)}) copy-start(f32[128,3,128]{2,0,1:T(8,128)} %param.25) | copy-start | bytes 589828
  0.1 26.0 %copy-start.5 = (f32[64,3,128]{2,0,1:T(8,128)S(1)}, f32[64,3,128]{2,0,1:T(8,128)}, u32[]{:S(2)}) copy-start(f32[64,3,128]{2,0,1:T(8,128)} %param.26) | copy-start | bytes 294916
  1.7 26.9 %copy-start.28 = (s32[1,16]{1,0:T(1,128)S(1)}, s32[1,16]{1,0:T(1,128)}, u32[]{:S(2)}) copy-start(s32[1,16]{1,0:T(1,128)} %param.27) | copy-start | bytes 196
  1.7 27.9 %copy-start.1 = (f32[1,512,128]{2,1,0:T(8,128)S(1)}, f32[1,512,128]{2,1,0:T(8,128)}, u32[]{:S(2)}) copy-start(f32[1,512,128]{2,1,0:T(8,128)} %param.17) | copy-start | bytes 786436
  4.3 39.8 %collective-permute-start.6 = (f32[655,128]{1,0:T(8,128)S(1)}, f32[655,128]{1,0:T(8,128)S(1)}, u32[]{:S(2)}, u32[]{:S(2)}) collective-permute-start(f32[655,128]{1,0:T(8,128)S(1)} %pad_maximum_fusion), channel_id=1, source_target_pairs={{0,1},{1,2},{2,3},{3,4},{4,5},{5,6},{6,7},{7,8},{8,9},{9,10},{10,1... | collective-permute-start | bytes 1006088 | tf_op jit(solution)/shard_map/ppermute | solution.py:32
  6.2 40.0 %collective-permute-start.7 = (f32[655,128]{1,0:T(8,128)S(1)}, f32[655,128]{1,0:T(8,128)S(1)}, u32[]{:S(2)}, u32[]{:S(2)}) collective-permute-start(f32[655,128]{1,0:T(8,128)S(1)} %pad_maximum_fusion), channel_id=1, source_target_pairs={{1,0},{2,1},{3,2},{4,3},{5,4},{6,5},{7,6},{8,7},{9,8},{10,9},{11,1... | collective-permute-start | bytes 1006088 | tf_op jit(solution)/shard_map/ppermute | solution.py:32
  19.5 12.6 %collective-permute-start.1 = (f32[32,128]{1,0:T(8,128)S(1)}, f32[32,128]{1,0:T(8,128)S(1)}, u32[]{:S(2)}, u32[]{:S(2)}) collective-permute-start(f32[32,128]{1,0:T(8,128)S(1)} %copy-done.22), channel_id=1, source_target_pairs={{0,1},{1,0},{2,3},{3,2},{4,5},{5,4},{6,7},{7,6},{8,9},{9,8},{10,11... | collective-permute-start | bytes 49160 | tf_op jit(solution)/shard_map/ppermute | solution.py:26
  21.4 12.6 %collective-permute-start = (f32[64,128]{1,0:T(8,128)S(1)}, f32[64,128]{1,0:T(8,128)S(1)}, u32[]{:S(2)}, u32[]{:S(2)}) collective-permute-start(f32[64,128]{1,0:T(8,128)S(1)} %copy-done.6), channel_id=1, source_target_pairs={{0,1},{1,0},{2,3},{3,2},{4,5},{5,4},{6,7},{7,6},{8,9},{9,8},{10,11... | collective-permute-start | bytes 98312 | tf_op jit(solution)/shard_map/ppermute | solution.py:26
  32.1 5.8 %collective-permute-start.2 = (f32[64,128]{1,0:T(8,128)S(1)}, f32[64,128]{1,0:T(8,128)S(1)}, u32[]{:S(2)}, u32[]{:S(2)}) collective-permute-start(f32[64,128]{1,0:T(8,128)S(1)} %maximum_select_fusion.6), channel_id=1, source_target_pairs={{0,2},{1,3},{2,0},{3,1},{4,6},{5,7},{6,4},{7,5},{8,10},{9,11},{10,... | collective-permute-start | bytes 98312 | tf_op jit(solution)/shard_map/ppermute | solution.py:26
  38.2 3.3 %collective-permute-start.3 = (f32[3,128,128]{2,1,0:T(8,128)S(1)}, f32[3,128,128]{2,1,0:T(8,128)S(1)}, u32[]{:S(2)}, u32[]{:S(2)}) collective-permute-start(f32[3,128,128]{2,1,0:T(8,128)S(1)} %pad_maximum_fusion.1), channel_id=1, source_target_pairs={{0,1},{1,0},{2,3},{3,2},{4,5},{5,4},{6,7},{7,6},{8,9},{9,8},{10,11... | collective-permute-start | bytes 589832 | tf_op jit(solution)/shard_map/ppermute | solution.py:26
  42.2 13.3 %collective-permute-start.4 = (f32[2,128,128]{2,1,0:T(8,128)S(1)}, f32[2,128,128]{2,1,0:T(8,128)S(1)}, u32[]{:S(2)}, u32[]{:S(2)}) collective-permute-start(f32[2,128,128]{2,1,0:T(8,128)S(1)} %slice.660), channel_id=1, source_target_pairs={{0,2},{1,3},{2,0},{3,1},{4,6},{5,7},{6,4},{7,5},{8,10},{9,11},{10,... | collective-permute-start | bytes 393224 | tf_op jit(solution)/shard_map/ppermute | solution.py:26
  44.1 22.5 %collective-permute-start.8 = (f32[655,128]{1,0:T(8,128)S(1)}, f32[655,128]{1,0:T(8,128)S(1)}, u32[]{:S(2)}, u32[]{:S(2)}) collective-permute-start(f32[655,128]{1,0:T(8,128)S(1)} %collective-permute-done.6), channel_id=1, source_target_pairs={{0,1},{1,2},{2,3},{3,4},{4,5},{5,6},{6,7},{7,8},{8,9},{9,10},{10,1... | collective-permute-start | bytes 1006088 | tf_op jit(solution)/shard_map/ppermute | solution.py:32
  46.2 17.2 %collective-permute-start.9 = (f32[655,128]{1,0:T(8,128)S(1)}, f32[655,128]{1,0:T(8,128)S(1)}, u32[]{:S(2)}, u32[]{:S(2)}) collective-permute-start(f32[655,128]{1,0:T(8,128)S(1)} %collective-permute-done.7), channel_id=1, source_target_pairs={{1,0},{2,1},{3,2},{4,3},{5,4},{6,5},{7,6},{8,7},{9,8},{10,9},{11,1... | collective-permute-start | bytes 1006088 | tf_op jit(solution)/shard_map/ppermute | solution.py:32
  56.2 7.0 %collective-permute-start.5 = (f32[128,128]{1,0:T(8,128)S(1)}, f32[128,128]{1,0:T(8,128)S(1)}, u32[]{:S(2)}, u32[]{:S(2)}) collective-permute-start(f32[128,128]{1,0:T(8,128)S(1)} %get-tuple-element.98), channel_id=1, source_target_pairs={{0,4},{1,5},{2,6},{3,7},{4,0},{5,1},{6,2},{7,3},{8,12},{9,13},{10,... | collective-permute-start | bytes 196616 | tf_op jit(solution)/shard_map/ppermute | solution.py:26
  63.4 6.8 %copy-start.9 = (f32[655,128]{1,0:T(8,128)}, f32[655,128]{1,0:T(8,128)S(1)}, u32[]{:S(2)}) copy-start(f32[655,128]{1,0:T(8,128)S(1)} %collective-permute-done.9) | copy-start | bytes 1006084
  63.4 8.3 %collective-permute-start.11 = (f32[655,128]{1,0:T(8,128)S(1)}, f32[655,128]{1,0:T(8,128)S(1)}, u32[]{:S(2)}, u32[]{:S(2)}) collective-permute-start(f32[655,128]{1,0:T(8,128)S(1)} %collective-permute-done.9), channel_id=1, source_target_pairs={{1,0},{2,1},{3,2},{4,3},{5,4},{6,5},{7,6},{8,7},{9,8},{10,9},{11,1... | collective-permute-start | bytes 1006088 | tf_op jit(solution)/shard_map/ppermute | solution.py:32
  66.7 3.5 %copy-start.10 = (f32[655,128]{1,0:T(8,128)}, f32[655,128]{1,0:T(8,128)S(1)}, u32[]{:S(2)}) copy-start(f32[655,128]{1,0:T(8,128)S(1)} %collective-permute-done.8) | copy-start | bytes 1006084
  66.7 13.0 %collective-permute-start.10 = (f32[655,128]{1,0:T(8,128)S(1)}, f32[655,128]{1,0:T(8,128)S(1)}, u32[]{:S(2)}, u32[]{:S(2)}) collective-permute-start(f32[655,128]{1,0:T(8,128)S(1)} %collective-permute-done.8), channel_id=1, source_target_pairs={{0,1},{1,2},{2,3},{3,4},{4,5},{5,6},{6,7},{7,8},{8,9},{9,10},{10,1... | collective-permute-start | bytes 1006088 | tf_op jit(solution)/shard_map/ppermute | solution.py:32
  71.7 11.3 %copy-start.11 = (f32[655,128]{1,0:T(8,128)}, f32[655,128]{1,0:T(8,128)S(1)}, u32[]{:S(2)}) copy-start(f32[655,128]{1,0:T(8,128)S(1)} %collective-permute-done.11) | copy-start | bytes 1006084
  71.8 12.9 %collective-permute-start.13 = (f32[655,128]{1,0:T(8,128)S(1)}, f32[655,128]{1,0:T(8,128)S(1)}, u32[]{:S(2)}, u32[]{:S(2)}) collective-permute-start(f32[655,128]{1,0:T(8,128)S(1)} %collective-permute-done.11), channel_id=1, source_target_pairs={{1,0},{2,1},{3,2},{4,3},{5,4},{6,5},{7,6},{8,7},{9,8},{10,9},{11,1... | collective-permute-start | bytes 1006088 | tf_op jit(solution)/shard_map/ppermute | solution.py:32
  79.6 3.4 %copy-start.12 = (f32[655,128]{1,0:T(8,128)}, f32[655,128]{1,0:T(8,128)S(1)}, u32[]{:S(2)}) copy-start(f32[655,128]{1,0:T(8,128)S(1)} %collective-permute-done.10) | copy-start | bytes 1006084
  79.7 12.9 %collective-permute-start.12 = (f32[655,128]{1,0:T(8,128)S(1)}, f32[655,128]{1,0:T(8,128)S(1)}, u32[]{:S(2)}, u32[]{:S(2)}) collective-permute-start(f32[655,128]{1,0:T(8,128)S(1)} %collective-permute-done.10), channel_id=1, source_target_pairs={{0,1},{1,2},{2,3},{3,4},{4,5},{5,6},{6,7},{7,8},{8,9},{9,10},{10,1... | collective-permute-start | bytes 1006088 | tf_op jit(solution)/shard_map/ppermute | solution.py:32
  84.6 13.1 %collective-permute-start.15 = (f32[655,128]{1,0:T(8,128)S(1)}, f32[655,128]{1,0:T(8,128)S(1)}, u32[]{:S(2)}, u32[]{:S(2)}) collective-permute-start(f32[655,128]{1,0:T(8,128)S(1)} %collective-permute-done.13), channel_id=1, source_target_pairs={{1,0},{2,1},{3,2},{4,3},{5,4},{6,5},{7,6},{8,7},{9,8},{10,9},{11,1... | collective-permute-start | bytes 1006088 | tf_op jit(solution)/shard_map/ppermute | solution.py:32
  92.5 3.6 %copy-start.14 = (f32[655,128]{1,0:T(8,128)}, f32[655,128]{1,0:T(8,128)S(1)}, u32[]{:S(2)}) copy-start(f32[655,128]{1,0:T(8,128)S(1)} %collective-permute-done.12) | copy-start | bytes 1006084
  92.5 13.1 %collective-permute-start.14 = (f32[655,128]{1,0:T(8,128)S(1)}, f32[655,128]{1,0:T(8,128)S(1)}, u32[]{:S(2)}, u32[]{:S(2)}) collective-permute-start(f32[655,128]{1,0:T(8,128)S(1)} %collective-permute-done.12), channel_id=1, source_target_pairs={{0,1},{1,2},{2,3},{3,4},{4,5},{5,6},{6,7},{7,8},{8,9},{9,10},{10,1... | collective-permute-start | bytes 1006088 | tf_op jit(solution)/shard_map/ppermute | solution.py:32
  97.7 11.3 %copy-start.13 = (f32[655,128]{1,0:T(8,128)}, f32[655,128]{1,0:T(8,128)S(1)}, u32[]{:S(2)}) copy-start(f32[655,128]{1,0:T(8,128)S(1)} %collective-permute-done.15) | copy-start | bytes 1006084
  97.7 13.0 %collective-permute-start.17 = (f32[655,128]{1,0:T(8,128)S(1)}, f32[655,128]{1,0:T(8,128)S(1)}, u32[]{:S(2)}, u32[]{:S(2)}) collective-permute-start(f32[655,128]{1,0:T(8,128)S(1)} %collective-permute-done.15), channel_id=1, source_target_pairs={{1,0},{2,1},{3,2},{4,3},{5,4},{6,5},{7,6},{8,7},{9,8},{10,9},{11,1... | collective-permute-start | bytes 1006088 | tf_op jit(solution)/shard_map/ppermute | solution.py:32
  105.6 3.5 %copy-start.16 = (f32[655,128]{1,0:T(8,128)}, f32[655,128]{1,0:T(8,128)S(1)}, u32[]{:S(2)}) copy-start(f32[655,128]{1,0:T(8,128)S(1)} %collective-permute-done.14) | copy-start | bytes 1006084
  105.6 13.0 %collective-permute-start.16 = (f32[655,128]{1,0:T(8,128)S(1)}, f32[655,128]{1,0:T(8,128)S(1)}, u32[]{:S(2)}, u32[]{:S(2)}) collective-permute-start(f32[655,128]{1,0:T(8,128)S(1)} %collective-permute-done.14), channel_id=1, source_target_pairs={{0,1},{1,2},{2,3},{3,4},{4,5},{5,6},{6,7},{7,8},{8,9},{9,10},{10,1... | collective-permute-start | bytes 1006088 | tf_op jit(solution)/shard_map/ppermute | solution.py:32
  110.7 11.3 %copy-start.15 = (f32[655,128]{1,0:T(8,128)}, f32[655,128]{1,0:T(8,128)S(1)}, u32[]{:S(2)}) copy-start(f32[655,128]{1,0:T(8,128)S(1)} %collective-permute-done.17) | copy-start | bytes 1006084
  110.7 12.8 %collective-permute-start.19 = (f32[655,128]{1,0:T(8,128)S(1)}, f32[655,128]{1,0:T(8,128)S(1)}, u32[]{:S(2)}, u32[]{:S(2)}) collective-permute-start(f32[655,128]{1,0:T(8,128)S(1)} %collective-permute-done.17), channel_id=1, source_target_pairs={{1,0},{2,1},{3,2},{4,3},{5,4},{6,5},{7,6},{8,7},{9,8},{10,9},{11,1... | collective-permute-start | bytes 1006088 | tf_op jit(solution)/shard_map/ppermute | solution.py:32
  118.6 3.4 %copy-start.18 = (f32[655,128]{1,0:T(8,128)}, f32[655,128]{1,0:T(8,128)S(1)}, u32[]{:S(2)}) copy-start(f32[655,128]{1,0:T(8,128)S(1)} %collective-permute-done.16) | copy-start | bytes 1006084
  118.6 12.8 %collective-permute-start.18 = (f32[655,128]{1,0:T(8,128)S(1)}, f32[655,128]{1,0:T(8,128)S(1)}, u32[]{:S(2)}, u32[]{:S(2)}) collective-permute-start(f32[655,128]{1,0:T(8,128)S(1)} %collective-permute-done.16), channel_id=1, source_target_pairs={{0,1},{1,2},{2,3},{3,4},{4,5},{5,6},{6,7},{7,8},{8,9},{9,10},{10,1... | collective-permute-start | bytes 1006088 | tf_op jit(solution)/shard_map/ppermute | solution.py:32
  123.6 11.4 %copy-start.17 = (f32[655,128]{1,0:T(8,128)}, f32[655,128]{1,0:T(8,128)S(1)}, u32[]{:S(2)}) copy-start(f32[655,128]{1,0:T(8,128)S(1)} %collective-permute-done.19) | copy-start | bytes 1006084
  123.6 13.0 %collective-permute-start.21 = (f32[655,128]{1,0:T(8,128)S(1)}, f32[655,128]{1,0:T(8,128)S(1)}, u32[]{:S(2)}, u32[]{:S(2)}) collective-permute-start(f32[655,128]{1,0:T(8,128)S(1)} %collective-permute-done.19), channel_id=1, source_target_pairs={{1,0},{2,1},{3,2},{4,3},{5,4},{6,5},{7,6},{8,7},{9,8},{10,9},{11,1... | collective-permute-start | bytes 1006088 | tf_op jit(solution)/shard_map/ppermute | solution.py:32
  131.5 3.5 %copy-start.20 = (f32[655,128]{1,0:T(8,128)}, f32[655,128]{1,0:T(8,128)S(1)}, u32[]{:S(2)}) copy-start(f32[655,128]{1,0:T(8,128)S(1)} %collective-permute-done.18) | copy-start | bytes 1006084
  131.5 12.7 %collective-permute-start.20 = (f32[655,128]{1,0:T(8,128)S(1)}, f32[655,128]{1,0:T(8,128)S(1)}, u32[]{:S(2)}, u32[]{:S(2)}) collective-permute-start(f32[655,128]{1,0:T(8,128)S(1)} %collective-permute-done.18), channel_id=1, source_target_pairs={{0,1},{1,2},{2,3},{3,4},{4,5},{5,6},{6,7},{7,8},{8,9},{9,10},{10,1... | collective-permute-start | bytes 1006088 | tf_op jit(solution)/shard_map/ppermute | solution.py:32
  136.6 9.1 %copy-start.19 = (f32[655,128]{1,0:T(8,128)}, f32[655,128]{1,0:T(8,128)S(1)}, u32[]{:S(2)}) copy-start(f32[655,128]{1,0:T(8,128)S(1)} %collective-permute-done.21) | copy-start | bytes 1006084
  144.2 1.5 copy-start.21
  246.5 1.0 copy-start.3
  246.6 1.5 copy-start.2

commit v6 on v5

--- a/solution.py
+++ b/solution.py
@@ -173,7 +173,7 @@
     slots = jnp.clip(slot_of(chosen - cluster), 0, stacked.shape[0] - 1)
     values = jnp.take(stacked, slots, axis=0)
     return batched_far(own_coords, coords, values, entries >= 0) + jnp.dot(
-        transfer, above, precision=HIGHEST
+        transfer, above, precision=lax.Precision.HIGH
     )
 
 
@@ -393,7 +393,7 @@
     leaf_blocks = jnp.take(leaf_rim, positions, axis=0)
     local_leaf = batched_far(
         skel_leaf[0], leaf_blocks[:, rank:], leaf_blocks[:, :rank], leaf_entries >= 0
-    ) + jnp.dot(transfer_leaf[0], local_pair, precision=HIGHEST)
+    ) + jnp.dot(transfer_leaf[0], local_pair, precision=lax.Precision.HIGH)
     product = near_field + jnp.dot(leaf_basis[0], local_leaf, precision=lax.Precision.HIGH)
     return product[None]
 

time: 257 us -> 257 us (level)
  no operation moved by 1% of the time
where the time goes in v6:
time: 257 us; the launch traced here: 252 us
  starting transfers between devices  91.2 us (35%)
  Pallas kernels  69.7 us (27%)
  matrix products  32.3 us (13%)
  local copies, waits for them, and re-layouts  22.6 us (9%)
  waiting for transfers between devices  16.2 us (6%)
  blocking collectives  14.5 us (6%)
  other arithmetic  4.61 us (2%)
    ppermute x16, starting transfers between devices, from_behind(): return lax.ppermute(block, axis, route)  79.2 us
    pallas_call x1, Pallas kernels, exchange(): pl.pallas_call(functools.partial(exchange_kernel, clusters), out_shape=(j...  69.7 us
    dot_general x17, matrix products, contribution(): jnp.dot(kernel_block(own_points, coords), block[:leaf_points], precision=...  26 us
    all_gather x1, blocking collectives, per_device(): local_top = lax.all_gather(top_cols, MEMBERS, axis=1, tiled=True)  14.5 us
    unnamed x75, local copies, waits for them, and re-layouts  12.5 us
    ppermute x6, starting transfers between devices, from_partner(): return lax.ppermute(value, axis, pairs)  12 us
    ppermute x6, waiting for transfers between devices, from_partner(): return lax.ppermute(value, axis, pairs)  8.61 us
    ppermute x16, waiting for transfers between devices, from_behind(): return lax.ppermute(block, axis, route)  7.59 us
  transfers between devices with their start and end apart: 22, of which 4 were waited for; matrix products, arithmetic and copies ran while one was open for 12% of the time, Pallas kernels for 0%

profile of v6, /device:TPU:24, one launch (start us, length us, event | category | flops | bytes accessed | tf_op | source)
XLA Modules:
  0.0 252.4 jit_solution(6733663940036780900)
XLA Ops:
  1.7 1.6 fusion.407
  3.3 1.0 pad_maximum_fusion
  4.3 1.9 collective-permute-start.6
  6.2 13.2 %collective-permute-start.7 = (f32[655,128]{1,0:T(8,128)S(1)}, f32[655,128]{1,0:T(8,128)S(1)}, u32[]{:S(2)}, u32[]{:S(2)}) collective-permute-start(f32[655,128]{1,0:T(8,128)S(1)} %pad_maximum_fusion), channel_id=1, source_target_pairs={{1,0},{2,1},{3,2},{4,3},{5,4},{6,5},{7,6},{8,7},{9,8},{10,9},{11,1... | collective-permute-start | bytes 1006088 | tf_op jit(solution)/shard_map/ppermute | solution.py:32
  19.5 1.9 collective-permute-start.1
  21.4 2.4 collective-permute-start
  26.9 1.6 gather_fusion.1
  28.6 1.0 compare_reduce_fusion.8
  29.6 1.6 convolution_select_fusion.16
  32.1 1.9 collective-permute-start.2
  34.3 3.6 %collective-permute-done.2 = f32[64,128]{1,0:T(8,128)S(1)} collective-permute-done((f32[64,128]{1,0:T(8,128)S(1)}, f32[64,128]{1,0:T(8,128)S(1)}, u32[]{:S(2)}, u32[]{:S(2)}) %collective-permute-start.2) | collective-permute-done | bytes 32800 | tf_op jit(solution)/shard_map/ppermute | solution.py:26
  38.2 1.9 collective-permute-start.3
  40.1 1.4 collective-permute-done.3
  42.2 1.9 collective-permute-start.4
  44.1 2.0 collective-permute-start.8
  46.2 7.7 %collective-permute-start.9 = (f32[655,128]{1,0:T(8,128)S(1)}, f32[655,128]{1,0:T(8,128)S(1)}, u32[]{:S(2)}, u32[]{:S(2)}) collective-permute-start(f32[655,128]{1,0:T(8,128)S(1)} %collective-permute-done.7), channel_id=1, source_target_pairs={{1,0},{2,1},{3,2},{4,3},{5,4},{6,5},{7,6},{8,7},{9,8},{10,9},{11,1... | collective-permute-start | bytes 1006088 | tf_op jit(solution)/shard_map/ppermute | solution.py:32
  54.0 1.6 fusion.17
  56.2 1.9 collective-permute-start.5
  58.1 1.5 fusion.16
  59.6 3.6 %collective-permute-done.5 = f32[128,128]{1,0:T(8,128)S(1)} collective-permute-done((f32[128,128]{1,0:T(8,128)S(1)}, f32[128,128]{1,0:T(8,128)S(1)}, u32[]{:S(2)}, u32[]{:S(2)}) %collective-permute-start.5) | collective-permute-done | bytes 65568 | tf_op jit(solution)/shard_map/ppermute | solution.py:26
  63.4 3.2 %collective-permute-start.11 = (f32[655,128]{1,0:T(8,128)S(1)}, f32[655,128]{1,0:T(8,128)S(1)}, u32[]{:S(2)}, u32[]{:S(2)}) collective-permute-start(f32[655,128]{1,0:T(8,128)S(1)} %collective-permute-done.9), channel_id=1, source_target_pairs={{1,0},{2,1},{3,2},{4,3},{5,4},{6,5},{7,6},{8,7},{9,8},{10,9},{11,1... | collective-permute-start | bytes 1006088 | tf_op jit(solution)/shard_map/ppermute | solution.py:32
  66.7 1.9 collective-permute-start.10
  68.6 1.5 convolution_select_fusion.12
  70.2 1.5 fusion.15
  71.8 7.9 %collective-permute-start.13 = (f32[655,128]{1,0:T(8,128)S(1)}, f32[655,128]{1,0:T(8,128)S(1)}, u32[]{:S(2)}, u32[]{:S(2)}) collective-permute-start(f32[655,128]{1,0:T(8,128)S(1)} %collective-permute-done.11), channel_id=1, source_target_pairs={{1,0},{2,1},{3,2},{4,3},{5,4},{6,5},{7,6},{8,7},{9,8},{10,9},{11,1... | collective-permute-start | bytes 1006088 | tf_op jit(solution)/shard_map/ppermute | solution.py:32
  79.7 1.9 collective-permute-start.12
  81.6 1.5 convolution_select_fusion.10
  83.1 1.5 fusion.13
  84.6 7.9 %collective-permute-start.15 = (f32[655,128]{1,0:T(8,128)S(1)}, f32[655,128]{1,0:T(8,128)S(1)}, u32[]{:S(2)}, u32[]{:S(2)}) collective-permute-start(f32[655,128]{1,0:T(8,128)S(1)} %collective-permute-done.13), channel_id=1, source_target_pairs={{1,0},{2,1},{3,2},{4,3},{5,4},{6,5},{7,6},{8,7},{9,8},{10,9},{11,1... | collective-permute-start | bytes 1006088 | tf_op jit(solution)/shard_map/ppermute | solution.py:32
  92.5 2.1 collective-permute-start.14
  94.7 1.5 convolution_select_fusion.8
  96.2 1.6 fusion.11
  97.7 7.9 %collective-permute-start.17 = (f32[655,128]{1,0:T(8,128)S(1)}, f32[655,128]{1,0:T(8,128)S(1)}, u32[]{:S(2)}, u32[]{:S(2)}) collective-permute-start(f32[655,128]{1,0:T(8,128)S(1)} %collective-permute-done.15), channel_id=1, source_target_pairs={{1,0},{2,1},{3,2},{4,3},{5,4},{6,5},{7,6},{8,7},{9,8},{10,9},{11,1... | collective-permute-start | bytes 1006088 | tf_op jit(solution)/shard_map/ppermute | solution.py:32
  105.6 1.9 collective-permute-start.16
  107.6 1.5 convolution_select_fusion.6
  109.1 1.6 fusion.9
  110.7 7.9 %collective-permute-start.19 = (f32[655,128]{1,0:T(8,128)S(1)}, f32[655,128]{1,0:T(8,128)S(1)}, u32[]{:S(2)}, u32[]{:S(2)}) collective-permute-start(f32[655,128]{1,0:T(8,128)S(1)} %collective-permute-done.17), channel_id=1, source_target_pairs={{1,0},{2,1},{3,2},{4,3},{5,4},{6,5},{7,6},{8,7},{9,8},{10,9},{11,1... | collective-permute-start | bytes 1006088 | tf_op jit(solution)/shard_map/ppermute | solution.py:32
  118.6 1.9 collective-permute-start.18
  120.6 1.5 convolution_select_fusion.4
  122.1 1.5 fusion.7
  123.6 7.9 %collective-permute-start.21 = (f32[655,128]{1,0:T(8,128)S(1)}, f32[655,128]{1,0:T(8,128)S(1)}, u32[]{:S(2)}, u32[]{:S(2)}) collective-permute-start(f32[655,128]{1,0:T(8,128)S(1)} %collective-permute-done.19), channel_id=1, source_target_pairs={{1,0},{2,1},{3,2},{4,3},{5,4},{6,5},{7,6},{8,7},{9,8},{10,9},{11,1... | collective-permute-start | bytes 1006088 | tf_op jit(solution)/shard_map/ppermute | solution.py:32
  131.5 1.9 collective-permute-start.20
  133.4 1.5 convolution_select_fusion.2
  135.0 1.6 fusion.5
  136.6 7.5 %collective-permute-done.20 = f32[655,128]{1,0:T(8,128)S(1)} collective-permute-done((f32[655,128]{1,0:T(8,128)S(1)}, f32[655,128]{1,0:T(8,128)S(1)}, u32[]{:S(2)}, u32[]{:S(2)}) %collective-permute-start.20) | collective-permute-done | bytes 335392 | tf_op jit(solution)/shard_map/ppermute | solution.py:32
  144.2 1.5 convolution_select_fusion
  145.7 1.6 fusion.3
  148.0 69.7 %shard_map.145 = (f32[64,16,128]{2,1,0:T(8,128)}, f32[8,128,128]{2,1,0:T(8,128)}, f32[8,128,128]{2,1,0:T(8,128)}) custom-call(f32[16,128]{1,0:T(8,128)} %copy.36.top_ref, f32[128,128]{1,0:T(8,128)} %slice_bitcast_fusion.17.pair_ref, f32[128,128]{1,0:T(8,128)} %get-tuple-element.97.quad_ref), custom_call_target="tpu_custom_call" | custom-call | tf_op jit(solution)/shard_map/pallas_call | solution.py:309
  217.6 1.6 gather_fusion.4
  219.8 14.5 %all_gather.3 = f32[128,128]{0,1:T(8,128)S(1)} all-gather(f32[128,16]{0,1:T(8,128)S(1)} %fusion.206), channel_id=1, replica_groups=mesh['cl'=64,'q'=2,'p'=2,'c'=2] {'q','p','c'}, dimensions={1}, use_global_device_ids=true | all-gather | bytes 73728 | tf_op jit(solution)/shard_map/all_gather | solution.py:388
  234.3 0.9 fusion.456
  235.2 0.9 fusion.455
  236.1 0.9 fusion.454
  237.0 0.9 fusion.453
  237.8 0.9 fusion.452
  238.7 0.9 fusion.451
  239.6 0.9 fusion.450
  240.6 0.9 fusion.447
  241.5 0.9 fusion.446
  242.4 0.9 fusion.444
  243.2 0.9 fusion.443
  244.1 0.9 fusion.442
  245.0 0.9 fusion.441
  251.4 1.0 fusion.1
  (161 shorter events, 14.3 us)
Async XLA Ops:
  0.0 1.7 copy-start
  0.0 25.0 %copy-start.26 = (f32[1,3,128]{2,0,1:T(1,128)S(1)}, f32[1,3,128]{2,0,1:T(1,128)}, u32[]{:S(2)}) copy-start(f32[1,3,128]{2,0,1:T(1,128)} %param.23) | copy-start | bytes 4612
  0.0 23.8 %copy-start.8 = (f32[1,3,512]{2,0,1:T(1,128)S(1)}, f32[1,3,512]{2,0,1:T(1,128)}, u32[]{:S(2)}) copy-start(f32[1,3,512]{2,0,1:T(1,128)} %param.18) | copy-start | bytes 18436
  0.0 19.4 %copy-start.22 = (f32[32,128]{1,0:T(8,128)S(1)}, f32[32,128]{1,0:T(8,128)}, u32[]{:S(2)}) copy-start(f32[32,128]{1,0:T(8,128)} %param.22) | copy-start | bytes 49156
  0.0 21.4 %copy-start.6 = (f32[64,128]{1,0:T(8,128)S(1)}, f32[64,128]{1,0:T(8,128)}, u32[]{:S(2)}) copy-start(f32[64,128]{1,0:T(8,128)} %param.21) | copy-start | bytes 98308
  0.0 23.8 %copy-start.23 = (s32[128,8]{0,1:T(8,128)S(1)}, s32[128,8]{0,1:T(8,128)}, u32[]{:S(2)}) copy-start(s32[128,8]{0,1:T(8,128)} %param.30) | copy-start | bytes 12292
  0.0 23.8 %copy-start.24 = (s32[64,8]{0,1:T(8,128)S(1)}, s32[64,8]{0,1:T(8,128)}, u32[]{:S(2)}) copy-start(s32[64,8]{0,1:T(8,128)} %param.31) | copy-start | bytes 6148
  0.1 24.3 %copy-start.25 = (s32[256,8]{0,1:T(8,128)S(1)}, s32[256,8]{0,1:T(8,128)}, u32[]{:S(2)}) copy-start(s32[256,8]{0,1:T(8,128)} %param.29) | copy-start | bytes 24580
  0.1 24.6 %copy-start.27 = (s32[1,8]{1,0:T(1,128)S(1)}, s32[1,8]{1,0:T(1,128)}, u32[]{:S(2)}) copy-start(s32[1,8]{1,0:T(1,128)} %param.28) | copy-start | bytes 100
  0.1 25.0 %copy-start.4 = (f32[1,128,128]{2,1,0:T(8,128)S(1)}, f32[1,128,128]{2,1,0:T(8,128)}, u32[]{:S(2)}) copy-start(f32[1,128,128]{2,1,0:T(8,128)} %param.20) | copy-start | bytes 196612
  0.1 25.3 %copy-start.7 = (f32[128,3,128]{2,0,1:T(8,128)S(1)}, f32[128,3,128]{2,0,1:T(8,128)}, u32[]{:S(2)}) copy-start(f32[128,3,128]{2,0,1:T(8,128)} %param.25) | copy-start | bytes 589828
  0.1 26.0 %copy-start.5 = (f32[64,3,128]{2,0,1:T(8,128)S(1)}, f32[64,3,128]{2,0,1:T(8,128)}, u32[]{:S(2)}) copy-start(f32[64,3,128]{2,0,1:T(8,128)} %param.26) | copy-start | bytes 294916
  1.7 26.9 %copy-start.28 = (s32[1,16]{1,0:T(1,128)S(1)}, s32[1,16]{1,0:T(1,128)}, u32[]{:S(2)}) copy-start(s32[1,16]{1,0:T(1,128)} %param.27) | copy-start | bytes 196
  1.7 27.9 %copy-start.1 = (f32[1,512,128]{2,1,0:T(8,128)S(1)}, f32[1,512,128]{2,1,0:T(8,128)}, u32[]{:S(2)}) copy-start(f32[1,512,128]{2,1,0:T(8,128)} %param.17) | copy-start | bytes 786436
  4.3 39.8 %collective-permute-start.6 = (f32[655,128]{1,0:T(8,128)S(1)}, f32[655,128]{1,0:T(8,128)S(1)}, u32[]{:S(2)}, u32[]{:S(2)}) collective-permute-start(f32[655,128]{1,0:T(8,128)S(1)} %pad_maximum_fusion), channel_id=1, source_target_pairs={{0,1},{1,2},{2,3},{3,4},{4,5},{5,6},{6,7},{7,8},{8,9},{9,10},{10,1... | collective-permute-start | bytes 1006088 | tf_op jit(solution)/shard_map/ppermute | solution.py:32
  6.2 40.0 %collective-permute-start.7 = (f32[655,128]{1,0:T(8,128)S(1)}, f32[655,128]{1,0:T(8,128)S(1)}, u32[]{:S(2)}, u32[]{:S(2)}) collective-permute-start(f32[655,128]{1,0:T(8,128)S(1)} %pad_maximum_fusion), channel_id=1, source_target_pairs={{1,0},{2,1},{3,2},{4,3},{5,4},{6,5},{7,6},{8,7},{9,8},{10,9},{11,1... | collective-permute-start | bytes 1006088 | tf_op jit(solution)/shard_map/ppermute | solution.py:32
  19.5 12.6 %collective-permute-start.1 = (f32[32,128]{1,0:T(8,128)S(1)}, f32[32,128]{1,0:T(8,128)S(1)}, u32[]{:S(2)}, u32[]{:S(2)}) collective-permute-start(f32[32,128]{1,0:T(8,128)S(1)} %copy-done.22), channel_id=1, source_target_pairs={{0,1},{1,0},{2,3},{3,2},{4,5},{5,4},{6,7},{7,6},{8,9},{9,8},{10,11... | collective-permute-start | bytes 49160 | tf_op jit(solution)/shard_map/ppermute | solution.py:26
  21.4 12.6 %collective-permute-start = (f32[64,128]{1,0:T(8,128)S(1)}, f32[64,128]{1,0:T(8,128)S(1)}, u32[]{:S(2)}, u32[]{:S(2)}) collective-permute-start(f32[64,128]{1,0:T(8,128)S(1)} %copy-done.6), channel_id=1, source_target_pairs={{0,1},{1,0},{2,3},{3,2},{4,5},{5,4},{6,7},{7,6},{8,9},{9,8},{10,11... | collective-permute-start | bytes 98312 | tf_op jit(solution)/shard_map/ppermute | solution.py:26
  32.1 5.8 %collective-permute-start.2 = (f32[64,128]{1,0:T(8,128)S(1)}, f32[64,128]{1,0:T(8,128)S(1)}, u32[]{:S(2)}, u32[]{:S(2)}) collective-permute-start(f32[64,128]{1,0:T(8,128)S(1)} %maximum_select_fusion.6), channel_id=1, source_target_pairs={{0,2},{1,3},{2,0},{3,1},{4,6},{5,7},{6,4},{7,5},{8,10},{9,11},{10,... | collective-permute-start | bytes 98312 | tf_op jit(solution)/shard_map/ppermute | solution.py:26
  38.2 3.3 %collective-permute-start.3 = (f32[3,128,128]{2,1,0:T(8,128)S(1)}, f32[3,128,128]{2,1,0:T(8,128)S(1)}, u32[]{:S(2)}, u32[]{:S(2)}) collective-permute-start(f32[3,128,128]{2,1,0:T(8,128)S(1)} %pad_maximum_fusion.1), channel_id=1, source_target_pairs={{0,1},{1,0},{2,3},{3,2},{4,5},{5,4},{6,7},{7,6},{8,9},{9,8},{10,11... | collective-permute-start | bytes 589832 | tf_op jit(solution)/shard_map/ppermute | solution.py:26
  42.2 13.3 %collective-permute-start.4 = (f32[2,128,128]{2,1,0:T(8,128)S(1)}, f32[2,128,128]{2,1,0:T(8,128)S(1)}, u32[]{:S(2)}, u32[]{:S(2)}) collective-permute-start(f32[2,128,128]{2,1,0:T(8,128)S(1)} %slice.660), channel_id=1, source_target_pairs={{0,2},{1,3},{2,0},{3,1},{4,6},{5,7},{6,4},{7,5},{8,10},{9,11},{10,... | collective-permute-start | bytes 393224 | tf_op jit(solution)/shard_map/ppermute | solution.py:26
  44.1 22.5 %collective-permute-start.8 = (f32[655,128]{1,0:T(8,128)S(1)}, f32[655,128]{1,0:T(8,128)S(1)}, u32[]{:S(2)}, u32[]{:S(2)}) collective-permute-start(f32[655,128]{1,0:T(8,128)S(1)} %collective-permute-done.6), channel_id=1, source_target_pairs={{0,1},{1,2},{2,3},{3,4},{4,5},{5,6},{6,7},{7,8},{8,9},{9,10},{10,1... | collective-permute-start | bytes 1006088 | tf_op jit(solution)/shard_map/ppermute | solution.py:32
  46.2 17.2 %collective-permute-start.9 = (f32[655,128]{1,0:T(8,128)S(1)}, f32[655,128]{1,0:T(8,128)S(1)}, u32[]{:S(2)}, u32[]{:S(2)}) collective-permute-start(f32[655,128]{1,0:T(8,128)S(1)} %collective-permute-done.7), channel_id=1, source_target_pairs={{1,0},{2,1},{3,2},{4,3},{5,4},{6,5},{7,6},{8,7},{9,8},{10,9},{11,1... | collective-permute-start | bytes 1006088 | tf_op jit(solution)/shard_map/ppermute | solution.py:32
  56.2 7.0 %collective-permute-start.5 = (f32[128,128]{1,0:T(8,128)S(1)}, f32[128,128]{1,0:T(8,128)S(1)}, u32[]{:S(2)}, u32[]{:S(2)}) collective-permute-start(f32[128,128]{1,0:T(8,128)S(1)} %get-tuple-element.98), channel_id=1, source_target_pairs={{0,4},{1,5},{2,6},{3,7},{4,0},{5,1},{6,2},{7,3},{8,12},{9,13},{10,... | collective-permute-start | bytes 196616 | tf_op jit(solution)/shard_map/ppermute | solution.py:26
  63.4 6.8 %copy-start.9 = (f32[655,128]{1,0:T(8,128)}, f32[655,128]{1,0:T(8,128)S(1)}, u32[]{:S(2)}) copy-start(f32[655,128]{1,0:T(8,128)S(1)} %collective-permute-done.9) | copy-start | bytes 1006084
  63.4 8.3 %collective-permute-start.11 = (f32[655,128]{1,0:T(8,128)S(1)}, f32[655,128]{1,0:T(8,128)S(1)}, u32[]{:S(2)}, u32[]{:S(2)}) collective-permute-start(f32[655,128]{1,0:T(8,128)S(1)} %collective-permute-done.9), channel_id=1, source_target_pairs={{1,0},{2,1},{3,2},{4,3},{5,4},{6,5},{7,6},{8,7},{9,8},{10,9},{11,1... | collective-permute-start | bytes 1006088 | tf_op jit(solution)/shard_map/ppermute | solution.py:32
  66.7 3.5 %copy-start.10 = (f32[655,128]{1,0:T(8,128)}, f32[655,128]{1,0:T(8,128)S(1)}, u32[]{:S(2)}) copy-start(f32[655,128]{1,0:T(8,128)S(1)} %collective-permute-done.8) | copy-start | bytes 1006084
  66.7 13.0 %collective-permute-start.10 = (f32[655,128]{1,0:T(8,128)S(1)}, f32[655,128]{1,0:T(8,128)S(1)}, u32[]{:S(2)}, u32[]{:S(2)}) collective-permute-start(f32[655,128]{1,0:T(8,128)S(1)} %collective-permute-done.8), channel_id=1, source_target_pairs={{0,1},{1,2},{2,3},{3,4},{4,5},{5,6},{6,7},{7,8},{8,9},{9,10},{10,1... | collective-permute-start | bytes 1006088 | tf_op jit(solution)/shard_map/ppermute | solution.py:32
  71.7 11.3 %copy-start.11 = (f32[655,128]{1,0:T(8,128)}, f32[655,128]{1,0:T(8,128)S(1)}, u32[]{:S(2)}) copy-start(f32[655,128]{1,0:T(8,128)S(1)} %collective-permute-done.11) | copy-start | bytes 1006084
  71.8 12.9 %collective-permute-start.13 = (f32[655,128]{1,0:T(8,128)S(1)}, f32[655,128]{1,0:T(8,128)S(1)}, u32[]{:S(2)}, u32[]{:S(2)}) collective-permute-start(f32[655,128]{1,0:T(8,128)S(1)} %collective-permute-done.11), channel_id=1, source_target_pairs={{1,0},{2,1},{3,2},{4,3},{5,4},{6,5},{7,6},{8,7},{9,8},{10,9},{11,1... | collective-permute-start | bytes 1006088 | tf_op jit(solution)/shard_map/ppermute | solution.py:32
  79.6 3.4 %copy-start.12 = (f32[655,128]{1,0:T(8,128)}, f32[655,128]{1,0:T(8,128)S(1)}, u32[]{:S(2)}) copy-start(f32[655,128]{1,0:T(8,128)S(1)} %collective-permute-done.10) | copy-start | bytes 1006084
  79.7 12.9 %collective-permute-start.12 = (f32[655,128]{1,0:T(8,128)S(1)}, f32[655,128]{1,0:T(8,128)S(1)}, u32[]{:S(2)}, u32[]{:S(2)}) collective-permute-start(f32[655,128]{1,0:T(8,128)S(1)} %collective-permute-done.10), channel_id=1, source_target_pairs={{0,1},{1,2},{2,3},{3,4},{4,5},{5,6},{6,7},{7,8},{8,9},{9,10},{10,1... | collective-permute-start | bytes 1006088 | tf_op jit(solution)/shard_map/ppermute | solution.py:32
  84.6 13.1 %collective-permute-start.15 = (f32[655,128]{1,0:T(8,128)S(1)}, f32[655,128]{1,0:T(8,128)S(1)}, u32[]{:S(2)}, u32[]{:S(2)}) collective-permute-start(f32[655,128]{1,0:T(8,128)S(1)} %collective-permute-done.13), channel_id=1, source_target_pairs={{1,0},{2,1},{3,2},{4,3},{5,4},{6,5},{7,6},{8,7},{9,8},{10,9},{11,1... | collective-permute-start | bytes 1006088 | tf_op jit(solution)/shard_map/ppermute | solution.py:32
  92.5 3.6 %copy-start.14 = (f32[655,128]{1,0:T(8,128)}, f32[655,128]{1,0:T(8,128)S(1)}, u32[]{:S(2)}) copy-start(f32[655,128]{1,0:T(8,128)S(1)} %collective-permute-done.12) | copy-start | bytes 1006084
  92.5 13.1 %collective-permute-start.14 = (f32[655,128]{1,0:T(8,128)S(1)}, f32[655,128]{1,0:T(8,128)S(1)}, u32[]{:S(2)}, u32[]{:S(2)}) collective-permute-start(f32[655,128]{1,0:T(8,128)S(1)} %collective-permute-done.12), channel_id=1, source_target_pairs={{0,1},{1,2},{2,3},{3,4},{4,5},{5,6},{6,7},{7,8},{8,9},{9,10},{10,1... | collective-permute-start | bytes 1006088 | tf_op jit(solution)/shard_map/ppermute | solution.py:32
  97.7 11.3 %copy-start.13 = (f32[655,128]{1,0:T(8,128)}, f32[655,128]{1,0:T(8,128)S(1)}, u32[]{:S(2)}) copy-start(f32[655,128]{1,0:T(8,128)S(1)} %collective-permute-done.15) | copy-start | bytes 1006084
  97.7 13.0 %collective-permute-start.17 = (f32[655,128]{1,0:T(8,128)S(1)}, f32[655,128]{1,0:T(8,128)S(1)}, u32[]{:S(2)}, u32[]{:S(2)}) collective-permute-start(f32[655,128]{1,0:T(8,128)S(1)} %collective-permute-done.15), channel_id=1, source_target_pairs={{1,0},{2,1},{3,2},{4,3},{5,4},{6,5},{7,6},{8,7},{9,8},{10,9},{11,1... | collective-permute-start | bytes 1006088 | tf_op jit(solution)/shard_map/ppermute | solution.py:32
  105.6 3.5 %copy-start.16 = (f32[655,128]{1,0:T(8,128)}, f32[655,128]{1,0:T(8,128)S(1)}, u32[]{:S(2)}) copy-start(f32[655,128]{1,0:T(8,128)S(1)} %collective-permute-done.14) | copy-start | bytes 1006084
  105.6 13.0 %collective-permute-start.16 = (f32[655,128]{1,0:T(8,128)S(1)}, f32[655,128]{1,0:T(8,128)S(1)}, u32[]{:S(2)}, u32[]{:S(2)}) collective-permute-start(f32[655,128]{1,0:T(8,128)S(1)} %collective-permute-done.14), channel_id=1, source_target_pairs={{0,1},{1,2},{2,3},{3,4},{4,5},{5,6},{6,7},{7,8},{8,9},{9,10},{10,1... | collective-permute-start | bytes 1006088 | tf_op jit(solution)/shard_map/ppermute | solution.py:32
  110.7 11.3 %copy-start.15 = (f32[655,128]{1,0:T(8,128)}, f32[655,128]{1,0:T(8,128)S(1)}, u32[]{:S(2)}) copy-start(f32[655,128]{1,0:T(8,128)S(1)} %collective-permute-done.17) | copy-start | bytes 1006084
  110.7 12.8 %collective-permute-start.19 = (f32[655,128]{1,0:T(8,128)S(1)}, f32[655,128]{1,0:T(8,128)S(1)}, u32[]{:S(2)}, u32[]{:S(2)}) collective-permute-start(f32[655,128]{1,0:T(8,128)S(1)} %collective-permute-done.17), channel_id=1, source_target_pairs={{1,0},{2,1},{3,2},{4,3},{5,4},{6,5},{7,6},{8,7},{9,8},{10,9},{11,1... | collective-permute-start | bytes 1006088 | tf_op jit(solution)/shard_map/ppermute | solution.py:32
  118.6 3.4 %copy-start.18 = (f32[655,128]{1,0:T(8,128)}, f32[655,128]{1,0:T(8,128)S(1)}, u32[]{:S(2)}) copy-start(f32[655,128]{1,0:T(8,128)S(1)} %collective-permute-done.16) | copy-start | bytes 1006084
  118.6 12.8 %collective-permute-start.18 = (f32[655,128]{1,0:T(8,128)S(1)}, f32[655,128]{1,0:T(8,128)S(1)}, u32[]{:S(2)}, u32[]{:S(2)}) collective-permute-start(f32[655,128]{1,0:T(8,128)S(1)} %collective-permute-done.16), channel_id=1, source_target_pairs={{0,1},{1,2},{2,3},{3,4},{4,5},{5,6},{6,7},{7,8},{8,9},{9,10},{10,1... | collective-permute-start | bytes 1006088 | tf_op jit(solution)/shard_map/ppermute | solution.py:32
  123.6 11.4 %copy-start.17 = (f32[655,128]{1,0:T(8,128)}, f32[655,128]{1,0:T(8,128)S(1)}, u32[]{:S(2)}) copy-start(f32[655,128]{1,0:T(8,128)S(1)} %collective-permute-done.19) | copy-start | bytes 1006084
  123.6 13.0 %collective-permute-start.21 = (f32[655,128]{1,0:T(8,128)S(1)}, f32[655,128]{1,0:T(8,128)S(1)}, u32[]{:S(2)}, u32[]{:S(2)}) collective-permute-start(f32[655,128]{1,0:T(8,128)S(1)} %collective-permute-done.19), channel_id=1, source_target_pairs={{1,0},{2,1},{3,2},{4,3},{5,4},{6,5},{7,6},{8,7},{9,8},{10,9},{11,1... | collective-permute-start | bytes 1006088 | tf_op jit(solution)/shard_map/ppermute | solution.py:32
  131.5 3.5 %copy-start.20 = (f32[655,128]{1,0:T(8,128)}, f32[655,128]{1,0:T(8,128)S(1)}, u32[]{:S(2)}) copy-start(f32[655,128]{1,0:T(8,128)S(1)} %collective-permute-done.18) | copy-start | bytes 1006084
  131.5 12.7 %collective-permute-start.20 = (f32[655,128]{1,0:T(8,128)S(1)}, f32[655,128]{1,0:T(8,128)S(1)}, u32[]{:S(2)}, u32[]{:S(2)}) collective-permute-start(f32[655,128]{1,0:T(8,128)S(1)} %collective-permute-done.18), channel_id=1, source_target_pairs={{0,1},{1,2},{2,3},{3,4},{4,5},{5,6},{6,7},{7,8},{8,9},{9,10},{10,1... | collective-permute-start | bytes 1006088 | tf_op jit(solution)/shard_map/ppermute | solution.py:32
  136.6 9.1 %copy-start.19 = (f32[655,128]{1,0:T(8,128)}, f32[655,128]{1,0:T(8,128)S(1)}, u32[]{:S(2)}) copy-start(f32[655,128]{1,0:T(8,128)S(1)} %collective-permute-done.21) | copy-start | bytes 1006084
  144.2 1.5 copy-start.21
  246.5 1.0 copy-start.3
  246.6 1.5 copy-start.2

commit v7 on v5

--- a/solution.py
+++ b/solution.py
@@ -299,6 +299,70 @@
     top_out[...] = top_land[...]
     pair_out[...] = pair_land[...]
     quad_out[...] = quad_land[...]
+
+
+def mates_kernel(block_ref, out_ref, landing, send_sem, recv_sem):
+    dev = lax.axis_index(AX)
+    member = dev % 8
+    base = dev - member
+    mesh_id = pl.DeviceIdType.MESH
+    barrier = pltpu.get_barrier_semaphore()
+    for step in range(1, 8):
+        pl.semaphore_signal(
+            barrier,
+            inc=1,
+            device_id=device_coords(base + lax.rem(member + step, 8)),
+            device_id_type=mesh_id,
+        )
+    pl.semaphore_wait(barrier, 7)
+
+    def outgoing(step):
+        return pltpu.make_async_remote_copy(
+            src_ref=block_ref,
+            dst_ref=landing.at[member],
+            send_sem=send_sem.at[step],
+            recv_sem=recv_sem.at[member],
+            device_id=device_coords(base + lax.rem(member + step, 8)),
+            device_id_type=mesh_id,
+        )
+
+    def incoming(step):
+        source = lax.rem(member - step + 8, 8)
+        return pltpu.make_async_remote_copy(
+            src_ref=block_ref,
+            dst_ref=landing.at[source],
+            send_sem=send_sem.at[step],
+            recv_sem=recv_sem.at[source],
+            device_id=device_coords(base + source),
+            device_id_type=mesh_id,
+        )
+
+    for step in range(1, 8):
+        outgoing(step).start()
+    own = pltpu.make_async_copy(block_ref, landing.at[member], send_sem.at[0])
+    own.start()
+    own.wait()
+    for step in range(1, 8):
+        outgoing(step).wait_send()
+        incoming(step).wait_recv()
+    out_ref[...] = landing[...]
+
+
+def mates_gather(block):
+    rows, cols = block.shape
+    vmem = pl.BlockSpec(memory_space=pltpu.VMEM)
+    return pl.pallas_call(
+        mates_kernel,
+        out_shape=jax.ShapeDtypeStruct((8, rows, cols), jnp.float32),
+        in_specs=[vmem],
+        out_specs=vmem,
+        scratch_shapes=[
+            pltpu.VMEM((8, rows, cols), jnp.float32),
+            pltpu.SemaphoreType.DMA((8,)),
+            pltpu.SemaphoreType.DMA((8,)),
+        ],
+        compiler_params=pltpu.CompilerParams(collective_id=1, has_side_effects=True),
+    )(block)
 
 
 def exchange(top_block, coef_pair, coef_quad):
@@ -385,7 +449,7 @@
         jnp.take(all_top, top_chosen, axis=0),
         top_entries >= 0,
     )
-    local_top = lax.all_gather(top_cols, MEMBERS, axis=1, tiled=True)
+    local_top = mates_gather(top_cols.T).reshape(rank, width).T
     local_quad = middle_full(quad_stack, skel_quad, far_quad, quad_matrix, local_top, 4, device)
     local_pair = middle_full(pair_stack, skel_pair, far_pair, pair_matrix, local_quad, 2, device)
     leaf_entries = far_leaf[0]

time: 257 us -> 253 us (0.984)
  blocking collectives: 14.5 us -> 0 us
  Pallas kernels: 69.6 us -> 80 us
    all_gather x1 -> x0, blocking collectives: 14.5 us -> none  [per_device(): local_top = lax.all_gather(top_cols, MEMBERS, axis=1, tiled=True)]
    pallas_call x0 -> x1, Pallas kernels: none -> 10.3 us  [mates_gather(): pl.pallas_call(mates_kernel, out_shape=jax.ShapeDtypeStruct((8, rows, col...]
  transfers between devices with their start and end apart: 22 -> 22, of which waited for: 4 -> 4; matrix products, arithmetic and copies ran while one was open for 12% -> 13% of each run, Pallas kernels for 0% -> 0%
where the time goes in v7:
time: 253 us; the launch traced here: 248 us
  starting transfers between devices  91.4 us (36%)
  Pallas kernels  80 us (32%)
  matrix products  33.1 us (13%)
  local copies, waits for them, and re-layouts  21.9 us (9%)
  waiting for transfers between devices  16.1 us (6%)
  other arithmetic  4.6 us (2%)
    ppermute x16, starting transfers between devices, from_behind(): return lax.ppermute(block, axis, route)  79.4 us
    pallas_call x1, Pallas kernels, exchange(): pl.pallas_call(functools.partial(exchange_kernel, clusters), out_shape=(j...  69.7 us
    dot_general x17, matrix products, contribution(): jnp.dot(kernel_block(own_points, coords), block[:leaf_points], precision=...  26.1 us
    ppermute x6, starting transfers between devices, from_partner(): return lax.ppermute(value, axis, pairs)  12 us
    unnamed x75, local copies, waits for them, and re-layouts  11.9 us
    pallas_call x1, Pallas kernels, mates_gather(): pl.pallas_call(mates_kernel, out_shape=jax.ShapeDtypeStruct((8, rows, col...  10.3 us
    ppermute x6, waiting for transfers between devices, from_partner(): return lax.ppermute(value, axis, pairs)  8.61 us
    ppermute x16, waiting for transfers between devices, from_behind(): return lax.ppermute(block, axis, route)  7.45 us
  transfers between devices with their start and end apart: 22, of which 4 were waited for; matrix products, arithmetic and copies ran while one was open for 13% of the time, Pallas kernels for 0%

profile of v7, /device:TPU:24, one launch (start us, length us, event | category | flops | bytes accessed | tf_op | source)
XLA Modules:
  0.0 248.4 jit_solution(15575100173905825247)
XLA Ops:
  1.7 1.6 fusion.407
  3.3 1.0 pad_maximum_fusion
  4.3 1.9 collective-permute-start.6
  6.2 13.2 %collective-permute-start.7 = (f32[655,128]{1,0:T(8,128)S(1)}, f32[655,128]{1,0:T(8,128)S(1)}, u32[]{:S(2)}, u32[]{:S(2)}) collective-permute-start(f32[655,128]{1,0:T(8,128)S(1)} %pad_maximum_fusion), channel_id=1, source_target_pairs={{1,0},{2,1},{3,2},{4,3},{5,4},{6,5},{7,6},{8,7},{9,8},{10,9},{11,1... | collective-permute-start | bytes 1006088 | tf_op jit(solution)/shard_map/ppermute | solution.py:32
  19.5 1.9 collective-permute-start.1
  21.4 2.4 collective-permute-start
  26.9 1.6 gather_fusion.1
  28.6 1.0 compare_reduce_fusion.8
  29.6 1.6 convolution_select_fusion.16
  32.1 1.9 collective-permute-start.2
  34.3 3.6 %collective-permute-done.2 = f32[64,128]{1,0:T(8,128)S(1)} collective-permute-done((f32[64,128]{1,0:T(8,128)S(1)}, f32[64,128]{1,0:T(8,128)S(1)}, u32[]{:S(2)}, u32[]{:S(2)}) %collective-permute-start.2) | collective-permute-done | bytes 32800 | tf_op jit(solution)/shard_map/ppermute | solution.py:26
  38.2 1.9 collective-permute-start.3
  40.1 1.4 collective-permute-done.3
  42.2 1.9 collective-permute-start.4
  44.1 2.0 collective-permute-start.8
  46.2 7.7 %collective-permute-start.9 = (f32[655,128]{1,0:T(8,128)S(1)}, f32[655,128]{1,0:T(8,128)S(1)}, u32[]{:S(2)}, u32[]{:S(2)}) collective-permute-start(f32[655,128]{1,0:T(8,128)S(1)} %collective-permute-done.7), channel_id=1, source_target_pairs={{1,0},{2,1},{3,2},{4,3},{5,4},{6,5},{7,6},{8,7},{9,8},{10,9},{11,1... | collective-permute-start | bytes 1006088 | tf_op jit(solution)/shard_map/ppermute | solution.py:32
  53.9 1.6 fusion.17
  56.2 1.9 collective-permute-start.5
  58.1 1.5 fusion.16
  59.6 3.6 %collective-permute-done.5 = f32[128,128]{1,0:T(8,128)S(1)} collective-permute-done((f32[128,128]{1,0:T(8,128)S(1)}, f32[128,128]{1,0:T(8,128)S(1)}, u32[]{:S(2)}, u32[]{:S(2)}) %collective-permute-start.5) | collective-permute-done | bytes 65568 | tf_op jit(solution)/shard_map/ppermute | solution.py:26
  63.4 3.2 %collective-permute-start.11 = (f32[655,128]{1,0:T(8,128)S(1)}, f32[655,128]{1,0:T(8,128)S(1)}, u32[]{:S(2)}, u32[]{:S(2)}) collective-permute-start(f32[655,128]{1,0:T(8,128)S(1)} %collective-permute-done.9), channel_id=1, source_target_pairs={{1,0},{2,1},{3,2},{4,3},{5,4},{6,5},{7,6},{8,7},{9,8},{10,9},{11,1... | collective-permute-start | bytes 1006088 | tf_op jit(solution)/shard_map/ppermute | solution.py:32
  66.7 1.9 collective-permute-start.10
  68.6 1.5 convolution_select_fusion.12
  70.2 1.5 fusion.15
  71.7 7.9 %collective-permute-start.13 = (f32[655,128]{1,0:T(8,128)S(1)}, f32[655,128]{1,0:T(8,128)S(1)}, u32[]{:S(2)}, u32[]{:S(2)}) collective-permute-start(f32[655,128]{1,0:T(8,128)S(1)} %collective-permute-done.11), channel_id=1, source_target_pairs={{1,0},{2,1},{3,2},{4,3},{5,4},{6,5},{7,6},{8,7},{9,8},{10,9},{11,1... | collective-permute-start | bytes 1006088 | tf_op jit(solution)/shard_map/ppermute | solution.py:32
  79.6 1.9 collective-permute-start.12
  81.6 1.5 convolution_select_fusion.10
  83.1 1.5 fusion.13
  84.6 7.9 %collective-permute-start.15 = (f32[655,128]{1,0:T(8,128)S(1)}, f32[655,128]{1,0:T(8,128)S(1)}, u32[]{:S(2)}, u32[]{:S(2)}) collective-permute-start(f32[655,128]{1,0:T(8,128)S(1)} %collective-permute-done.13), channel_id=1, source_target_pairs={{1,0},{2,1},{3,2},{4,3},{5,4},{6,5},{7,6},{8,7},{9,8},{10,9},{11,1... | collective-permute-start | bytes 1006088 | tf_op jit(solution)/shard_map/ppermute | solution.py:32
  92.5 2.1 collective-permute-start.14
  94.6 1.5 convolution_select_fusion.8
  96.1 1.6 fusion.11
  97.7 7.9 %collective-permute-start.17 = (f32[655,128]{1,0:T(8,128)S(1)}, f32[655,128]{1,0:T(8,128)S(1)}, u32[]{:S(2)}, u32[]{:S(2)}) collective-permute-start(f32[655,128]{1,0:T(8,128)S(1)} %collective-permute-done.15), channel_id=1, source_target_pairs={{1,0},{2,1},{3,2},{4,3},{5,4},{6,5},{7,6},{8,7},{9,8},{10,9},{11,1... | collective-permute-start | bytes 1006088 | tf_op jit(solution)/shard_map/ppermute | solution.py:32
  105.6 1.9 collective-permute-start.16
  107.5 1.6 convolution_select_fusion.6
  109.1 1.5 fusion.9
  110.7 7.9 %collective-permute-start.19 = (f32[655,128]{1,0:T(8,128)S(1)}, f32[655,128]{1,0:T(8,128)S(1)}, u32[]{:S(2)}, u32[]{:S(2)}) collective-permute-start(f32[655,128]{1,0:T(8,128)S(1)} %collective-permute-done.17), channel_id=1, source_target_pairs={{1,0},{2,1},{3,2},{4,3},{5,4},{6,5},{7,6},{8,7},{9,8},{10,9},{11,1... | collective-permute-start | bytes 1006088 | tf_op jit(solution)/shard_map/ppermute | solution.py:32
  118.6 1.9 collective-permute-start.18
  120.5 1.5 convolution_select_fusion.4
  122.0 1.6 fusion.7
  123.7 7.9 %collective-permute-start.21 = (f32[655,128]{1,0:T(8,128)S(1)}, f32[655,128]{1,0:T(8,128)S(1)}, u32[]{:S(2)}, u32[]{:S(2)}) collective-permute-start(f32[655,128]{1,0:T(8,128)S(1)} %collective-permute-done.19), channel_id=1, source_target_pairs={{1,0},{2,1},{3,2},{4,3},{5,4},{6,5},{7,6},{8,7},{9,8},{10,9},{11,1... | collective-permute-start | bytes 1006088 | tf_op jit(solution)/shard_map/ppermute | solution.py:32
  131.6 2.1 collective-permute-start.20
  133.7 1.5 convolution_select_fusion.2
  135.3 1.5 fusion.5
  136.9 7.4 %collective-permute-done.20 = f32[655,128]{1,0:T(8,128)S(1)} collective-permute-done((f32[655,128]{1,0:T(8,128)S(1)}, f32[655,128]{1,0:T(8,128)S(1)}, u32[]{:S(2)}, u32[]{:S(2)}) %collective-permute-start.20) | collective-permute-done | bytes 335392 | tf_op jit(solution)/shard_map/ppermute | solution.py:32
  144.3 1.5 convolution_select_fusion
  145.8 1.6 fusion.3
  148.1 69.7 %shard_map.145 = (f32[64,16,128]{2,1,0:T(8,128)}, f32[8,128,128]{2,1,0:T(8,128)}, f32[8,128,128]{2,1,0:T(8,128)}) custom-call(f32[16,128]{1,0:T(8,128)} %copy.28.top_ref, f32[128,128]{1,0:T(8,128)} %slice_bitcast_fusion.17.pair_ref, f32[128,128]{1,0:T(8,128)} %get-tuple-element.97.quad_ref), custom_call_target="tpu_custom_call" | custom-call | tf_op jit(solution)/shard_map/pallas_call | solution.py:373
  217.8 1.6 gather_fusion.3
  219.4 1.2 fusion.206.block_ref
  220.5 10.3 %shard_map.146 = f32[8,16,128]{2,1,0:T(8,128)} custom-call(f32[16,128]{1,0:T(8,128)} %fusion.206.block_ref), custom_call_target="tpu_custom_call" | custom-call | tf_op jit(solution)/shard_map/pallas_call | solution.py:354
  230.8 0.9 fusion.456
  231.7 0.9 fusion.455
  232.6 0.9 fusion.454
  233.5 0.9 fusion.453
  234.4 0.9 fusion.451
  235.3 0.9 fusion.450
  236.2 0.9 fusion.447
  237.1 0.9 fusion.446
  238.0 0.9 fusion.444
  238.9 0.9 fusion.443
  239.8 0.9 fusion.442
  240.7 0.9 fusion.441
  247.4 1.0 fusion.1
  (161 shorter events, 14.0 us)
Async XLA Ops:
  0.0 1.7 copy-start
  0.0 25.0 %copy-start.26 = (f32[1,3,128]{2,0,1:T(1,128)S(1)}, f32[1,3,128]{2,0,1:T(1,128)}, u32[]{:S(2)}) copy-start(f32[1,3,128]{2,0,1:T(1,128)} %param.23) | copy-start | bytes 4612
  0.0 23.8 %copy-start.9 = (f32[1,3,512]{2,0,1:T(1,128)S(1)}, f32[1,3,512]{2,0,1:T(1,128)}, u32[]{:S(2)}) copy-start(f32[1,3,512]{2,0,1:T(1,128)} %param.18) | copy-start | bytes 18436
  0.0 19.4 %copy-start.22 = (f32[32,128]{1,0:T(8,128)S(1)}, f32[32,128]{1,0:T(8,128)}, u32[]{:S(2)}) copy-start(f32[32,128]{1,0:T(8,128)} %param.22) | copy-start | bytes 49156
  0.0 21.4 %copy-start.7 = (f32[64,128]{1,0:T(8,128)S(1)}, f32[64,128]{1,0:T(8,128)}, u32[]{:S(2)}) copy-start(f32[64,128]{1,0:T(8,128)} %param.21) | copy-start | bytes 98308
  0.0 23.8 %copy-start.23 = (s32[128,8]{0,1:T(8,128)S(1)}, s32[128,8]{0,1:T(8,128)}, u32[]{:S(2)}) copy-start(s32[128,8]{0,1:T(8,128)} %param.30) | copy-start | bytes 12292
  0.0 23.8 %copy-start.24 = (s32[64,8]{0,1:T(8,128)S(1)}, s32[64,8]{0,1:T(8,128)}, u32[]{:S(2)}) copy-start(s32[64,8]{0,1:T(8,128)} %param.31) | copy-start | bytes 6148
  0.1 24.3 %copy-start.25 = (s32[256,8]{0,1:T(8,128)S(1)}, s32[256,8]{0,1:T(8,128)}, u32[]{:S(2)}) copy-start(s32[256,8]{0,1:T(8,128)} %param.29) | copy-start | bytes 24580
  0.1 24.6 %copy-start.27 = (s32[1,8]{1,0:T(1,128)S(1)}, s32[1,8]{1,0:T(1,128)}, u32[]{:S(2)}) copy-start(s32[1,8]{1,0:T(1,128)} %param.28) | copy-start | bytes 100
  0.1 25.0 %copy-start.4 = (f32[1,128,128]{2,1,0:T(8,128)S(1)}, f32[1,128,128]{2,1,0:T(8,128)}, u32[]{:S(2)}) copy-start(f32[1,128,128]{2,1,0:T(8,128)} %param.20) | copy-start | bytes 196612
  0.1 25.3 %copy-start.8 = (f32[128,3,128]{2,0,1:T(8,128)S(1)}, f32[128,3,128]{2,0,1:T(8,128)}, u32[]{:S(2)}) copy-start(f32[128,3,128]{2,0,1:T(8,128)} %param.25) | copy-start | bytes 589828
  0.1 26.0 %copy-start.6 = (f32[64,3,128]{2,0,1:T(8,128)S(1)}, f32[64,3,128]{2,0,1:T(8,128)}, u32[]{:S(2)}) copy-start(f32[64,3,128]{2,0,1:T(8,128)} %param.26) | copy-start | bytes 294916
  1.7 26.9 %copy-start.28 = (s32[1,16]{1,0:T(1,128)S(1)}, s32[1,16]{1,0:T(1,128)}, u32[]{:S(2)}) copy-start(s32[1,16]{1,0:T(1,128)} %param.27) | copy-start | bytes 196
  1.7 27.9 %copy-start.1 = (f32[1,512,128]{2,1,0:T(8,128)S(1)}, f32[1,512,128]{2,1,0:T(8,128)}, u32[]{:S(2)}) copy-start(f32[1,512,128]{2,1,0:T(8,128)} %param.17) | copy-start | bytes 786436
  4.3 39.8 %collective-permute-start.6 = (f32[655,128]{1,0:T(8,128)S(1)}, f32[655,128]{1,0:T(8,128)S(1)}, u32[]{:S(2)}, u32[]{:S(2)}) collective-permute-start(f32[655,128]{1,0:T(8,128)S(1)} %pad_maximum_fusion), channel_id=1, source_target_pairs={{0,1},{1,2},{2,3},{3,4},{4,5},{5,6},{6,7},{7,8},{8,9},{9,10},{10,1... | collective-permute-start | bytes 1006088 | tf_op jit(solution)/shard_map/ppermute | solution.py:32
  6.2 40.0 %collective-permute-start.7 = (f32[655,128]{1,0:T(8,128)S(1)}, f32[655,128]{1,0:T(8,128)S(1)}, u32[]{:S(2)}, u32[]{:S(2)}) collective-permute-start(f32[655,128]{1,0:T(8,128)S(1)} %pad_maximum_fusion), channel_id=1, source_target_pairs={{1,0},{2,1},{3,2},{4,3},{5,4},{6,5},{7,6},{8,7},{9,8},{10,9},{11,1... | collective-permute-start | bytes 1006088 | tf_op jit(solution)/shard_map/ppermute | solution.py:32
  19.5 12.6 %collective-permute-start.1 = (f32[32,128]{1,0:T(8,128)S(1)}, f32[32,128]{1,0:T(8,128)S(1)}, u32[]{:S(2)}, u32[]{:S(2)}) collective-permute-start(f32[32,128]{1,0:T(8,128)S(1)} %copy-done.22), channel_id=1, source_target_pairs={{0,1},{1,0},{2,3},{3,2},{4,5},{5,4},{6,7},{7,6},{8,9},{9,8},{10,11... | collective-permute-start | bytes 49160 | tf_op jit(solution)/shard_map/ppermute | solution.py:26
  21.4 12.6 %collective-permute-start = (f32[64,128]{1,0:T(8,128)S(1)}, f32[64,128]{1,0:T(8,128)S(1)}, u32[]{:S(2)}, u32[]{:S(2)}) collective-permute-start(f32[64,128]{1,0:T(8,128)S(1)} %copy-done.7), channel_id=1, source_target_pairs={{0,1},{1,0},{2,3},{3,2},{4,5},{5,4},{6,7},{7,6},{8,9},{9,8},{10,11... | collective-permute-start | bytes 98312 | tf_op jit(solution)/shard_map/ppermute | solution.py:26
  32.1 5.8 %collective-permute-start.2 = (f32[64,128]{1,0:T(8,128)S(1)}, f32[64,128]{1,0:T(8,128)S(1)}, u32[]{:S(2)}, u32[]{:S(2)}) collective-permute-start(f32[64,128]{1,0:T(8,128)S(1)} %maximum_select_fusion.6), channel_id=1, source_target_pairs={{0,2},{1,3},{2,0},{3,1},{4,6},{5,7},{6,4},{7,5},{8,10},{9,11},{10,... | collective-permute-start | bytes 98312 | tf_op jit(solution)/shard_map/ppermute | solution.py:26
  38.2 3.3 %collective-permute-start.3 = (f32[3,128,128]{2,1,0:T(8,128)S(1)}, f32[3,128,128]{2,1,0:T(8,128)S(1)}, u32[]{:S(2)}, u32[]{:S(2)}) collective-permute-start(f32[3,128,128]{2,1,0:T(8,128)S(1)} %pad_maximum_fusion.1), channel_id=1, source_target_pairs={{0,1},{1,0},{2,3},{3,2},{4,5},{5,4},{6,7},{7,6},{8,9},{9,8},{10,11... | collective-permute-start | bytes 589832 | tf_op jit(solution)/shard_map/ppermute | solution.py:26
  42.2 13.4 %collective-permute-start.4 = (f32[2,128,128]{2,1,0:T(8,128)S(1)}, f32[2,128,128]{2,1,0:T(8,128)S(1)}, u32[]{:S(2)}, u32[]{:S(2)}) collective-permute-start(f32[2,128,128]{2,1,0:T(8,128)S(1)} %slice.660), channel_id=1, source_target_pairs={{0,2},{1,3},{2,0},{3,1},{4,6},{5,7},{6,4},{7,5},{8,10},{9,11},{10,... | collective-permute-start | bytes 393224 | tf_op jit(solution)/shard_map/ppermute | solution.py:26
  44.1 22.5 %collective-permute-start.8 = (f32[655,128]{1,0:T(8,128)S(1)}, f32[655,128]{1,0:T(8,128)S(1)}, u32[]{:S(2)}, u32[]{:S(2)}) collective-permute-start(f32[655,128]{1,0:T(8,128)S(1)} %collective-permute-done.6), channel_id=1, source_target_pairs={{0,1},{1,2},{2,3},{3,4},{4,5},{5,6},{6,7},{7,8},{8,9},{9,10},{10,1... | collective-permute-start | bytes 1006088 | tf_op jit(solution)/shard_map/ppermute | solution.py:32
  46.2 17.2 %collective-permute-start.9 = (f32[655,128]{1,0:T(8,128)S(1)}, f32[655,128]{1,0:T(8,128)S(1)}, u32[]{:S(2)}, u32[]{:S(2)}) collective-permute-start(f32[655,128]{1,0:T(8,128)S(1)} %collective-permute-done.7), channel_id=1, source_target_pairs={{1,0},{2,1},{3,2},{4,3},{5,4},{6,5},{7,6},{8,7},{9,8},{10,9},{11,1... | collective-permute-start | bytes 1006088 | tf_op jit(solution)/shard_map/ppermute | solution.py:32
  56.2 7.0 %collective-permute-start.5 = (f32[128,128]{1,0:T(8,128)S(1)}, f32[128,128]{1,0:T(8,128)S(1)}, u32[]{:S(2)}, u32[]{:S(2)}) collective-permute-start(f32[128,128]{1,0:T(8,128)S(1)} %get-tuple-element.98), channel_id=1, source_target_pairs={{0,4},{1,5},{2,6},{3,7},{4,0},{5,1},{6,2},{7,3},{8,12},{9,13},{10,... | collective-permute-start | bytes 196616 | tf_op jit(solution)/shard_map/ppermute | solution.py:26
  63.4 6.7 %copy-start.10 = (f32[655,128]{1,0:T(8,128)}, f32[655,128]{1,0:T(8,128)S(1)}, u32[]{:S(2)}) copy-start(f32[655,128]{1,0:T(8,128)S(1)} %collective-permute-done.9) | copy-start | bytes 1006084
  63.4 8.3 %collective-permute-start.11 = (f32[655,128]{1,0:T(8,128)S(1)}, f32[655,128]{1,0:T(8,128)S(1)}, u32[]{:S(2)}, u32[]{:S(2)}) collective-permute-start(f32[655,128]{1,0:T(8,128)S(1)} %collective-permute-done.9), channel_id=1, source_target_pairs={{1,0},{2,1},{3,2},{4,3},{5,4},{6,5},{7,6},{8,7},{9,8},{10,9},{11,1... | collective-permute-start | bytes 1006088 | tf_op jit(solution)/shard_map/ppermute | solution.py:32
  66.7 3.5 %copy-start.11 = (f32[655,128]{1,0:T(8,128)}, f32[655,128]{1,0:T(8,128)S(1)}, u32[]{:S(2)}) copy-start(f32[655,128]{1,0:T(8,128)S(1)} %collective-permute-done.8) | copy-start | bytes 1006084
  66.7 13.0 %collective-permute-start.10 = (f32[655,128]{1,0:T(8,128)S(1)}, f32[655,128]{1,0:T(8,128)S(1)}, u32[]{:S(2)}, u32[]{:S(2)}) collective-permute-start(f32[655,128]{1,0:T(8,128)S(1)} %collective-permute-done.8), channel_id=1, source_target_pairs={{0,1},{1,2},{2,3},{3,4},{4,5},{5,6},{6,7},{7,8},{8,9},{9,10},{10,1... | collective-permute-start | bytes 1006088 | tf_op jit(solution)/shard_map/ppermute | solution.py:32
  71.7 11.3 %copy-start.12 = (f32[655,128]{1,0:T(8,128)}, f32[655,128]{1,0:T(8,128)S(1)}, u32[]{:S(2)}) copy-start(f32[655,128]{1,0:T(8,128)S(1)} %collective-permute-done.11) | copy-start | bytes 1006084
  71.7 12.9 %collective-permute-start.13 = (f32[655,128]{1,0:T(8,128)S(1)}, f32[655,128]{1,0:T(8,128)S(1)}, u32[]{:S(2)}, u32[]{:S(2)}) collective-permute-start(f32[655,128]{1,0:T(8,128)S(1)} %collective-permute-done.11), channel_id=1, source_target_pairs={{1,0},{2,1},{3,2},{4,3},{5,4},{6,5},{7,6},{8,7},{9,8},{10,9},{11,1... | collective-permute-start | bytes 1006088 | tf_op jit(solution)/shard_map/ppermute | solution.py:32
  79.6 3.4 %copy-start.13 = (f32[655,128]{1,0:T(8,128)}, f32[655,128]{1,0:T(8,128)S(1)}, u32[]{:S(2)}) copy-start(f32[655,128]{1,0:T(8,128)S(1)} %collective-permute-done.10) | copy-start | bytes 1006084
  79.6 12.9 %collective-permute-start.12 = (f32[655,128]{1,0:T(8,128)S(1)}, f32[655,128]{1,0:T(8,128)S(1)}, u32[]{:S(2)}, u32[]{:S(2)}) collective-permute-start(f32[655,128]{1,0:T(8,128)S(1)} %collective-permute-done.10), channel_id=1, source_target_pairs={{0,1},{1,2},{2,3},{3,4},{4,5},{5,6},{6,7},{7,8},{8,9},{9,10},{10,1... | collective-permute-start | bytes 1006088 | tf_op jit(solution)/shard_map/ppermute | solution.py:32
  84.6 13.1 %collective-permute-start.15 = (f32[655,128]{1,0:T(8,128)S(1)}, f32[655,128]{1,0:T(8,128)S(1)}, u32[]{:S(2)}, u32[]{:S(2)}) collective-permute-start(f32[655,128]{1,0:T(8,128)S(1)} %collective-permute-done.13), channel_id=1, source_target_pairs={{1,0},{2,1},{3,2},{4,3},{5,4},{6,5},{7,6},{8,7},{9,8},{10,9},{11,1... | collective-permute-start | bytes 1006088 | tf_op jit(solution)/shard_map/ppermute | solution.py:32
  92.5 13.1 %collective-permute-start.14 = (f32[655,128]{1,0:T(8,128)S(1)}, f32[655,128]{1,0:T(8,128)S(1)}, u32[]{:S(2)}, u32[]{:S(2)}) collective-permute-start(f32[655,128]{1,0:T(8,128)S(1)} %collective-permute-done.12), channel_id=1, source_target_pairs={{0,1},{1,2},{2,3},{3,4},{4,5},{5,6},{6,7},{7,8},{8,9},{9,10},{10,1... | collective-permute-start | bytes 1006088 | tf_op jit(solution)/shard_map/ppermute | solution.py:32
  97.7 11.4 %copy-start.14 = (f32[655,128]{1,0:T(8,128)}, f32[655,128]{1,0:T(8,128)S(1)}, u32[]{:S(2)}) copy-start(f32[655,128]{1,0:T(8,128)S(1)} %collective-permute-done.15) | copy-start | bytes 1006084
  97.7 13.0 %collective-permute-start.17 = (f32[655,128]{1,0:T(8,128)S(1)}, f32[655,128]{1,0:T(8,128)S(1)}, u32[]{:S(2)}, u32[]{:S(2)}) collective-permute-start(f32[655,128]{1,0:T(8,128)S(1)} %collective-permute-done.15), channel_id=1, source_target_pairs={{1,0},{2,1},{3,2},{4,3},{5,4},{6,5},{7,6},{8,7},{9,8},{10,9},{11,1... | collective-permute-start | bytes 1006088 | tf_op jit(solution)/shard_map/ppermute | solution.py:32
  105.6 3.5 %copy-start.16 = (f32[655,128]{1,0:T(8,128)}, f32[655,128]{1,0:T(8,128)S(1)}, u32[]{:S(2)}) copy-start(f32[655,128]{1,0:T(8,128)S(1)} %collective-permute-done.14) | copy-start | bytes 1006084
  105.6 13.0 %collective-permute-start.16 = (f32[655,128]{1,0:T(8,128)S(1)}, f32[655,128]{1,0:T(8,128)S(1)}, u32[]{:S(2)}, u32[]{:S(2)}) collective-permute-start(f32[655,128]{1,0:T(8,128)S(1)} %collective-permute-done.14), channel_id=1, source_target_pairs={{0,1},{1,2},{2,3},{3,4},{4,5},{5,6},{6,7},{7,8},{8,9},{9,10},{10,1... | collective-permute-start | bytes 1006088 | tf_op jit(solution)/shard_map/ppermute | solution.py:32
  110.7 11.3 %copy-start.15 = (f32[655,128]{1,0:T(8,128)}, f32[655,128]{1,0:T(8,128)S(1)}, u32[]{:S(2)}) copy-start(f32[655,128]{1,0:T(8,128)S(1)} %collective-permute-done.17) | copy-start | bytes 1006084
  110.7 12.9 %collective-permute-start.19 = (f32[655,128]{1,0:T(8,128)S(1)}, f32[655,128]{1,0:T(8,128)S(1)}, u32[]{:S(2)}, u32[]{:S(2)}) collective-permute-start(f32[655,128]{1,0:T(8,128)S(1)} %collective-permute-done.17), channel_id=1, source_target_pairs={{1,0},{2,1},{3,2},{4,3},{5,4},{6,5},{7,6},{8,7},{9,8},{10,9},{11,1... | collective-permute-start | bytes 1006088 | tf_op jit(solution)/shard_map/ppermute | solution.py:32
  118.6 3.4 %copy-start.18 = (f32[655,128]{1,0:T(8,128)}, f32[655,128]{1,0:T(8,128)S(1)}, u32[]{:S(2)}) copy-start(f32[655,128]{1,0:T(8,128)S(1)} %collective-permute-done.16) | copy-start | bytes 1006084
  118.6 12.9 %collective-permute-start.18 = (f32[655,128]{1,0:T(8,128)S(1)}, f32[655,128]{1,0:T(8,128)S(1)}, u32[]{:S(2)}, u32[]{:S(2)}) collective-permute-start(f32[655,128]{1,0:T(8,128)S(1)} %collective-permute-done.16), channel_id=1, source_target_pairs={{0,1},{1,2},{2,3},{3,4},{4,5},{5,6},{6,7},{7,8},{8,9},{9,10},{10,1... | collective-permute-start | bytes 1006088 | tf_op jit(solution)/shard_map/ppermute | solution.py:32
  123.7 11.6 %copy-start.17 = (f32[655,128]{1,0:T(8,128)}, f32[655,128]{1,0:T(8,128)S(1)}, u32[]{:S(2)}) copy-start(f32[655,128]{1,0:T(8,128)S(1)} %collective-permute-done.19) | copy-start | bytes 1006084
  123.7 13.2 %collective-permute-start.21 = (f32[655,128]{1,0:T(8,128)S(1)}, f32[655,128]{1,0:T(8,128)S(1)}, u32[]{:S(2)}, u32[]{:S(2)}) collective-permute-start(f32[655,128]{1,0:T(8,128)S(1)} %collective-permute-done.19), channel_id=1, source_target_pairs={{1,0},{2,1},{3,2},{4,3},{5,4},{6,5},{7,6},{8,7},{9,8},{10,9},{11,1... | collective-permute-start | bytes 1006088 | tf_op jit(solution)/shard_map/ppermute | solution.py:32
  131.6 3.7 %copy-start.20 = (f32[655,128]{1,0:T(8,128)}, f32[655,128]{1,0:T(8,128)S(1)}, u32[]{:S(2)}) copy-start(f32[655,128]{1,0:T(8,128)S(1)} %collective-permute-done.18) | copy-start | bytes 1006084
  131.6 12.7 %collective-permute-start.20 = (f32[655,128]{1,0:T(8,128)S(1)}, f32[655,128]{1,0:T(8,128)S(1)}, u32[]{:S(2)}, u32[]{:S(2)}) collective-permute-start(f32[655,128]{1,0:T(8,128)S(1)} %collective-permute-done.18), channel_id=1, source_target_pairs={{0,1},{1,2},{2,3},{3,4},{4,5},{5,6},{6,7},{7,8},{8,9},{9,10},{10,1... | collective-permute-start | bytes 1006088 | tf_op jit(solution)/shard_map/ppermute | solution.py:32
  136.8 8.9 %copy-start.19 = (f32[655,128]{1,0:T(8,128)}, f32[655,128]{1,0:T(8,128)S(1)}, u32[]{:S(2)}) copy-start(f32[655,128]{1,0:T(8,128)S(1)} %collective-permute-done.21) | copy-start | bytes 1006084
  144.3 1.5 copy-start.21
  242.2 1.0 copy-start.3
  242.3 1.5 copy-start.2
  245.9 0.8 copy-start.5

commit v8 on v7

--- a/solution.py
+++ b/solution.py
@@ -41,7 +41,9 @@
 
 
 def transposed_dot(matrix, values):
-    return lax.dot_general(matrix, values, (((0,), (0,)), ((), ())), precision=HIGHEST)
+    return lax.dot_general(
+        matrix, values, (((0,), (0,)), ((), ())), precision=lax.Precision.HIGH
+    )
 
 
 def listed_sum(own_coords, entries, fetcher, width):

time: 253 us -> 252 us (level)
  no operation moved by 1% of the time
where the time goes in v8:
time: 252 us; the launch traced here: 248 us
  starting transfers between devices  91.4 us (36%)
  Pallas kernels  80 us (32%)
  matrix products  32.8 us (13%)
  local copies, waits for them, and re-layouts  21.9 us (9%)
  waiting for transfers between devices  16.1 us (6%)
  other arithmetic  4.6 us (2%)
    ppermute x16, starting transfers between devices, from_behind(): return lax.ppermute(block, axis, route)  79.4 us
    pallas_call x1, Pallas kernels, exchange(): pl.pallas_call(functools.partial(exchange_kernel, clusters), out_shape=(j...  69.7 us
    dot_general x17, matrix products, contribution(): jnp.dot(kernel_block(own_points, coords), block[:leaf_points], precision=...  26.1 us
    ppermute x6, starting transfers between devices, from_partner(): return lax.ppermute(value, axis, pairs)  12 us
    unnamed x75, local copies, waits for them, and re-layouts  11.9 us
    pallas_call x1, Pallas kernels, mates_gather(): pl.pallas_call(mates_kernel, out_shape=jax.ShapeDtypeStruct((8, rows, col...  10.3 us
    ppermute x6, waiting for transfers between devices, from_partner(): return lax.ppermute(value, axis, pairs)  8.63 us
    ppermute x16, waiting for transfers between devices, from_behind(): return lax.ppermute(block, axis, route)  7.45 us
  transfers between devices with their start and end apart: 22, of which 4 were waited for; matrix products, arithmetic and copies ran while one was open for 13% of the time, Pallas kernels for 0%

profile of v8, /device:TPU:24, one launch (start us, length us, event | category | flops | bytes accessed | tf_op | source)
XLA Modules:
  0.0 248.1 jit_solution(5814911584109164203)
XLA Ops:
  1.7 1.4 fusion.407
  3.1 1.0 pad_maximum_fusion
  4.1 1.9 collective-permute-start.6
  6.0 13.2 %collective-permute-start.7 = (f32[655,128]{1,0:T(8,128)S(1)}, f32[655,128]{1,0:T(8,128)S(1)}, u32[]{:S(2)}, u32[]{:S(2)}) collective-permute-start(f32[655,128]{1,0:T(8,128)S(1)} %pad_maximum_fusion), channel_id=1, source_target_pairs={{1,0},{2,1},{3,2},{4,3},{5,4},{6,5},{7,6},{8,7},{9,8},{10,9},{11,1... | collective-permute-start | bytes 1006088 | tf_op jit(solution)/shard_map/ppermute | solution.py:32
  19.3 1.9 collective-permute-start.1
  21.2 2.4 collective-permute-start
  26.6 1.6 gather_fusion.1
  28.3 1.0 compare_reduce_fusion.8
  29.3 1.6 convolution_select_fusion.16
  31.8 1.9 collective-permute-start.2
  34.0 3.6 %collective-permute-done.2 = f32[64,128]{1,0:T(8,128)S(1)} collective-permute-done((f32[64,128]{1,0:T(8,128)S(1)}, f32[64,128]{1,0:T(8,128)S(1)}, u32[]{:S(2)}, u32[]{:S(2)}) %collective-permute-start.2) | collective-permute-done | bytes 32800 | tf_op jit(solution)/shard_map/ppermute | solution.py:26
  37.9 1.9 collective-permute-start.3
  39.8 1.4 collective-permute-done.3
  41.9 1.9 collective-permute-start.4
  43.8 2.0 collective-permute-start.8
  45.9 7.7 %collective-permute-start.9 = (f32[655,128]{1,0:T(8,128)S(1)}, f32[655,128]{1,0:T(8,128)S(1)}, u32[]{:S(2)}, u32[]{:S(2)}) collective-permute-start(f32[655,128]{1,0:T(8,128)S(1)} %collective-permute-done.7), channel_id=1, source_target_pairs={{1,0},{2,1},{3,2},{4,3},{5,4},{6,5},{7,6},{8,7},{9,8},{10,9},{11,1... | collective-permute-start | bytes 1006088 | tf_op jit(solution)/shard_map/ppermute | solution.py:32
  53.7 1.6 fusion.17
  55.9 1.9 collective-permute-start.5
  57.9 1.5 fusion.16
  59.3 3.6 %collective-permute-done.5 = f32[128,128]{1,0:T(8,128)S(1)} collective-permute-done((f32[128,128]{1,0:T(8,128)S(1)}, f32[128,128]{1,0:T(8,128)S(1)}, u32[]{:S(2)}, u32[]{:S(2)}) %collective-permute-start.5) | collective-permute-done | bytes 65568 | tf_op jit(solution)/shard_map/ppermute | solution.py:26
  63.1 3.2 %collective-permute-start.11 = (f32[655,128]{1,0:T(8,128)S(1)}, f32[655,128]{1,0:T(8,128)S(1)}, u32[]{:S(2)}, u32[]{:S(2)}) collective-permute-start(f32[655,128]{1,0:T(8,128)S(1)} %collective-permute-done.9), channel_id=1, source_target_pairs={{1,0},{2,1},{3,2},{4,3},{5,4},{6,5},{7,6},{8,7},{9,8},{10,9},{11,1... | collective-permute-start | bytes 1006088 | tf_op jit(solution)/shard_map/ppermute | solution.py:32
  66.4 1.9 collective-permute-start.10
  68.3 1.5 convolution_select_fusion.12
  69.9 1.5 fusion.15
  71.4 7.9 %collective-permute-start.13 = (f32[655,128]{1,0:T(8,128)S(1)}, f32[655,128]{1,0:T(8,128)S(1)}, u32[]{:S(2)}, u32[]{:S(2)}) collective-permute-start(f32[655,128]{1,0:T(8,128)S(1)} %collective-permute-done.11), channel_id=1, source_target_pairs={{1,0},{2,1},{3,2},{4,3},{5,4},{6,5},{7,6},{8,7},{9,8},{10,9},{11,1... | collective-permute-start | bytes 1006088 | tf_op jit(solution)/shard_map/ppermute | solution.py:32
  79.4 1.9 collective-permute-start.12
  81.3 1.5 convolution_select_fusion.10
  82.8 1.5 fusion.13
  84.3 7.9 %collective-permute-start.15 = (f32[655,128]{1,0:T(8,128)S(1)}, f32[655,128]{1,0:T(8,128)S(1)}, u32[]{:S(2)}, u32[]{:S(2)}) collective-permute-start(f32[655,128]{1,0:T(8,128)S(1)} %collective-permute-done.13), channel_id=1, source_target_pairs={{1,0},{2,1},{3,2},{4,3},{5,4},{6,5},{7,6},{8,7},{9,8},{10,9},{11,1... | collective-permute-start | bytes 1006088 | tf_op jit(solution)/shard_map/ppermute | solution.py:32
  92.2 2.1 collective-permute-start.14
  94.3 1.5 convolution_select_fusion.8
  95.8 1.6 fusion.11
  97.4 7.9 %collective-permute-start.17 = (f32[655,128]{1,0:T(8,128)S(1)}, f32[655,128]{1,0:T(8,128)S(1)}, u32[]{:S(2)}, u32[]{:S(2)}) collective-permute-start(f32[655,128]{1,0:T(8,128)S(1)} %collective-permute-done.15), channel_id=1, source_target_pairs={{1,0},{2,1},{3,2},{4,3},{5,4},{6,5},{7,6},{8,7},{9,8},{10,9},{11,1... | collective-permute-start | bytes 1006088 | tf_op jit(solution)/shard_map/ppermute | solution.py:32
  105.3 1.9 collective-permute-start.16
  107.3 1.6 convolution_select_fusion.6
  108.8 1.5 fusion.9
  110.4 7.9 %collective-permute-start.19 = (f32[655,128]{1,0:T(8,128)S(1)}, f32[655,128]{1,0:T(8,128)S(1)}, u32[]{:S(2)}, u32[]{:S(2)}) collective-permute-start(f32[655,128]{1,0:T(8,128)S(1)} %collective-permute-done.17), channel_id=1, source_target_pairs={{1,0},{2,1},{3,2},{4,3},{5,4},{6,5},{7,6},{8,7},{9,8},{10,9},{11,1... | collective-permute-start | bytes 1006088 | tf_op jit(solution)/shard_map/ppermute | solution.py:32
  118.3 1.9 collective-permute-start.18
  120.2 1.5 convolution_select_fusion.4
  121.8 1.6 fusion.7
  123.4 7.9 %collective-permute-start.21 = (f32[655,128]{1,0:T(8,128)S(1)}, f32[655,128]{1,0:T(8,128)S(1)}, u32[]{:S(2)}, u32[]{:S(2)}) collective-permute-start(f32[655,128]{1,0:T(8,128)S(1)} %collective-permute-done.19), channel_id=1, source_target_pairs={{1,0},{2,1},{3,2},{4,3},{5,4},{6,5},{7,6},{8,7},{9,8},{10,9},{11,1... | collective-permute-start | bytes 1006088 | tf_op jit(solution)/shard_map/ppermute | solution.py:32
  131.3 2.1 collective-permute-start.20
  133.4 1.5 convolution_select_fusion.2
  135.0 1.5 fusion.5
  136.6 7.4 %collective-permute-done.20 = f32[655,128]{1,0:T(8,128)S(1)} collective-permute-done((f32[655,128]{1,0:T(8,128)S(1)}, f32[655,128]{1,0:T(8,128)S(1)}, u32[]{:S(2)}, u32[]{:S(2)}) %collective-permute-start.20) | collective-permute-done | bytes 335392 | tf_op jit(solution)/shard_map/ppermute | solution.py:32
  144.0 1.5 convolution_select_fusion
  145.5 1.6 fusion.3
  147.8 69.7 %shard_map.145 = (f32[64,16,128]{2,1,0:T(8,128)}, f32[8,128,128]{2,1,0:T(8,128)}, f32[8,128,128]{2,1,0:T(8,128)}) custom-call(f32[16,128]{1,0:T(8,128)} %copy.28.top_ref, f32[128,128]{1,0:T(8,128)} %slice_bitcast_fusion.17.pair_ref, f32[128,128]{1,0:T(8,128)} %get-tuple-element.97.quad_ref), custom_call_target="tpu_custom_call" | custom-call | tf_op jit(solution)/shard_map/pallas_call | solution.py:375
  217.4 1.6 gather_fusion.3
  219.0 1.2 fusion.206.block_ref
  220.2 10.3 %shard_map.146 = f32[8,16,128]{2,1,0:T(8,128)} custom-call(f32[16,128]{1,0:T(8,128)} %fusion.206.block_ref), custom_call_target="tpu_custom_call" | custom-call | tf_op jit(solution)/shard_map/pallas_call | solution.py:356
  230.5 0.9 fusion.456
  231.4 0.9 fusion.455
  232.3 0.9 fusion.454
  233.2 0.9 fusion.453
  234.1 0.9 fusion.451
  235.0 0.9 fusion.450
  235.9 0.9 fusion.447
  236.8 0.9 fusion.446
  237.7 0.9 fusion.444
  238.6 0.9 fusion.443
  239.5 0.9 fusion.442
  240.4 0.9 fusion.441
  247.1 1.0 fusion.1
  (161 shorter events, 13.9 us)
Async XLA Ops:
  0.0 1.7 copy-start
  0.0 24.8 %copy-start.26 = (f32[1,3,128]{2,0,1:T(1,128)S(1)}, f32[1,3,128]{2,0,1:T(1,128)}, u32[]{:S(2)}) copy-start(f32[1,3,128]{2,0,1:T(1,128)} %param.23) | copy-start | bytes 4612
  0.0 23.6 %copy-start.9 = (f32[1,3,512]{2,0,1:T(1,128)S(1)}, f32[1,3,512]{2,0,1:T(1,128)}, u32[]{:S(2)}) copy-start(f32[1,3,512]{2,0,1:T(1,128)} %param.18) | copy-start | bytes 18436
  0.0 19.2 %copy-start.22 = (f32[32,128]{1,0:T(8,128)S(1)}, f32[32,128]{1,0:T(8,128)}, u32[]{:S(2)}) copy-start(f32[32,128]{1,0:T(8,128)} %param.22) | copy-start | bytes 49156
  0.0 21.2 %copy-start.7 = (f32[64,128]{1,0:T(8,128)S(1)}, f32[64,128]{1,0:T(8,128)}, u32[]{:S(2)}) copy-start(f32[64,128]{1,0:T(8,128)} %param.21) | copy-start | bytes 98308
  0.0 23.6 %copy-start.23 = (s32[128,8]{0,1:T(8,128)S(1)}, s32[128,8]{0,1:T(8,128)}, u32[]{:S(2)}) copy-start(s32[128,8]{0,1:T(8,128)} %param.30) | copy-start | bytes 12292
  0.0 23.6 %copy-start.24 = (s32[64,8]{0,1:T(8,128)S(1)}, s32[64,8]{0,1:T(8,128)}, u32[]{:S(2)}) copy-start(s32[64,8]{0,1:T(8,128)} %param.31) | copy-start | bytes 6148
  0.1 24.1 %copy-start.25 = (s32[256,8]{0,1:T(8,128)S(1)}, s32[256,8]{0,1:T(8,128)}, u32[]{:S(2)}) copy-start(s32[256,8]{0,1:T(8,128)} %param.29) | copy-start | bytes 24580
  0.1 24.3 %copy-start.27 = (s32[1,8]{1,0:T(1,128)S(1)}, s32[1,8]{1,0:T(1,128)}, u32[]{:S(2)}) copy-start(s32[1,8]{1,0:T(1,128)} %param.28) | copy-start | bytes 100
  0.1 24.8 %copy-start.4 = (f32[1,128,128]{2,1,0:T(8,128)S(1)}, f32[1,128,128]{2,1,0:T(8,128)}, u32[]{:S(2)}) copy-start(f32[1,128,128]{2,1,0:T(8,128)} %param.20) | copy-start | bytes 196612
  0.1 25.1 %copy-start.8 = (f32[128,3,128]{2,0,1:T(8,128)S(1)}, f32[128,3,128]{2,0,1:T(8,128)}, u32[]{:S(2)}) copy-start(f32[128,3,128]{2,0,1:T(8,128)} %param.25) | copy-start | bytes 589828
  0.1 25.8 %copy-start.6 = (f32[64,3,128]{2,0,1:T(8,128)S(1)}, f32[64,3,128]{2,0,1:T(8,128)}, u32[]{:S(2)}) copy-start(f32[64,3,128]{2,0,1:T(8,128)} %param.26) | copy-start | bytes 294916
  1.7 26.7 %copy-start.28 = (s32[1,16]{1,0:T(1,128)S(1)}, s32[1,16]{1,0:T(1,128)}, u32[]{:S(2)}) copy-start(s32[1,16]{1,0:T(1,128)} %param.27) | copy-start | bytes 196
  1.7 27.6 %copy-start.1 = (f32[1,512,128]{2,1,0:T(8,128)S(1)}, f32[1,512,128]{2,1,0:T(8,128)}, u32[]{:S(2)}) copy-start(f32[1,512,128]{2,1,0:T(8,128)} %param.17) | copy-start | bytes 786436
  4.1 39.7 %collective-permute-start.6 = (f32[655,128]{1,0:T(8,128)S(1)}, f32[655,128]{1,0:T(8,128)S(1)}, u32[]{:S(2)}, u32[]{:S(2)}) collective-permute-start(f32[655,128]{1,0:T(8,128)S(1)} %pad_maximum_fusion), channel_id=1, source_target_pairs={{0,1},{1,2},{2,3},{3,4},{4,5},{5,6},{6,7},{7,8},{8,9},{9,10},{10,1... | collective-permute-start | bytes 1006088 | tf_op jit(solution)/shard_map/ppermute | solution.py:32
  6.0 39.9 %collective-permute-start.7 = (f32[655,128]{1,0:T(8,128)S(1)}, f32[655,128]{1,0:T(8,128)S(1)}, u32[]{:S(2)}, u32[]{:S(2)}) collective-permute-start(f32[655,128]{1,0:T(8,128)S(1)} %pad_maximum_fusion), channel_id=1, source_target_pairs={{1,0},{2,1},{3,2},{4,3},{5,4},{6,5},{7,6},{8,7},{9,8},{10,9},{11,1... | collective-permute-start | bytes 1006088 | tf_op jit(solution)/shard_map/ppermute | solution.py:32
  19.3 12.5 %collective-permute-start.1 = (f32[32,128]{1,0:T(8,128)S(1)}, f32[32,128]{1,0:T(8,128)S(1)}, u32[]{:S(2)}, u32[]{:S(2)}) collective-permute-start(f32[32,128]{1,0:T(8,128)S(1)} %copy-done.22), channel_id=1, source_target_pairs={{0,1},{1,0},{2,3},{3,2},{4,5},{5,4},{6,7},{7,6},{8,9},{9,8},{10,11... | collective-permute-start | bytes 49160 | tf_op jit(solution)/shard_map/ppermute | solution.py:26
  21.2 12.5 %collective-permute-start = (f32[64,128]{1,0:T(8,128)S(1)}, f32[64,128]{1,0:T(8,128)S(1)}, u32[]{:S(2)}, u32[]{:S(2)}) collective-permute-start(f32[64,128]{1,0:T(8,128)S(1)} %copy-done.7), channel_id=1, source_target_pairs={{0,1},{1,0},{2,3},{3,2},{4,5},{5,4},{6,7},{7,6},{8,9},{9,8},{10,11... | collective-permute-start | bytes 98312 | tf_op jit(solution)/shard_map/ppermute | solution.py:26
  31.8 5.8 %collective-permute-start.2 = (f32[64,128]{1,0:T(8,128)S(1)}, f32[64,128]{1,0:T(8,128)S(1)}, u32[]{:S(2)}, u32[]{:S(2)}) collective-permute-start(f32[64,128]{1,0:T(8,128)S(1)} %maximum_select_fusion.6), channel_id=1, source_target_pairs={{0,2},{1,3},{2,0},{3,1},{4,6},{5,7},{6,4},{7,5},{8,10},{9,11},{10,... | collective-permute-start | bytes 98312 | tf_op jit(solution)/shard_map/ppermute | solution.py:26
  37.9 3.3 %collective-permute-start.3 = (f32[3,128,128]{2,1,0:T(8,128)S(1)}, f32[3,128,128]{2,1,0:T(8,128)S(1)}, u32[]{:S(2)}, u32[]{:S(2)}) collective-permute-start(f32[3,128,128]{2,1,0:T(8,128)S(1)} %pad_maximum_fusion.1), channel_id=1, source_target_pairs={{0,1},{1,0},{2,3},{3,2},{4,5},{5,4},{6,7},{7,6},{8,9},{9,8},{10,11... | collective-permute-start | bytes 589832 | tf_op jit(solution)/shard_map/ppermute | solution.py:26
  41.9 13.4 %collective-permute-start.4 = (f32[2,128,128]{2,1,0:T(8,128)S(1)}, f32[2,128,128]{2,1,0:T(8,128)S(1)}, u32[]{:S(2)}, u32[]{:S(2)}) collective-permute-start(f32[2,128,128]{2,1,0:T(8,128)S(1)} %slice.660), channel_id=1, source_target_pairs={{0,2},{1,3},{2,0},{3,1},{4,6},{5,7},{6,4},{7,5},{8,10},{9,11},{10,... | collective-permute-start | bytes 393224 | tf_op jit(solution)/shard_map/ppermute | solution.py:26
  43.8 22.5 %collective-permute-start.8 = (f32[655,128]{1,0:T(8,128)S(1)}, f32[655,128]{1,0:T(8,128)S(1)}, u32[]{:S(2)}, u32[]{:S(2)}) collective-permute-start(f32[655,128]{1,0:T(8,128)S(1)} %collective-permute-done.6), channel_id=1, source_target_pairs={{0,1},{1,2},{2,3},{3,4},{4,5},{5,6},{6,7},{7,8},{8,9},{9,10},{10,1... | collective-permute-start | bytes 1006088 | tf_op jit(solution)/shard_map/ppermute | solution.py:32
  45.9 17.2 %collective-permute-start.9 = (f32[655,128]{1,0:T(8,128)S(1)}, f32[655,128]{1,0:T(8,128)S(1)}, u32[]{:S(2)}, u32[]{:S(2)}) collective-permute-start(f32[655,128]{1,0:T(8,128)S(1)} %collective-permute-done.7), channel_id=1, source_target_pairs={{1,0},{2,1},{3,2},{4,3},{5,4},{6,5},{7,6},{8,7},{9,8},{10,9},{11,1... | collective-permute-start | bytes 1006088 | tf_op jit(solution)/shard_map/ppermute | solution.py:32
  55.9 7.0 %collective-permute-start.5 = (f32[128,128]{1,0:T(8,128)S(1)}, f32[128,128]{1,0:T(8,128)S(1)}, u32[]{:S(2)}, u32[]{:S(2)}) collective-permute-start(f32[128,128]{1,0:T(8,128)S(1)} %get-tuple-element.98), channel_id=1, source_target_pairs={{0,4},{1,5},{2,6},{3,7},{4,0},{5,1},{6,2},{7,3},{8,12},{9,13},{10,... | collective-permute-start | bytes 196616 | tf_op jit(solution)/shard_map/ppermute | solution.py:26
  63.1 6.7 %copy-start.10 = (f32[655,128]{1,0:T(8,128)}, f32[655,128]{1,0:T(8,128)S(1)}, u32[]{:S(2)}) copy-start(f32[655,128]{1,0:T(8,128)S(1)} %collective-permute-done.9) | copy-start | bytes 1006084
  63.1 8.3 %collective-permute-start.11 = (f32[655,128]{1,0:T(8,128)S(1)}, f32[655,128]{1,0:T(8,128)S(1)}, u32[]{:S(2)}, u32[]{:S(2)}) collective-permute-start(f32[655,128]{1,0:T(8,128)S(1)} %collective-permute-done.9), channel_id=1, source_target_pairs={{1,0},{2,1},{3,2},{4,3},{5,4},{6,5},{7,6},{8,7},{9,8},{10,9},{11,1... | collective-permute-start | bytes 1006088 | tf_op jit(solution)/shard_map/ppermute | solution.py:32
  66.4 3.5 %copy-start.11 = (f32[655,128]{1,0:T(8,128)}, f32[655,128]{1,0:T(8,128)S(1)}, u32[]{:S(2)}) copy-start(f32[655,128]{1,0:T(8,128)S(1)} %collective-permute-done.8) | copy-start | bytes 1006084
  66.4 13.0 %collective-permute-start.10 = (f32[655,128]{1,0:T(8,128)S(1)}, f32[655,128]{1,0:T(8,128)S(1)}, u32[]{:S(2)}, u32[]{:S(2)}) collective-permute-start(f32[655,128]{1,0:T(8,128)S(1)} %collective-permute-done.8), channel_id=1, source_target_pairs={{0,1},{1,2},{2,3},{3,4},{4,5},{5,6},{6,7},{7,8},{8,9},{9,10},{10,1... | collective-permute-start | bytes 1006088 | tf_op jit(solution)/shard_map/ppermute | solution.py:32
  71.4 11.3 %copy-start.12 = (f32[655,128]{1,0:T(8,128)}, f32[655,128]{1,0:T(8,128)S(1)}, u32[]{:S(2)}) copy-start(f32[655,128]{1,0:T(8,128)S(1)} %collective-permute-done.11) | copy-start | bytes 1006084
  71.4 12.9 %collective-permute-start.13 = (f32[655,128]{1,0:T(8,128)S(1)}, f32[655,128]{1,0:T(8,128)S(1)}, u32[]{:S(2)}, u32[]{:S(2)}) collective-permute-start(f32[655,128]{1,0:T(8,128)S(1)} %collective-permute-done.11), channel_id=1, source_target_pairs={{1,0},{2,1},{3,2},{4,3},{5,4},{6,5},{7,6},{8,7},{9,8},{10,9},{11,1... | collective-permute-start | bytes 1006088 | tf_op jit(solution)/shard_map/ppermute | solution.py:32
  79.3 3.4 %copy-start.13 = (f32[655,128]{1,0:T(8,128)}, f32[655,128]{1,0:T(8,128)S(1)}, u32[]{:S(2)}) copy-start(f32[655,128]{1,0:T(8,128)S(1)} %collective-permute-done.10) | copy-start | bytes 1006084
  79.4 12.9 %collective-permute-start.12 = (f32[655,128]{1,0:T(8,128)S(1)}, f32[655,128]{1,0:T(8,128)S(1)}, u32[]{:S(2)}, u32[]{:S(2)}) collective-permute-start(f32[655,128]{1,0:T(8,128)S(1)} %collective-permute-done.10), channel_id=1, source_target_pairs={{0,1},{1,2},{2,3},{3,4},{4,5},{5,6},{6,7},{7,8},{8,9},{9,10},{10,1... | collective-permute-start | bytes 1006088 | tf_op jit(solution)/shard_map/ppermute | solution.py:32
  84.3 13.1 %collective-permute-start.15 = (f32[655,128]{1,0:T(8,128)S(1)}, f32[655,128]{1,0:T(8,128)S(1)}, u32[]{:S(2)}, u32[]{:S(2)}) collective-permute-start(f32[655,128]{1,0:T(8,128)S(1)} %collective-permute-done.13), channel_id=1, source_target_pairs={{1,0},{2,1},{3,2},{4,3},{5,4},{6,5},{7,6},{8,7},{9,8},{10,9},{11,1... | collective-permute-start | bytes 1006088 | tf_op jit(solution)/shard_map/ppermute | solution.py:32
  92.2 13.1 %collective-permute-start.14 = (f32[655,128]{1,0:T(8,128)S(1)}, f32[655,128]{1,0:T(8,128)S(1)}, u32[]{:S(2)}, u32[]{:S(2)}) collective-permute-start(f32[655,128]{1,0:T(8,128)S(1)} %collective-permute-done.12), channel_id=1, source_target_pairs={{0,1},{1,2},{2,3},{3,4},{4,5},{5,6},{6,7},{7,8},{8,9},{9,10},{10,1... | collective-permute-start | bytes 1006088 | tf_op jit(solution)/shard_map/ppermute | solution.py:32
  97.4 11.4 %copy-start.14 = (f32[655,128]{1,0:T(8,128)}, f32[655,128]{1,0:T(8,128)S(1)}, u32[]{:S(2)}) copy-start(f32[655,128]{1,0:T(8,128)S(1)} %collective-permute-done.15) | copy-start | bytes 1006084
  97.4 13.0 %collective-permute-start.17 = (f32[655,128]{1,0:T(8,128)S(1)}, f32[655,128]{1,0:T(8,128)S(1)}, u32[]{:S(2)}, u32[]{:S(2)}) collective-permute-start(f32[655,128]{1,0:T(8,128)S(1)} %collective-permute-done.15), channel_id=1, source_target_pairs={{1,0},{2,1},{3,2},{4,3},{5,4},{6,5},{7,6},{8,7},{9,8},{10,9},{11,1... | collective-permute-start | bytes 1006088 | tf_op jit(solution)/shard_map/ppermute | solution.py:32
  105.3 3.5 %copy-start.16 = (f32[655,128]{1,0:T(8,128)}, f32[655,128]{1,0:T(8,128)S(1)}, u32[]{:S(2)}) copy-start(f32[655,128]{1,0:T(8,128)S(1)} %collective-permute-done.14) | copy-start | bytes 1006084
  105.3 13.0 %collective-permute-start.16 = (f32[655,128]{1,0:T(8,128)S(1)}, f32[655,128]{1,0:T(8,128)S(1)}, u32[]{:S(2)}, u32[]{:S(2)}) collective-permute-start(f32[655,128]{1,0:T(8,128)S(1)} %collective-permute-done.14), channel_id=1, source_target_pairs={{0,1},{1,2},{2,3},{3,4},{4,5},{5,6},{6,7},{7,8},{8,9},{9,10},{10,1... | collective-permute-start | bytes 1006088 | tf_op jit(solution)/shard_map/ppermute | solution.py:32
  110.4 11.3 %copy-start.15 = (f32[655,128]{1,0:T(8,128)}, f32[655,128]{1,0:T(8,128)S(1)}, u32[]{:S(2)}) copy-start(f32[655,128]{1,0:T(8,128)S(1)} %collective-permute-done.17) | copy-start | bytes 1006084
  110.4 12.9 %collective-permute-start.19 = (f32[655,128]{1,0:T(8,128)S(1)}, f32[655,128]{1,0:T(8,128)S(1)}, u32[]{:S(2)}, u32[]{:S(2)}) collective-permute-start(f32[655,128]{1,0:T(8,128)S(1)} %collective-permute-done.17), channel_id=1, source_target_pairs={{1,0},{2,1},{3,2},{4,3},{5,4},{6,5},{7,6},{8,7},{9,8},{10,9},{11,1... | collective-permute-start | bytes 1006088 | tf_op jit(solution)/shard_map/ppermute | solution.py:32
  118.3 3.4 %copy-start.18 = (f32[655,128]{1,0:T(8,128)}, f32[655,128]{1,0:T(8,128)S(1)}, u32[]{:S(2)}) copy-start(f32[655,128]{1,0:T(8,128)S(1)} %collective-permute-done.16) | copy-start | bytes 1006084
  118.3 12.9 %collective-permute-start.18 = (f32[655,128]{1,0:T(8,128)S(1)}, f32[655,128]{1,0:T(8,128)S(1)}, u32[]{:S(2)}, u32[]{:S(2)}) collective-permute-start(f32[655,128]{1,0:T(8,128)S(1)} %collective-permute-done.16), channel_id=1, source_target_pairs={{0,1},{1,2},{2,3},{3,4},{4,5},{5,6},{6,7},{7,8},{8,9},{9,10},{10,1... | collective-permute-start | bytes 1006088 | tf_op jit(solution)/shard_map/ppermute | solution.py:32
  123.4 11.6 %copy-start.17 = (f32[655,128]{1,0:T(8,128)}, f32[655,128]{1,0:T(8,128)S(1)}, u32[]{:S(2)}) copy-start(f32[655,128]{1,0:T(8,128)S(1)} %collective-permute-done.19) | copy-start | bytes 1006084
  123.4 13.2 %collective-permute-start.21 = (f32[655,128]{1,0:T(8,128)S(1)}, f32[655,128]{1,0:T(8,128)S(1)}, u32[]{:S(2)}, u32[]{:S(2)}) collective-permute-start(f32[655,128]{1,0:T(8,128)S(1)} %collective-permute-done.19), channel_id=1, source_target_pairs={{1,0},{2,1},{3,2},{4,3},{5,4},{6,5},{7,6},{8,7},{9,8},{10,9},{11,1... | collective-permute-start | bytes 1006088 | tf_op jit(solution)/shard_map/ppermute | solution.py:32
  131.3 3.7 %copy-start.20 = (f32[655,128]{1,0:T(8,128)}, f32[655,128]{1,0:T(8,128)S(1)}, u32[]{:S(2)}) copy-start(f32[655,128]{1,0:T(8,128)S(1)} %collective-permute-done.18) | copy-start | bytes 1006084
  131.3 12.7 %collective-permute-start.20 = (f32[655,128]{1,0:T(8,128)S(1)}, f32[655,128]{1,0:T(8,128)S(1)}, u32[]{:S(2)}, u32[]{:S(2)}) collective-permute-start(f32[655,128]{1,0:T(8,128)S(1)} %collective-permute-done.18), channel_id=1, source_target_pairs={{0,1},{1,2},{2,3},{3,4},{4,5},{5,6},{6,7},{7,8},{8,9},{9,10},{10,1... | collective-permute-start | bytes 1006088 | tf_op jit(solution)/shard_map/ppermute | solution.py:32
  136.5 8.9 %copy-start.19 = (f32[655,128]{1,0:T(8,128)}, f32[655,128]{1,0:T(8,128)S(1)}, u32[]{:S(2)}) copy-start(f32[655,128]{1,0:T(8,128)S(1)} %collective-permute-done.21) | copy-start | bytes 1006084
  144.0 1.5 copy-start.21
  241.9 1.0 copy-start.3
  242.0 1.5 copy-start.2
  245.6 0.8 copy-start.5

commit v9 on v7

--- a/solution.py
+++ b/solution.py
@@ -141,10 +141,13 @@
     def contribution(block, distance):
         listed = jnp.any(near_entries == device + distance)
         coords = block[leaf_points:point_rows].reshape(3, leaf_points)
-        contrib = jnp.dot(
-            kernel_block(own_points, coords), block[:leaf_points], precision=lax.Precision.HIGH
-        )
-        return jnp.where(listed, contrib, 0.0)
+        def compute(coords, values):
+            return jnp.dot(kernel_block(own_points, coords), values, precision=lax.Precision.HIGH)
+
+        def skip(coords, values):
+            return jnp.zeros(values.shape, jnp.float32)
+
+        return lax.cond(listed, compute, skip, coords, block[:leaf_points])
 
     total = contribution(shipped, 0)
     ahead = shipped

time: 253 us -> 289 us (1.14)
  Pallas kernels: 80 us -> 111 us
  matrix products: 33.1 us -> 9.26 us
  local copies, waits for them, and re-layouts: 21.9 us -> 37.6 us
  between operations: 1.33 us -> 12.3 us
  waiting for transfers between devices: 16.1 us -> 5.69 us
  other arithmetic: 4.6 us -> 11.4 us
  starting transfers between devices: 91.4 us -> 95.6 us
    pallas_call x1, Pallas kernels: 69.7 us -> 103 us  [exchange(): pl.pallas_call(functools.partial(exchange_kernel, clusters), out_shape=(j...]
    dot_general x17 -> x0, matrix products: 26.1 us -> none  [contribution(): jnp.dot(kernel_block(own_points, coords), block[:leaf_points], precision=...]
    ppermute x6, waiting for transfers between devices: 8.61 us -> 0.02 us  [from_partner(): return lax.ppermute(value, axis, pairs)]
    unnamed x75 -> x144, local copies, waits for them, and re-layouts: 11.9 us -> 19.9 us
    sub x22 -> x7, local copies, waits for them, and re-layouts: 0.85 us -> 5.07 us  [kernel_block(): offset_gap = left_pts[axis_id][:, None] - right_pts[axis_id][None, :]]
    ppermute x16, starting transfers between devices: 79.4 us -> 83.6 us  [from_behind(): return lax.ppermute(block, axis, route)]
    cond x0 -> x2, matrix products: none -> 3.03 us  [contribution(): return lax.cond(listed, compute, skip, coords, block[:leaf_points])]
  transfers between devices with their start and end apart: 22 -> 22, of which waited for: 4 -> 4; matrix products, arithmetic and copies ran while one was open for 13% -> 7% of each run, Pallas kernels for 0% -> 0%
where the time goes in v9:
time: 289 us; the launch traced here: 283 us
  Pallas kernels  111 us (38%)
  starting transfers between devices  95.6 us (33%)
  local copies, waits for them, and re-layouts  37.6 us (13%)
  between operations  12.3 us (4%)
  other arithmetic  11.4 us (4%)
  matrix products  9.26 us (3%)
  waiting for transfers between devices  5.69 us (2%)
    pallas_call x1, Pallas kernels, exchange(): pl.pallas_call(functools.partial(exchange_kernel, clusters), out_shape=(j...  103 us
    ppermute x16, starting transfers between devices, from_behind(): return lax.ppermute(block, axis, route)  83.6 us
    unnamed x144, local copies, waits for them, and re-layouts  19.9 us
    ppermute x6, starting transfers between devices, from_partner(): return lax.ppermute(value, axis, pairs)  12 us
    pallas_call x1, Pallas kernels, mates_gather(): pl.pallas_call(mates_kernel, out_shape=jax.ShapeDtypeStruct((8, rows, col...  7.62 us
  transfers between devices with their start and end apart: 22, of which 4 were waited for; matrix products, arithmetic and copies ran while one was open for 7% of the time, Pallas kernels for 0%

profile of v9, /device:TPU:24, one launch (start us, length us, event | category | flops | bytes accessed | tf_op | source)
XLA Modules:
  0.0 283.2 jit_solution(8032973858022519220)
XLA Ops:
  0.1 0.9 copy.110
  1.0 0.7 reduce.17
  1.7 1.5 fusion.442
  3.2 1.0 pad_maximum_fusion
  4.2 1.9 collective-permute-start.6
  6.2 13.2 %collective-permute-start.7 = (f32[655,128]{1,0:T(8,128)S(1)}, f32[655,128]{1,0:T(8,128)S(1)}, u32[]{:S(2)}, u32[]{:S(2)}) collective-permute-start(f32[655,128]{1,0:T(8,128)S(1)} %pad_maximum_fusion), channel_id=1, source_target_pairs={{1,0},{2,1},{3,2},{4,3},{5,4},{6,5},{7,6},{8,7},{9,8},{10,9},{11,1... | collective-permute-start | bytes 1006088 | tf_op jit(solution)/shard_map/ppermute | solution.py:32
  19.4 1.9 collective-permute-start.1
  21.3 2.4 collective-permute-start
  26.1 0.8 compare_reduce_fusion.5
  31.3 1.6 gather_fusion.1
  33.0 0.9 compare_reduce_fusion.22
  34.5 1.9 collective-permute-start.8
  36.5 7.9 %collective-permute-start.9 = (f32[655,128]{1,0:T(8,128)S(1)}, f32[655,128]{1,0:T(8,128)S(1)}, u32[]{:S(2)}, u32[]{:S(2)}) collective-permute-start(f32[655,128]{1,0:T(8,128)S(1)} %collective-permute-done.7), channel_id=1, source_target_pairs={{1,0},{2,1},{3,2},{4,3},{5,4},{6,5},{7,6},{8,7},{9,8},{10,9},{11,1... | collective-permute-start | bytes 1006088 | tf_op jit(solution)/shard_map/ppermute | solution.py:32
  45.2 2.0 collective-permute-done.8
  47.2 1.9 collective-permute-start.10
  49.1 7.9 %collective-permute-start.11 = (f32[655,128]{1,0:T(8,128)S(1)}, f32[655,128]{1,0:T(8,128)S(1)}, u32[]{:S(2)}, u32[]{:S(2)}) collective-permute-start(f32[655,128]{1,0:T(8,128)S(1)} %collective-permute-done.9), channel_id=1, source_target_pairs={{1,0},{2,1},{3,2},{4,3},{5,4},{6,5},{7,6},{8,7},{9,8},{10,9},{11,1... | collective-permute-start | bytes 1006088 | tf_op jit(solution)/shard_map/ppermute | solution.py:32
  58.3 1.9 collective-permute-start.2
  60.3 1.9 collective-permute-start.12
  62.2 7.9 %collective-permute-start.13 = (f32[655,128]{1,0:T(8,128)S(1)}, f32[655,128]{1,0:T(8,128)}, u32[]{:S(2)}, u32[]{:S(2)}) collective-permute-start(f32[655,128]{1,0:T(8,128)S(1)} %collective-permute-done.11), channel_id=1, source_target_pairs={{1,0},{2,1},{3,2},{4,3},{5,4},{6,5},{7,6},{8,7},{9,8},{10,9},{11,1... | collective-permute-start | bytes 1006088 | tf_op jit(solution)/shard_map/ppermute | solution.py:32
  70.8 2.3 collective-permute-done.12
  73.1 1.9 collective-permute-start.14
  75.0 7.9 %collective-permute-start.15 = (f32[655,128]{1,0:T(8,128)}, f32[655,128]{1,0:T(8,128)}, u32[]{:S(2)}, u32[]{:S(2)}) collective-permute-start(f32[655,128]{1,0:T(8,128)} %collective-permute-done.13), channel_id=1, source_target_pairs={{1,0},{2,1},{3,2},{4,3},{5,4},{6,5},{7,6},{8,7},{9,8},{10,9},{11,1... | collective-permute-start | bytes 1006088 | tf_op jit(solution)/shard_map/ppermute | solution.py:32
  82.9 1.9 collective-permute-start.3
  85.4 0.7 collective-permute-done.14
  86.1 1.9 collective-permute-start.16
  88.0 7.9 %collective-permute-start.17 = (f32[655,128]{1,0:T(8,128)}, f32[655,128]{1,0:T(8,128)}, u32[]{:S(2)}, u32[]{:S(2)}) collective-permute-start(f32[655,128]{1,0:T(8,128)} %collective-permute-done.15), channel_id=1, source_target_pairs={{1,0},{2,1},{3,2},{4,3},{5,4},{6,5},{7,6},{8,7},{9,8},{10,9},{11,1... | collective-permute-start | bytes 1006088 | tf_op jit(solution)/shard_map/ppermute | solution.py:32
  96.0 1.9 collective-permute-start.4
  97.9 1.3 fusion.514
  110.0 1.1 conditional.17
  110.1 1.1 fusion
  111.7 1.9 collective-permute-start.18
  113.7 7.9 %collective-permute-start.19 = (f32[655,128]{1,0:T(8,128)}, f32[655,128]{1,0:T(8,128)}, u32[]{:S(2)}, u32[]{:S(2)}) collective-permute-start(f32[655,128]{1,0:T(8,128)} %collective-permute-done.17), channel_id=1, source_target_pairs={{1,0},{2,1},{3,2},{4,3},{5,4},{6,5},{7,6},{8,7},{9,8},{10,9},{11,1... | collective-permute-start | bytes 1006088 | tf_op jit(solution)/shard_map/ppermute | solution.py:32
  122.2 1.9 collective-permute-start.5
  124.7 1.9 collective-permute-start.20
  126.7 7.9 %collective-permute-start.21 = (f32[655,128]{1,0:T(8,128)}, f32[655,128]{1,0:T(8,128)}, u32[]{:S(2)}, u32[]{:S(2)}) collective-permute-start(f32[655,128]{1,0:T(8,128)} %collective-permute-done.19), channel_id=1, source_target_pairs={{1,0},{2,1},{3,2},{4,3},{5,4},{6,5},{7,6},{8,7},{9,8},{10,9},{11,1... | collective-permute-start | bytes 1006088 | tf_op jit(solution)/shard_map/ppermute | solution.py:32
  135.3 0.7 fusion.496
  140.3 3.0 %conditional.33 = (f32[512,128]{0,1:T(8,128)S(1)}) conditional(s32[]{:T(128)} %convert_element_type.79, () %tuple.141, (f32[3,512]{1,0:T(4,128)S(1)}, f32[655,128]{1,0:T(8,128)}) %tuple.339), branch_computations={%region_49.50_spmd, %region_50.51_spmd} | conditional | flops 203948032 | bytes 561160 | solution.py:150
  140.3 0.8 slice_bitcast_fusion.47
  141.1 2.0 fusion.367
  144.0 1.8 add_add_fusion
  145.9 1.5 copy.62.top_ref
  147.4 103.1 %shard_map.145 = (f32[64,16,128]{2,1,0:T(8,128)}, f32[8,128,128]{2,1,0:T(8,128)}, f32[8,128,128]{2,1,0:T(8,128)}) custom-call(f32[16,128]{1,0:T(8,128)} %copy.62.top_ref, f32[128,128]{1,0:T(8,128)} %slice_bitcast_fusion.65.pair_ref, f32[128,128]{1,0:T(8,128)} %get-tuple-element.383.quad_ref), custom_call_target="tpu_custom_call" | custom-call | tf_op jit(solution)/shard_map/pallas_call | solution.py:376
  250.5 1.6 gather_fusion.3
  252.2 1.2 fusion.393.block_ref
  253.3 7.6 %shard_map.146 = f32[8,16,128]{2,1,0:T(8,128)} custom-call(f32[16,128]{1,0:T(8,128)} %fusion.393.block_ref), custom_call_target="tpu_custom_call" | custom-call | tf_op jit(solution)/shard_map/pallas_call | solution.py:357
  260.9 0.9 fusion.491
  261.8 0.9 fusion.490
  262.7 0.9 fusion.489
  263.6 0.9 fusion.488
  264.5 0.9 fusion.487
  265.4 0.9 fusion.486
  266.3 0.9 fusion.485
  267.2 0.9 fusion.484
  268.1 0.9 fusion.483
  269.0 0.9 fusion.482
  269.9 0.9 fusion.481
  270.8 0.9 fusion.480
  271.7 0.9 fusion.479
  272.5 0.9 fusion.478
  273.4 0.9 fusion.477
  274.3 0.9 fusion.476
  275.2 0.7 gather_fusion
  276.2 0.7 copy-done.9
  282.3 0.8 copy.64
  (235 shorter events, 23.7 us)
Async XLA Ops:
  0.0 1.7 copy-start
  0.0 27.0 %copy-start.31 = (f32[1,3,128]{2,0,1:T(1,128)S(1)}, f32[1,3,128]{2,0,1:T(1,128)}, u32[]{:S(2)}) copy-start(f32[1,3,128]{2,0,1:T(1,128)} %param.57) | copy-start | bytes 4612
  0.0 19.4 %copy-start.27 = (f32[32,128]{1,0:T(8,128)S(1)}, f32[32,128]{1,0:T(8,128)}, u32[]{:S(2)}) copy-start(f32[32,128]{1,0:T(8,128)} %param.56) | copy-start | bytes 49156
  0.0 21.3 %copy-start.14 = (f32[64,128]{1,0:T(8,128)S(1)}, f32[64,128]{1,0:T(8,128)}, u32[]{:S(2)}) copy-start(f32[64,128]{1,0:T(8,128)} %param.55) | copy-start | bytes 98308
  0.0 23.8 %copy-start.28 = (s32[128,8]{0,1:T(8,128)S(1)}, s32[128,8]{0,1:T(8,128)}, u32[]{:S(2)}) copy-start(s32[128,8]{0,1:T(8,128)} %param.64) | copy-start | bytes 12292
  0.0 23.8 %copy-start.29 = (s32[64,8]{0,1:T(8,128)S(1)}, s32[64,8]{0,1:T(8,128)}, u32[]{:S(2)}) copy-start(s32[64,8]{0,1:T(8,128)} %param.65) | copy-start | bytes 6148
  0.0 25.2 %copy-start.30 = (s32[256,8]{0,1:T(8,128)S(1)}, s32[256,8]{0,1:T(8,128)}, u32[]{:S(2)}) copy-start(s32[256,8]{0,1:T(8,128)} %param.63) | copy-start | bytes 24580
  0.1 25.9 %copy-start.47 = (s32[1,8]{1,0:T(1,128)S(1)}, s32[1,8]{1,0:T(1,128)}, u32[]{:S(2)}) copy-start(s32[1,8]{1,0:T(1,128)} %param.62) | copy-start | bytes 100
  0.1 27.5 %copy-start.19 = (f32[128,3,128]{2,0,1:T(8,128)S(1)}, f32[128,3,128]{2,0,1:T(8,128)}, u32[]{:S(2)}) copy-start(f32[128,3,128]{2,0,1:T(8,128)} %param.59) | copy-start | bytes 589828
  0.1 29.4 %copy-start.13 = (f32[64,3,128]{2,0,1:T(8,128)S(1)}, f32[64,3,128]{2,0,1:T(8,128)}, u32[]{:S(2)}) copy-start(f32[64,3,128]{2,0,1:T(8,128)} %param.60) | copy-start | bytes 294916
  0.1 32.9 %copy-start.48 = (s32[1,16]{1,0:T(1,128)S(1)}, s32[1,16]{1,0:T(1,128)}, u32[]{:S(2)}) copy-start(s32[1,16]{1,0:T(1,128)} %param.61) | copy-start | bytes 196
  0.1 44.8 %copy-start.10 = (f32[1,128,128]{2,1,0:T(8,128)S(1)}, f32[1,128,128]{2,1,0:T(8,128)}, u32[]{:S(2)}) copy-start(f32[1,128,128]{2,1,0:T(8,128)} %param.54) | copy-start | bytes 196612
  4.2 30.3 %collective-permute-start.6 = (f32[655,128]{1,0:T(8,128)S(1)}, f32[655,128]{1,0:T(8,128)S(1)}, u32[]{:S(2)}, u32[]{:S(2)}) collective-permute-start(f32[655,128]{1,0:T(8,128)S(1)} %pad_maximum_fusion), channel_id=1, source_target_pairs={{0,1},{1,2},{2,3},{3,4},{4,5},{5,6},{6,7},{7,8},{8,9},{9,10},{10,1... | collective-permute-start | bytes 1006088 | tf_op jit(solution)/shard_map/ppermute | solution.py:32
  6.2 30.3 %collective-permute-start.7 = (f32[655,128]{1,0:T(8,128)S(1)}, f32[655,128]{1,0:T(8,128)S(1)}, u32[]{:S(2)}, u32[]{:S(2)}) collective-permute-start(f32[655,128]{1,0:T(8,128)S(1)} %pad_maximum_fusion), channel_id=1, source_target_pairs={{1,0},{2,1},{3,2},{4,3},{5,4},{6,5},{7,6},{8,7},{9,8},{10,9},{11,1... | collective-permute-start | bytes 1006088 | tf_op jit(solution)/shard_map/ppermute | solution.py:32
  19.4 38.9 %collective-permute-start.1 = (f32[32,128]{1,0:T(8,128)S(1)}, f32[32,128]{1,0:T(8,128)S(1)}, u32[]{:S(2)}, u32[]{:S(2)}) collective-permute-start(f32[32,128]{1,0:T(8,128)S(1)} %copy-done.27), channel_id=1, source_target_pairs={{0,1},{1,0},{2,3},{3,2},{4,5},{5,4},{6,7},{7,6},{8,9},{9,8},{10,11... | collective-permute-start | bytes 49160 | tf_op jit(solution)/shard_map/ppermute | solution.py:26
  21.3 48.8 %collective-permute-start = (f32[64,128]{1,0:T(8,128)S(1)}, f32[64,128]{1,0:T(8,128)S(1)}, u32[]{:S(2)}, u32[]{:S(2)}) collective-permute-start(f32[64,128]{1,0:T(8,128)S(1)} %copy-done.14), channel_id=1, source_target_pairs={{0,1},{1,0},{2,3},{3,2},{4,5},{5,4},{6,7},{7,6},{8,9},{9,8},{10,11... | collective-permute-start | bytes 98312 | tf_op jit(solution)/shard_map/ppermute | solution.py:26
  31.3 67.9 %copy-start.20 = (f32[1,3,512]{2,0,1:T(1,128)S(1)}, f32[1,3,512]{2,0,1:T(1,128)}, u32[]{:S(2)}) copy-start(f32[1,3,512]{2,0,1:T(1,128)} %param.52) | copy-start | bytes 18436
  33.9 76.1 %copy-start.7 = (f32[1,512,128]{2,1,0:T(8,128)S(1)}, f32[1,512,128]{2,1,0:T(8,128)}, u32[]{:S(2)}) copy-start(f32[1,512,128]{2,1,0:T(8,128)} %param.51) | copy-start | bytes 786436
  34.5 100.6 %copy-start.22 = (f32[655,128]{1,0:T(8,128)}, f32[655,128]{1,0:T(8,128)S(1)}, u32[]{:S(2)}) copy-start(f32[655,128]{1,0:T(8,128)S(1)} %collective-permute-done.6) | copy-start | bytes 1006084
  34.5 12.7 %collective-permute-start.8 = (f32[655,128]{1,0:T(8,128)S(1)}, f32[655,128]{1,0:T(8,128)S(1)}, u32[]{:S(2)}, u32[]{:S(2)}) collective-permute-start(f32[655,128]{1,0:T(8,128)S(1)} %collective-permute-done.6), channel_id=1, source_target_pairs={{0,1},{1,2},{2,3},{3,4},{4,5},{5,6},{6,7},{7,8},{8,9},{9,10},{10,1... | collective-permute-start | bytes 1006088 | tf_op jit(solution)/shard_map/ppermute | solution.py:32
  36.4 98.7 %copy-start.21 = (f32[655,128]{1,0:T(8,128)}, f32[655,128]{1,0:T(8,128)S(1)}, u32[]{:S(2)}) copy-start(f32[655,128]{1,0:T(8,128)S(1)} %collective-permute-done.7) | copy-start | bytes 1006084
  36.5 12.7 %collective-permute-start.9 = (f32[655,128]{1,0:T(8,128)S(1)}, f32[655,128]{1,0:T(8,128)S(1)}, u32[]{:S(2)}, u32[]{:S(2)}) collective-permute-start(f32[655,128]{1,0:T(8,128)S(1)} %collective-permute-done.7), channel_id=1, source_target_pairs={{1,0},{2,1},{3,2},{4,3},{5,4},{6,5},{7,6},{8,7},{9,8},{10,9},{11,1... | collective-permute-start | bytes 1006088 | tf_op jit(solution)/shard_map/ppermute | solution.py:32
  47.2 88.8 %copy-start.24 = (f32[655,128]{1,0:T(8,128)}, f32[655,128]{1,0:T(8,128)S(1)}, u32[]{:S(2)}) copy-start(f32[655,128]{1,0:T(8,128)S(1)} %collective-permute-done.8) | copy-start | bytes 1006084
  47.2 13.1 %collective-permute-start.10 = (f32[655,128]{1,0:T(8,128)S(1)}, f32[655,128]{1,0:T(8,128)S(1)}, u32[]{:S(2)}, u32[]{:S(2)}) collective-permute-start(f32[655,128]{1,0:T(8,128)S(1)} %collective-permute-done.8), channel_id=1, source_target_pairs={{0,1},{1,2},{2,3},{3,4},{4,5},{5,6},{6,7},{7,8},{8,9},{9,10},{10,1... | collective-permute-start | bytes 1006088 | tf_op jit(solution)/shard_map/ppermute | solution.py:32
  49.1 86.9 %copy-start.23 = (f32[655,128]{1,0:T(8,128)}, f32[655,128]{1,0:T(8,128)S(1)}, u32[]{:S(2)}) copy-start(f32[655,128]{1,0:T(8,128)S(1)} %collective-permute-done.9) | copy-start | bytes 1006084
  49.1 13.1 %collective-permute-start.11 = (f32[655,128]{1,0:T(8,128)S(1)}, f32[655,128]{1,0:T(8,128)S(1)}, u32[]{:S(2)}, u32[]{:S(2)}) collective-permute-start(f32[655,128]{1,0:T(8,128)S(1)} %collective-permute-done.9), channel_id=1, source_target_pairs={{1,0},{2,1},{3,2},{4,3},{5,4},{6,5},{7,6},{8,7},{9,8},{10,9},{11,1... | collective-permute-start | bytes 1006088 | tf_op jit(solution)/shard_map/ppermute | solution.py:32
  58.3 12.1 %collective-permute-start.2 = (f32[64,128]{1,0:T(8,128)S(1)}, f32[64,128]{1,0:T(8,128)S(1)}, u32[]{:S(2)}, u32[]{:S(2)}) collective-permute-start(f32[64,128]{1,0:T(8,128)S(1)} %maximum_select_fusion.6), channel_id=1, source_target_pairs={{0,2},{1,3},{2,0},{3,1},{4,6},{5,7},{6,4},{7,5},{8,10},{9,11},{10,... | collective-permute-start | bytes 98312 | tf_op jit(solution)/shard_map/ppermute | solution.py:26
  60.3 75.8 %copy-start.26 = (f32[655,128]{1,0:T(8,128)}, f32[655,128]{1,0:T(8,128)S(1)}, u32[]{:S(2)}) copy-start(f32[655,128]{1,0:T(8,128)S(1)} %collective-permute-done.10) | copy-start | bytes 1006084
  60.3 12.8 %collective-permute-start.12 = (f32[655,128]{1,0:T(8,128)S(1)}, f32[655,128]{1,0:T(8,128)}, u32[]{:S(2)}, u32[]{:S(2)}) collective-permute-start(f32[655,128]{1,0:T(8,128)S(1)} %collective-permute-done.10), channel_id=1, source_target_pairs={{0,1},{1,2},{2,3},{3,4},{4,5},{5,6},{6,7},{7,8},{8,9},{9,10},{10,1... | collective-permute-start | bytes 1006088 | tf_op jit(solution)/shard_map/ppermute | solution.py:32
  62.2 73.9 %copy-start.25 = (f32[655,128]{1,0:T(8,128)}, f32[655,128]{1,0:T(8,128)S(1)}, u32[]{:S(2)}) copy-start(f32[655,128]{1,0:T(8,128)S(1)} %collective-permute-done.11) | copy-start | bytes 1006084
  62.2 12.8 %collective-permute-start.13 = (f32[655,128]{1,0:T(8,128)S(1)}, f32[655,128]{1,0:T(8,128)}, u32[]{:S(2)}, u32[]{:S(2)}) collective-permute-start(f32[655,128]{1,0:T(8,128)S(1)} %collective-permute-done.11), channel_id=1, source_target_pairs={{1,0},{2,1},{3,2},{4,3},{5,4},{6,5},{7,6},{8,7},{9,8},{10,9},{11,1... | collective-permute-start | bytes 1006088 | tf_op jit(solution)/shard_map/ppermute | solution.py:32
  70.1 12.8 %copy-start.15 = (f32[64,128]{1,0:T(8,128)}, f32[64,128]{1,0:T(8,128)S(1)}, u32[]{:S(2)}) copy-start(f32[64,128]{1,0:T(8,128)S(1)} %collective-permute-done) | copy-start | bytes 98308
  70.5 12.5 %copy-start.17 = (f32[64,128]{1,0:T(8,128)}, f32[64,128]{1,0:T(8,128)S(1)}, u32[]{:S(2)}) copy-start(f32[64,128]{1,0:T(8,128)S(1)} %collective-permute-done.2) | copy-start | bytes 98308
  73.1 13.0 %collective-permute-start.14 = (f32[655,128]{1,0:T(8,128)}, f32[655,128]{1,0:T(8,128)}, u32[]{:S(2)}, u32[]{:S(2)}) collective-permute-start(f32[655,128]{1,0:T(8,128)} %collective-permute-done.12), channel_id=1, source_target_pairs={{0,1},{1,2},{2,3},{3,4},{4,5},{5,6},{6,7},{7,8},{8,9},{9,10},{10,1... | collective-permute-start | bytes 1006088 | tf_op jit(solution)/shard_map/ppermute | solution.py:32
  75.0 13.0 %collective-permute-start.15 = (f32[655,128]{1,0:T(8,128)}, f32[655,128]{1,0:T(8,128)}, u32[]{:S(2)}, u32[]{:S(2)}) collective-permute-start(f32[655,128]{1,0:T(8,128)} %collective-permute-done.13), channel_id=1, source_target_pairs={{1,0},{2,1},{3,2},{4,3},{5,4},{6,5},{7,6},{8,7},{9,8},{10,9},{11,1... | collective-permute-start | bytes 1006088 | tf_op jit(solution)/shard_map/ppermute | solution.py:32
  82.9 13.0 %collective-permute-start.3 = (f32[3,128,128]{2,1,0:T(8,128)S(1)}, f32[3,128,128]{2,1,0:T(8,128)S(1)}, u32[]{:S(2)}, u32[]{:S(2)}) collective-permute-start(f32[3,128,128]{2,1,0:T(8,128)S(1)} %pad_maximum_fusion.1), channel_id=1, source_target_pairs={{0,1},{1,0},{2,3},{3,2},{4,5},{5,4},{6,7},{7,6},{8,9},{9,8},{10,11... | collective-permute-start | bytes 589832 | tf_op jit(solution)/shard_map/ppermute | solution.py:26
  86.1 25.6 %collective-permute-start.16 = (f32[655,128]{1,0:T(8,128)}, f32[655,128]{1,0:T(8,128)}, u32[]{:S(2)}, u32[]{:S(2)}) collective-permute-start(f32[655,128]{1,0:T(8,128)} %collective-permute-done.14), channel_id=1, source_target_pairs={{0,1},{1,2},{2,3},{3,4},{4,5},{5,6},{6,7},{7,8},{8,9},{9,10},{10,1... | collective-permute-start | bytes 1006088 | tf_op jit(solution)/shard_map/ppermute | solution.py:32
  88.0 25.6 %collective-permute-start.17 = (f32[655,128]{1,0:T(8,128)}, f32[655,128]{1,0:T(8,128)}, u32[]{:S(2)}, u32[]{:S(2)}) collective-permute-start(f32[655,128]{1,0:T(8,128)} %collective-permute-done.15), channel_id=1, source_target_pairs={{1,0},{2,1},{3,2},{4,3},{5,4},{6,5},{7,6},{8,7},{9,8},{10,9},{11,1... | collective-permute-start | bytes 1006088 | tf_op jit(solution)/shard_map/ppermute | solution.py:32
  96.0 25.6 %collective-permute-start.4 = (f32[2,128,128]{2,1,0:T(8,128)S(1)}, f32[2,128,128]{2,1,0:T(8,128)S(1)}, u32[]{:S(2)}, u32[]{:S(2)}) collective-permute-start(f32[2,128,128]{2,1,0:T(8,128)S(1)} %slice.724), channel_id=1, source_target_pairs={{0,2},{1,3},{2,0},{3,1},{4,6},{5,7},{6,4},{7,5},{8,10},{9,11},{10,... | collective-permute-start | bytes 393224 | tf_op jit(solution)/shard_map/ppermute | solution.py:26
  111.7 13.0 %collective-permute-start.18 = (f32[655,128]{1,0:T(8,128)}, f32[655,128]{1,0:T(8,128)}, u32[]{:S(2)}, u32[]{:S(2)}) collective-permute-start(f32[655,128]{1,0:T(8,128)} %collective-permute-done.16), channel_id=1, source_target_pairs={{0,1},{1,2},{2,3},{3,4},{4,5},{5,6},{6,7},{7,8},{8,9},{9,10},{10,1... | collective-permute-start | bytes 1006088 | tf_op jit(solution)/shard_map/ppermute | solution.py:32
  113.7 13.0 %collective-permute-start.19 = (f32[655,128]{1,0:T(8,128)}, f32[655,128]{1,0:T(8,128)}, u32[]{:S(2)}, u32[]{:S(2)}) collective-permute-start(f32[655,128]{1,0:T(8,128)} %collective-permute-done.17), channel_id=1, source_target_pairs={{1,0},{2,1},{3,2},{4,3},{5,4},{6,5},{7,6},{8,7},{9,8},{10,9},{11,1... | collective-permute-start | bytes 1006088 | tf_op jit(solution)/shard_map/ppermute | solution.py:32
  122.2 13.1 %collective-permute-start.5 = (f32[128,128]{1,0:T(8,128)S(1)}, f32[128,128]{1,0:T(8,128)S(1)}, u32[]{:S(2)}, u32[]{:S(2)}) collective-permute-start(f32[128,128]{1,0:T(8,128)S(1)} %get-tuple-element.384), channel_id=1, source_target_pairs={{0,4},{1,5},{2,6},{3,7},{4,0},{5,1},{6,2},{7,3},{8,12},{9,13},{10,... | collective-permute-start | bytes 196616 | tf_op jit(solution)/shard_map/ppermute | solution.py:26
  124.7 14.1 %collective-permute-start.20 = (f32[655,128]{1,0:T(8,128)}, f32[655,128]{1,0:T(8,128)}, u32[]{:S(2)}, u32[]{:S(2)}) collective-permute-start(f32[655,128]{1,0:T(8,128)} %collective-permute-done.18), channel_id=1, source_target_pairs={{0,1},{1,2},{2,3},{3,4},{4,5},{5,6},{6,7},{7,8},{8,9},{9,10},{10,1... | collective-permute-start | bytes 1006088 | tf_op jit(solution)/shard_map/ppermute | solution.py:32
  126.7 13.0 %collective-permute-start.21 = (f32[655,128]{1,0:T(8,128)}, f32[655,128]{1,0:T(8,128)}, u32[]{:S(2)}, u32[]{:S(2)}) collective-permute-start(f32[655,128]{1,0:T(8,128)} %collective-permute-done.19), channel_id=1, source_target_pairs={{1,0},{2,1},{3,2},{4,3},{5,4},{6,5},{7,6},{8,7},{9,8},{10,9},{11,1... | collective-permute-start | bytes 1006088 | tf_op jit(solution)/shard_map/ppermute | solution.py:32
  145.8 106.3 %copy-start.38 = (f32[1024]{0:T(1024)S(1)}, f32[1024]{0:T(1024)}, u32[]{:S(2)}) copy-start(f32[1024]{0:T(1024)} %get-tuple-element.391) | copy-start | bytes 12292
  145.8 106.3 %copy-start.39 = (f32[1024]{0:T(1024)S(1)}, f32[1024]{0:T(1024)}, u32[]{:S(2)}) copy-start(f32[1024]{0:T(1024)} %get-tuple-element.392) | copy-start | bytes 12292
  145.8 106.3 %copy-start.40 = (f32[1024]{0:T(1024)S(1)}, f32[1024]{0:T(1024)}, u32[]{:S(2)}) copy-start(f32[1024]{0:T(1024)} %get-tuple-element.393) | copy-start | bytes 12292
  145.8 106.3 %copy-start.52 = (f32[128]{0:T(128)S(1)}, f32[128]{0:T(128)}, u32[]{:S(2)}) copy-start(f32[128]{0:T(128)} %get-tuple-element.407) | copy-start | bytes 1540
  145.9 106.3 %copy-start.53 = (f32[128]{0:T(128)S(1)}, f32[128]{0:T(128)}, u32[]{:S(2)}) copy-start(f32[128]{0:T(128)} %get-tuple-element.408) | copy-start | bytes 1540
  145.9 106.3 %copy-start.54 = (f32[128]{0:T(128)S(1)}, f32[128]{0:T(128)}, u32[]{:S(2)}) copy-start(f32[128]{0:T(128)} %get-tuple-element.409) | copy-start | bytes 1540
  145.9 106.3 %copy-start.61 = (pred[1024]{0:T(1024)(128)(4,1)S(1)}, pred[1024]{0:T(1024)(128)(4,1)}, u32[]{:S(2)}) copy-start(pred[1024]{0:T(1024)(128)(4,1)} %broadcast_bitcast_fusion) | copy-start | bytes 3076
  145.9 106.3 %copy-start.62 = (pred[1024]{0:T(1024)(128)(4,1)S(1)}, pred[1024]{0:T(1024)(128)(4,1)}, u32[]{:S(2)}) copy-start(pred[1024]{0:T(1024)(128)(4,1)} %broadcast_bitcast_fusion.1) | copy-start | bytes 3076
  268.1 7.9 %copy-start.46 = (pred[8]{0:T(512)(128)(4,1)S(1)}, pred[8]{0:T(512)(128)(4,1)}, u32[]{:S(2)}) copy-start(pred[8]{0:T(512)(128)(4,1)} %compare_and_fusion.2) | copy-start | bytes 28
  274.3 1.8 copy-start.43
  276.1 1.7 copy-start.8
  276.2 2.3 copy-start.41
  276.2 2.3 copy-start.44
  278.7 1.1 copy-start.35
  278.7 1.1 copy-start.36
  278.7 1.1 copy-start.37
  278.7 1.1 copy-start.55
  278.7 1.1 copy-start.56
  278.7 1.1 copy-start.57
  280.5 1.3 copy-start.11
  (21 other events, 16.2 us)
